TPU v7x, 128 devices: a whole 4x4x4 slice. The times are simulated.
128 devices in a mesh: row: 8 (over z, y_hi), col: 16 (over y_lo, x, core).
Axes of the slice: x: 4, y: 4 (y_hi: 2, y_lo: 2; y = y_hi * 2 + y_lo), z: 4, core: 2. Of those that a mesh axis runs over, the one named last changes fastest.
Arguments:
- object_field: float32 [2, 2, 2048, 4096], P(None, None, 'row', 'col'), may hold values from -0.6 to 1
- probe_modes: float32 [2, 2, 256, 256], replicated, may hold values from -5 to 5
- amplitudes: float32 [2, 24, 16, 256, 256], P(None, 'row', 'col'), may hold values from 0 to 2
- offsets: int32 [2, 2, 24, 16], P(None, None, 'row', 'col'), may hold values from 0 to 255
- counts: int32 [2, 8, 16], P(None, 'row', 'col'), may hold values from 1 to 3, as said below
Outputs:
- new_object: float32 [2, 2, 2048, 4096], P(None, None, 'row', 'col')
- new_probe: float32 [2, 2, 256, 256], replicated
Inputs may be any that keep to these rules, and one draw needn't show every extreme that they name: offsets[b, 0, r * 3 + s, c] and offsets[b, 1, r * 3 + s, c] are the row and column, counted from tile (r, c)'s first cell, of the centre of slot s's 256 x 256 patch in batch b. Tile (r, c) has counts[b, r, c] scan positions in batch b, in its first slots; the other slots are unused; in each batch some tile has 3.
All inputs are finite; a program needn't handle non-finite values.
Results may differ from a plain program's by a relative error of at most 0.02.
Values sent between devices are 32-bit elements; how exact they have to be, the bound alone decides.
A program may use at most 128 MiB of HBM per device.

v0:
```python
import math

import jax
import jax.numpy as jnp
from jax import lax
from jax.sharding import PartitionSpec as P

AMPLITUDE_FLOOR = 0.5
OBJECT_STEP = 0.25
PROBE_STEP = 0.125


def from_behind(value, axis, steps):
    count = lax.axis_size(axis)
    leading, last = (max(0, -steps), min(count, count - steps))
    return lax.ppermute(value, axis, [(source, source + steps) for source in range(leading, last)])


def with_halo(array, sides, width):
    for axis, dim in sides:
        count, length = (lax.axis_size(axis), array.shape[dim])
        up = [(i, (i + 1) % count) for i in range(count - 1)]
        down = [(j, i) for i, j in up]
        last = lax.slice_in_dim(array, length - width, length, axis=dim)
        leading = lax.slice_in_dim(array, 0, width, axis=dim)
        before = lax.ppermute(last, axis, up)
        after = lax.ppermute(leading, axis, down)
        array = jnp.concatenate([before, array, after], axis=dim)
    return array


def tables(pattern_side):
    indices = jnp.arange(pattern_side, dtype=jnp.int32)
    products = indices[:, None] * indices[None, :] % pattern_side
    angles = products.astype(jnp.float32) * (2.0 * math.pi / pattern_side)
    norm_scale = 1.0 / math.sqrt(pattern_side)
    forward_re = (jnp.cos(angles) * norm_scale).astype(jnp.bfloat16)
    forward_im = (-jnp.sin(angles) * norm_scale).astype(jnp.bfloat16)
    frequency = jnp.where(indices < pattern_side // 2, indices, indices - pattern_side)
    phases = (frequency[:, None] * frequency[:, None] + frequency[None, :] * frequency[None, :]) % (
        16 * pattern_side
    )
    chirp_angles = phases.astype(jnp.float32) * (2.0 * math.pi / (16 * pattern_side))
    return (forward_re, forward_im, jnp.cos(chirp_angles), -jnp.sin(chirp_angles))


def contract(form, left, right):
    return jnp.einsum(form, left, right, preferred_element_type=jnp.float32)


def transform(field_re, field_im, table_re, table_im, inverse):
    sign_value = -1.0 if inverse else 1.0
    left_re = field_re.astype(jnp.bfloat16)
    left_im = field_im.astype(jnp.bfloat16)
    first_rr = contract("mjk,kl->mjl", left_re, table_re)
    first_ri = contract("mjk,kl->mjl", left_re, table_im)
    first_ir = contract("mjk,kl->mjl", left_im, table_re)
    first_ii = contract("mjk,kl->mjl", left_im, table_im)
    middle_re = (first_rr - sign_value * first_ii).astype(jnp.bfloat16)
    middle_im = (first_ir + sign_value * first_ri).astype(jnp.bfloat16)
    out_re = contract("jk,mkl->mjl", table_re, middle_re) - sign_value * contract(
        "jk,mkl->mjl", table_im, middle_im
    )
    out_im = contract("jk,mkl->mjl", table_re, middle_im) + sign_value * contract(
        "jk,mkl->mjl", table_im, middle_re
    )
    return (out_re, out_im)


def position_terms(patch_cells, probe_modes, amplitude, dft_table):
    forward_re, forward_im, chirp_re, chirp_im = dft_table
    slice_count = patch_cells.shape[1]
    wave_re = probe_modes[0]
    wave_im = probe_modes[1]
    incoming = []
    for slice_index in range(slice_count):
        incoming.append((wave_re, wave_im))
        object_re = patch_cells[0, slice_index]
        object_im = patch_cells[1, slice_index]
        exit_re = wave_re * object_re - wave_im * object_im
        exit_im = wave_re * object_im + wave_im * object_re
        if slice_index + 1 < slice_count:
            spread_re, spread_im = transform(exit_re, exit_im, forward_re, forward_im, False)
            turned_re = spread_re * chirp_re - spread_im * chirp_im
            turned_im = spread_re * chirp_im + spread_im * chirp_re
            wave_re, wave_im = transform(turned_re, turned_im, forward_re, forward_im, True)
    far_re, far_im = transform(exit_re, exit_im, forward_re, forward_im, False)
    intensity = jnp.sum(far_re * far_re + far_im * far_im, axis=0)
    modulus_ratio = 1.0 - amplitude / jnp.maximum(jnp.sqrt(intensity), AMPLITUDE_FLOOR)
    back_re, back_im = transform(
        far_re * modulus_ratio, far_im * modulus_ratio, forward_re, forward_im, True
    )
    object_terms = [None] * slice_count
    for slice_index in reversed(range(slice_count)):
        wave_re, wave_im = incoming[slice_index]
        object_re = patch_cells[0, slice_index]
        object_im = patch_cells[1, slice_index]
        term_re = jnp.sum(wave_re * back_re + wave_im * back_im, axis=0)
        term_im = jnp.sum(wave_re * back_im - wave_im * back_re, axis=0)
        object_terms[slice_index] = (term_re, term_im)
        inner_re = object_re * back_re + object_im * back_im
        inner_im = object_re * back_im - object_im * back_re
        if slice_index > 0:
            spread_re, spread_im = transform(inner_re, inner_im, forward_re, forward_im, False)
            turned_re = spread_re * chirp_re + spread_im * chirp_im
            turned_im = spread_im * chirp_re - spread_re * chirp_im
            back_re, back_im = transform(turned_re, turned_im, forward_re, forward_im, True)
    object_stack = jnp.stack(
        [
            jnp.stack([pair_terms[0] for pair_terms in object_terms]),
            jnp.stack([pair_terms[1] for pair_terms in object_terms]),
        ]
    )
    probe_stack = jnp.stack([inner_re, inner_im])
    return (object_stack, probe_stack)


def column_strip(piece, offset):
    return from_behind(piece, "col", offset)


def row_strip(piece, offset):
    return from_behind(piece, "row", offset)


def return_sectioned(gradient, rim_width, tile_cells):
    rim_start = rim_width + tile_cells
    rim_end = tile_cells - rim_width
    from_left = column_strip(gradient[:, :, :, rim_start:], 1)
    from_right = column_strip(gradient[:, :, :, :rim_width], -1)
    middle = gradient[:, :, :, rim_width:rim_start]
    middle = middle.at[:, :, :, :rim_width].add(from_left)
    middle = middle.at[:, :, :, rim_end:].add(from_right)
    from_above = row_strip(middle[:, :, rim_start:, :], 1)
    from_below = row_strip(middle[:, :, :rim_width, :], -1)
    tile_grad = middle[:, :, rim_width:rim_start, :]
    tile_grad = tile_grad.at[:, :, :rim_width, :].add(from_above)
    tile_grad = tile_grad.at[:, :, rim_end:, :].add(from_below)
    return tile_grad


def body(object_field, probe_modes, amplitudes, offsets, counts):
    pattern_side = probe_modes.shape[-1]
    rim_width = pattern_side // 2
    slice_count = object_field.shape[1]
    tile_cells = object_field.shape[-1]
    slot_count = amplitudes.shape[1]
    ext_side = tile_cells + 2 * rim_width
    dft_table = tables(pattern_side)
    current = object_field
    probe_total = jnp.zeros(probe_modes.shape, jnp.float32)
    for batch_index in range(amplitudes.shape[0]):
        extended = with_halo(current, (("row", 2), ("col", 3)), rim_width)
        batch_amplitudes = amplitudes[batch_index, :, 0]
        batch_rows = offsets[batch_index, 0, :, 0]
        batch_cols = offsets[batch_index, 1, :, 0]
        slot_limit = counts[batch_index, 0, 0]

        def slot_terms(slot_index):
            start_row = batch_rows[slot_index]
            start_col = batch_cols[slot_index]
            zero_index = jnp.zeros((), jnp.int32)
            anchor = (zero_index, zero_index, start_row, start_col)
            patch_cells = lax.dynamic_slice(
                extended, anchor, (2, slice_count, pattern_side, pattern_side)
            )
            amplitude = lax.dynamic_index_in_dim(batch_amplitudes, slot_index, 0, keepdims=False)
            object_stack, probe_stack = position_terms(
                patch_cells, probe_modes, amplitude, dft_table
            )
            return (anchor, object_stack, probe_stack)

        def accumulate(running, anchor, object_stack, probe_stack):
            gradient, probe_part = running
            window = lax.dynamic_slice(gradient, anchor, object_stack.shape)
            gradient = lax.dynamic_update_slice(gradient, window + object_stack, anchor)
            return (gradient, probe_part + probe_stack)

        def visit_masked(slot_index, running):
            anchor, object_stack, probe_stack = slot_terms(slot_index)
            weight = (slot_index < slot_limit).astype(jnp.float32)
            return accumulate(running, anchor, object_stack * weight, probe_stack * weight)

        running = (
            jnp.zeros((2, slice_count, ext_side, ext_side), jnp.float32),
            jnp.zeros(probe_modes.shape, jnp.float32),
        )
        running = lax.fori_loop(0, slot_count, visit_masked, running)
        gradient, probe_part = running
        tile_grad = return_sectioned(gradient, rim_width, tile_cells)
        current = current - OBJECT_STEP * tile_grad
        probe_total = probe_total + lax.psum(probe_part, ("row", "col"))
    return (current, probe_modes - PROBE_STEP * probe_total)


def solution(mesh):
    return jax.shard_map(
        body,
        mesh=mesh,
        in_specs=(
            P(None, None, "row", "col"),
            P(),
            P(None, "row", "col", None, None),
            P(None, None, "row", "col"),
            P(None, "row", "col"),
        ),
        out_specs=(P(None, None, "row", "col"), P()),
        check_vma=False,
    )
```

profile of v0, /device:TPU:1, one launch (start us, length us, event | category | flops | bytes accessed | tf_op | source)
XLA Modules:
  0.0 909.3 jit_solution(2415965093989044361)
XLA Ops:
  8.9 5.7 collective-permute-start
  16.0 9.1 %collective-permute-done = f32[2,2,128,256]{2,3,1,0:T(8,128)S(1)} collective-permute-done((f32[2,2,128,256]{2,3,1,0:T(8,128)S(1)}, f32[2,2,128,256]{2,3,1,0:T(8,128)S(1)}, u32[]{:S(2)}, u32[]{:S(2)}) %collective-permute-start) | collective-permute-done | bytes 524320 | tf_op jit(solution)/shard_map/ppermute | solution.py:26
  25.1 13.4 %collective-permute-done.1 = f32[2,2,128,256]{2,3,1,0:T(8,128)S(1)} collective-permute-done((f32[2,2,128,256]{2,3,1,0:T(8,128)S(1)}, f32[2,2,128,256]{2,3,1,0:T(8,128)S(1)}, u32[]{:S(2)}, u32[]{:S(2)}) %collective-permute-start.1) | collective-permute-done | bytes 524320 | tf_op jit(solution)/shard_map/ppermute | solution.py:27
  40.3 4.7 collective-permute-start.2
  45.0 1.9 collective-permute-start.3
  47.3 2.7 fusion.773
  52.7 4.3 collective-permute-done.2
  57.0 4.4 collective-permute-done.3
  61.4 4.1 pad_maximum_fusion
  65.5 2.6 broadcast.240.clone2
  68.1 271.8 %while.46 = (s32[]{:T(128)}, f32[2,2,512,512]{3,2,1,0:T(8,128)}, f32[2,2,256,256]{2,3,1,0:T(8,128)}, s32[3]{0:T(128)S(1)}, s32[3]{0:T(128)S(1)}, /*index=5*/f32[...) while((s32[]{:T(128)}, f32[2,2,512,512]{3,2,1,0:T(8,128)}, ...), condition=%wide.region_6.7_spmd.clone.clone.clone.clone, body=%wide.region_0.6_spmd.clone.clone.clone.clone.sunk | while | flops 3292069888 | bytes 88081760 | solution.py:188
  134.5 2.4 add_bitcast_fusion.4
  138.6 1.8 constant_dynamic-slice_fusion.8
  140.7 3.1 fusion.1267
  145.4 11.6 %dynamic_update_slice.24 = f32[2,2,512,512]{3,2,1,0:T(8,128)} dynamic-update-slice(f32[2,2,512,512]{3,2,1,0:T(8,128)} %get-tuple-element.1607, f32[2,2,256,256]{3,2,1,0:T(8,128)S(1)} %copy.239, s32[]{:T(128)} %constant.326.clone.1..sunk, s32[]{:T(128)} %constant.326.clone.1..sunk, s32[]{:T(128)S(6)} %select_n.701, s32[]{:T(128)S(6)} %select_n.702) | dynamic-update-slice | bytes 2097156 | tf_op jit(solution)/shard_map/while/body/eval_jaxpr/dynamic_update_slice | solution.py:176
  164.2 1.7 dynamic-slice_bitcast_fusion.5
  223.6 2.4 add_bitcast_fusion.4
  227.7 1.8 constant_dynamic-slice_fusion.8
  229.8 3.5 fusion.1267
  234.9 11.9 %dynamic_update_slice.24 = f32[2,2,512,512]{3,2,1,0:T(8,128)} dynamic-update-slice(f32[2,2,512,512]{3,2,1,0:T(8,128)} %get-tuple-element.1607, f32[2,2,256,256]{3,2,1,0:T(8,128)S(1)} %copy.239, s32[]{:T(128)} %constant.326.clone.1..sunk, s32[]{:T(128)} %constant.326.clone.1..sunk, s32[]{:T(128)S(6)} %select_n.701, s32[]{:T(128)S(6)} %select_n.702) | dynamic-update-slice | bytes 2097156 | tf_op jit(solution)/shard_map/while/body/eval_jaxpr/dynamic_update_slice | solution.py:176
  253.8 1.7 dynamic-slice_bitcast_fusion.5
  313.5 2.4 add_bitcast_fusion.4
  317.5 1.8 constant_dynamic-slice_fusion.8
  319.7 3.5 fusion.1267
  324.8 11.8 %dynamic_update_slice.24 = f32[2,2,512,512]{3,2,1,0:T(8,128)} dynamic-update-slice(f32[2,2,512,512]{3,2,1,0:T(8,128)} %get-tuple-element.1607, f32[2,2,256,256]{3,2,1,0:T(8,128)S(1)} %copy.239, s32[]{:T(128)} %constant.326.clone.1..sunk, s32[]{:T(128)} %constant.326.clone.1..sunk, s32[]{:T(128)S(6)} %select_n.701, s32[]{:T(128)S(6)} %select_n.702) | dynamic-update-slice | bytes 2097156 | tf_op jit(solution)/shard_map/while/body/eval_jaxpr/dynamic_update_slice | solution.py:176
  339.9 1.9 fusion.768
  341.8 2.5 collective-permute-start.4
  344.3 2.1 collective-permute-start.5
  346.6 9.4 %collective-permute-done.4 = f32[2,2,512,128]{3,2,1,0:T(8,128)S(1)} collective-permute-done((f32[2,2,512,128]{3,2,1,0:T(8,128)S(1)}, f32[2,2,512,128]{3,2,1,0:T(8,128)S(1)}, u32[]{:S(2)}, u32[]{:S(2)}) %collective-permute-start.4) | collective-permute-done | bytes 1048608 | tf_op jit(solution)/shard_map/ppermute | solution.py:16
  356.2 4.2 collective-permute-done.5
  360.7 5.4 collective-permute-start.6
  367.4 4.7 collective-permute-done.6
  372.2 14.5 %collective-permute-done.7 = f32[2,2,128,256]{3,2,1,0:T(8,128)S(1)} collective-permute-done((f32[2,2,128,256]{3,2,1,0:T(8,128)S(1)}, f32[2,2,128,256]{3,2,1,0:T(8,128)S(1)}, u32[]{:S(2)}, u32[]{:S(2)}) %collective-permute-start.7) | collective-permute-done | bytes 524320 | tf_op jit(solution)/shard_map/ppermute | solution.py:16
  387.1 2.8 collective-permute-start.8
  391.3 5.5 collective-permute-done.8
  396.9 16.2 %collective-permute-done.9 = f32[2,2,128,256]{3,2,1,0:T(8,128)S(1)} collective-permute-done((f32[2,2,128,256]{3,2,1,0:T(8,128)S(1)}, f32[2,2,128,256]{3,2,1,0:T(8,128)S(1)}, u32[]{:S(2)}, u32[]{:S(2)}) %collective-permute-start.9) | collective-permute-done | bytes 524320 | tf_op jit(solution)/shard_map/ppermute | solution.py:27
  414.8 9.6 %collective-permute-start.10 = (f32[2,2,512,128]{3,2,1,0:T(8,128)}, f32[2,2,512,128]{3,2,1,0:T(8,128)}, u32[]{:S(2)}, u32[]{:S(2)}) collective-permute-start(f32[2,2,512,128]{3,2,1,0:T(8,128)} %get-tuple-element.1344), channel_id=1, source_target_pairs={{0,1},{1,2},{2,3},{3,4},{4,5},{5,6},{6,7},{7,8},{8,9},{9,10},{10,1... | collective-permute-start | bytes 3145736 | tf_op jit(solution)/shard_map/ppermute | solution.py:26
  424.4 1.9 collective-permute-start.11
  427.5 8.9 collective-permute-done.10
  436.4 4.4 collective-permute-done.11
  440.8 4.1 pad_maximum_fusion.1
  445.0 2.6 broadcast.240.clone
  447.5 274.5 %while.47 = (s32[]{:T(128)}, f32[2,2,512,512]{3,2,1,0:T(8,128)}, f32[2,2,256,256]{2,3,1,0:T(8,128)}, s32[3]{0:T(128)S(1)}, s32[3]{0:T(128)S(1)}, /*index=5*/f32[...) while((s32[]{:T(128)}, f32[2,2,512,512]{3,2,1,0:T(8,128)}, ...), condition=%wide.region_13.14_spmd.clone.clone.clone.clone, body=%wide.region_7.13_spmd.clone.clone.clone.clone.sunk | while | flops 3292069888 | bytes 83887400 | solution.py:188
  515.0 2.4 add_bitcast_fusion.5
  519.1 1.8 constant_dynamic-slice_fusion.9
  521.3 3.2 fusion.1400
  526.0 12.2 %dynamic_update_slice.25 = f32[2,2,512,512]{3,2,1,0:T(8,128)} dynamic-update-slice(f32[2,2,512,512]{3,2,1,0:T(8,128)} %get-tuple-element.1649, f32[2,2,256,256]{3,2,1,0:T(8,128)S(1)} %copy.245, s32[]{:T(128)} %constant.326.clone.1..sunk.1, s32[]{:T(128)} %constant.326.clone.1..sunk.1, s32[]{:T(128)S(6)} %select_n.752, s32[]{:T(128)S(6)} %select_n.753) | dynamic-update-slice | bytes 2097156 | tf_op jit(solution)/shard_map/while/body/eval_jaxpr/dynamic_update_slice | solution.py:176
  605.7 2.4 add_bitcast_fusion.5
  609.8 1.8 constant_dynamic-slice_fusion.9
  612.0 3.5 fusion.1400
  617.1 11.7 %dynamic_update_slice.25 = f32[2,2,512,512]{3,2,1,0:T(8,128)} dynamic-update-slice(f32[2,2,512,512]{3,2,1,0:T(8,128)} %get-tuple-element.1649, f32[2,2,256,256]{3,2,1,0:T(8,128)S(1)} %copy.245, s32[]{:T(128)} %constant.326.clone.1..sunk.1, s32[]{:T(128)} %constant.326.clone.1..sunk.1, s32[]{:T(128)S(6)} %select_n.752, s32[]{:T(128)S(6)} %select_n.753) | dynamic-update-slice | bytes 2097156 | tf_op jit(solution)/shard_map/while/body/eval_jaxpr/dynamic_update_slice | solution.py:176
  696.1 2.4 add_bitcast_fusion.5
  700.2 1.8 constant_dynamic-slice_fusion.9
  702.3 3.5 fusion.1400
  707.4 11.8 %dynamic_update_slice.25 = f32[2,2,512,512]{3,2,1,0:T(8,128)} dynamic-update-slice(f32[2,2,512,512]{3,2,1,0:T(8,128)} %get-tuple-element.1649, f32[2,2,256,256]{3,2,1,0:T(8,128)S(1)} %copy.245, s32[]{:T(128)} %constant.326.clone.1..sunk.1, s32[]{:T(128)} %constant.326.clone.1..sunk.1, s32[]{:T(128)S(6)} %select_n.752, s32[]{:T(128)S(6)} %select_n.753) | dynamic-update-slice | bytes 2097156 | tf_op jit(solution)/shard_map/while/body/eval_jaxpr/dynamic_update_slice | solution.py:176
  722.0 3.1 fusion.767
  725.2 2.2 collective-permute-start.12
  727.4 3.1 collective-permute-start.13
  731.9 3.2 slice.438
  736.4 2.5 add.859
  741.1 2.7 collective-permute-done.13
  746.4 4.9 collective-permute-start.14
  752.7 143.4 %all-reduce.2.cloned.1.call-done = f32[2,2,256,256]{3,2,1,0:T(8,128)} async-done(((f32[2,2,256,256]{3,2,1,0:T(8,128)}), f32[2,2,256,256]{3,2,1,0:T(8,128)}) %all-reduce.2.cloned.1.call-update) | async-done | bytes 1048592 | tf_op jit(solution)/shard_map/psum | solution.py:192
  896.1 2.6 multiply_subtract_fusion
  (441 shorter events, 418.9 us)
Async XLA Ops:
  7.2 888.9 %all-reduce.2.cloned.1.call-start = ((), (), s32[]{:S(2)}) async-start(), calls=%async_computation | async-start | bytes 2097152 | tf_op jit(solution)/shard_map/psum | solution.py:192
  8.9 16.2 %collective-permute-start = (f32[2,2,128,256]{2,3,1,0:T(8,128)S(1)}, f32[2,2,128,256]{2,3,1,0:T(8,128)S(1)}, u32[]{:S(2)}, u32[]{:S(2)}) collective-permute-start(f32[2,2,128,256]{2,3,1,0:T(8,128)S(1)} %get-tuple-element.1354), channel_id=1, source_target_pairs={{0,16},{16,32},{32,48},{48,64},{64,80},{80,96},{96,112},{1,17},{17... | collective-permute-start | bytes 1572872 | tf_op jit(solution)/shard_map/ppermute | solution.py:26
  14.5 32.4 %copy-start.9 = (f32[2,2,256,256]{3,2,1,0:T(8,128)S(1)}, f32[2,2,256,256]{3,2,1,0:T(8,128)}, u32[]{:S(2)}) copy-start(f32[2,2,256,256]{3,2,1,0:T(8,128)} %param.26) | copy-start | bytes 3145732
  14.6 23.9 %collective-permute-start.1 = (f32[2,2,128,256]{2,3,1,0:T(8,128)S(1)}, f32[2,2,128,256]{2,3,1,0:T(8,128)S(1)}, u32[]{:S(2)}, u32[]{:S(2)}) collective-permute-start(f32[2,2,128,256]{2,3,1,0:T(8,128)S(1)} %get-tuple-element.1355), channel_id=1, source_target_pairs={{16,0},{32,16},{48,32},{64,48},{80,64},{96,80},{112,96},{17,1},{33... | collective-permute-start | bytes 1572872 | tf_op jit(solution)/shard_map/ppermute | solution.py:27
  25.1 15.2 %copy-start.12 = (f32[2,2,128,256]{2,3,1,0:T(8,128)}, f32[2,2,128,256]{2,3,1,0:T(8,128)S(1)}, u32[]{:S(2)}) copy-start(f32[2,2,128,256]{2,3,1,0:T(8,128)S(1)} %collective-permute-done) | copy-start | bytes 1572868
  38.5 1.8 copy-start.14
  40.3 11.2 %copy-start.17 = (s32[2,1,1]{0,2,1:T(1,128)S(1)}, s32[2,1,1]{0,2,1:T(1,128)}, u32[]{:S(2)}) copy-start(s32[2,1,1]{0,2,1:T(1,128)} %param.29) | copy-start | bytes 28
  40.3 11.8 %copy-start.16 = (s32[2,2,3,1]{2,3,1,0:T(1,128)S(1)}, s32[2,2,3,1]{2,3,1,0:T(1,128)}, u32[]{:S(2)}) copy-start(s32[2,2,3,1]{2,3,1,0:T(1,128)} %param.28) | copy-start | bytes 148
  40.3 16.7 %collective-permute-start.2 = (f32[2,2,512,128]{2,3,1,0:T(8,128)}, f32[2,2,512,128]{2,3,1,0:T(8,128)}, u32[]{:S(2)}, u32[]{:S(2)}) collective-permute-start(f32[2,2,512,128]{2,3,1,0:T(8,128)} %get-tuple-element.1348), channel_id=1, source_target_pairs={{0,1},{1,2},{2,3},{3,4},{4,5},{5,6},{6,7},{7,8},{8,9},{9,10},{10,1... | collective-permute-start | bytes 3145736 | tf_op jit(solution)/shard_map/ppermute | solution.py:26
  45.0 16.4 %collective-permute-start.3 = (f32[2,2,512,128]{2,3,1,0:T(8,128)}, f32[2,2,512,128]{2,3,1,0:T(8,128)}, u32[]{:S(2)}, u32[]{:S(2)}) collective-permute-start(f32[2,2,512,128]{2,3,1,0:T(8,128)} %get-tuple-element.1349), channel_id=1, source_target_pairs={{1,0},{2,1},{3,2},{4,3},{5,4},{6,5},{7,6},{8,7},{9,8},{10,9},{11,1... | collective-permute-start | bytes 3145736 | tf_op jit(solution)/shard_map/ppermute | solution.py:27
  47.3 14.1 %copy-start.13 = (f32[2,2,128,256]{2,3,1,0:T(8,128)S(1)}, f32[2,2,128,256]{2,3,1,0:T(8,128)}, u32[]{:S(2)}) copy-start(f32[2,2,128,256]{2,3,1,0:T(8,128)} %copy-done.12) | copy-start | bytes 1572868
  68.3 38.0 %copy-start.6 = (f32[3,256,256]{1,2,0:T(8,128)}, f32[3,256,256]{1,2,0:T(8,128)S(1)}, u32[]{:S(2)}) copy-start(f32[3,256,256]{1,2,0:T(8,128)S(1)} %get-tuple-element.1627) | copy-start | bytes 2359300 | tf_op jit(solution)/shard_map/while
  143.8 13.2 %copy-start.7 = (f32[3,256,256]{1,2,0:T(8,128)S(1)}, f32[3,256,256]{1,2,0:T(8,128)}, u32[]{:S(2)}) copy-start(f32[3,256,256]{1,2,0:T(8,128)} %copy-done.6) | copy-start | bytes 2359300 | tf_op jit(solution)/shard_map/while
  157.4 37.8 %copy-start.6 = (f32[3,256,256]{1,2,0:T(8,128)}, f32[3,256,256]{1,2,0:T(8,128)S(1)}, u32[]{:S(2)}) copy-start(f32[3,256,256]{1,2,0:T(8,128)S(1)} %get-tuple-element.1627) | copy-start | bytes 2359300 | tf_op jit(solution)/shard_map/while
  233.3 13.6 %copy-start.7 = (f32[3,256,256]{1,2,0:T(8,128)S(1)}, f32[3,256,256]{1,2,0:T(8,128)}, u32[]{:S(2)}) copy-start(f32[3,256,256]{1,2,0:T(8,128)} %copy-done.6) | copy-start | bytes 2359300 | tf_op jit(solution)/shard_map/while
  247.0 38.0 %copy-start.6 = (f32[3,256,256]{1,2,0:T(8,128)}, f32[3,256,256]{1,2,0:T(8,128)S(1)}, u32[]{:S(2)}) copy-start(f32[3,256,256]{1,2,0:T(8,128)S(1)} %get-tuple-element.1627) | copy-start | bytes 2359300 | tf_op jit(solution)/shard_map/while
  323.1 13.5 %copy-start.7 = (f32[3,256,256]{1,2,0:T(8,128)S(1)}, f32[3,256,256]{1,2,0:T(8,128)}, u32[]{:S(2)}) copy-start(f32[3,256,256]{1,2,0:T(8,128)} %copy-done.6) | copy-start | bytes 2359300 | tf_op jit(solution)/shard_map/while
  339.9 6.4 copy-start
  341.8 14.2 %collective-permute-start.4 = (f32[2,2,512,128]{3,2,1,0:T(8,128)S(1)}, f32[2,2,512,128]{3,2,1,0:T(8,128)S(1)}, u32[]{:S(2)}, u32[]{:S(2)}) collective-permute-start(f32[2,2,512,128]{3,2,1,0:T(8,128)S(1)} %get-tuple-element.1341), channel_id=1, source_target_pairs={{0,1},{1,2},{2,3},{3,4},{4,5},{5,6},{6,7},{7,8},{8,9},{9,10},{10,1... | collective-permute-start | bytes 3145736 | tf_op jit(solution)/shard_map/ppermute | solution.py:16
  344.3 16.1 %collective-permute-start.5 = (f32[2,2,512,128]{3,2,1,0:T(8,128)S(1)}, f32[2,2,512,128]{3,2,1,0:T(8,128)S(1)}, u32[]{:S(2)}, u32[]{:S(2)}) collective-permute-start(f32[2,2,512,128]{3,2,1,0:T(8,128)S(1)} %get-tuple-element.1340), channel_id=1, source_target_pairs={{1,0},{2,1},{3,2},{4,3},{5,4},{6,5},{7,6},{8,7},{9,8},{10,9},{11,1... | collective-permute-start | bytes 3145736 | tf_op jit(solution)/shard_map/ppermute | solution.py:16
  360.6 26.2 %copy-start.8 = (f32[2,2,256,256]{3,2,1,0:T(8,128)S(1)}, f32[2,2,256,256]{3,2,1,0:T(8,128)}, u32[]{:S(2)}) copy-start(f32[2,2,256,256]{3,2,1,0:T(8,128)} %param.25) | copy-start | bytes 3145732
  360.7 11.5 %collective-permute-start.6 = (f32[2,2,128,256]{3,2,1,0:T(8,128)S(1)}, f32[2,2,128,256]{3,2,1,0:T(8,128)S(1)}, u32[]{:S(2)}, u32[]{:S(2)}) collective-permute-start(f32[2,2,128,256]{3,2,1,0:T(8,128)S(1)} %get-tuple-element.1347), channel_id=1, source_target_pairs={{0,16},{16,32},{32,48},{48,64},{64,80},{80,96},{96,112},{1,17},{17... | collective-permute-start | bytes 1572872 | tf_op jit(solution)/shard_map/ppermute | solution.py:16
  366.1 20.6 %collective-permute-start.7 = (f32[2,2,128,256]{3,2,1,0:T(8,128)S(1)}, f32[2,2,128,256]{3,2,1,0:T(8,128)S(1)}, u32[]{:S(2)}, u32[]{:S(2)}) collective-permute-start(f32[2,2,128,256]{3,2,1,0:T(8,128)S(1)} %get-tuple-element.1346), channel_id=1, source_target_pairs={{16,0},{32,16},{48,32},{64,48},{80,64},{96,80},{112,96},{17,1},{33... | collective-permute-start | bytes 1572872 | tf_op jit(solution)/shard_map/ppermute | solution.py:16
  387.0 53.9 %copy-start.3 = (f32[2,2,256,256]{3,2,1,0:T(8,128)}, f32[2,2,256,256]{3,2,1,0:T(8,128)S(1)}, u32[]{:S(2)}) copy-start(f32[2,2,256,256]{3,2,1,0:T(8,128)S(1)} %multiply_subtract_fusion.2) | copy-start | bytes 3145732
  387.1 9.8 %collective-permute-start.8 = (f32[2,2,128,256]{3,2,1,0:T(8,128)S(1)}, f32[2,2,128,256]{3,2,1,0:T(8,128)S(1)}, u32[]{:S(2)}, u32[]{:S(2)}) collective-permute-start(f32[2,2,128,256]{3,2,1,0:T(8,128)S(1)} %get-tuple-element.1352), channel_id=1, source_target_pairs={{0,16},{16,32},{32,48},{48,64},{64,80},{80,96},{96,112},{1,17},{17... | collective-permute-start | bytes 1572872 | tf_op jit(solution)/shard_map/ppermute | solution.py:26
  389.9 36.4 %copy-start.11 = (f32[1,3,1,256,256]{4,3,2,1,0:T(8,128)S(1)}, f32[1,3,1,256,256]{4,3,2,1,0:T(8,128)}, u32[]{:S(2)}) copy-start(f32[1,3,1,256,256]{4,3,2,1,0:T(8,128)} %get-tuple-element.1350) | copy-start | bytes 2359300
  389.9 23.2 %collective-permute-start.9 = (f32[2,2,128,256]{3,2,1,0:T(8,128)S(1)}, f32[2,2,128,256]{3,2,1,0:T(8,128)S(1)}, u32[]{:S(2)}, u32[]{:S(2)}) collective-permute-start(f32[2,2,128,256]{3,2,1,0:T(8,128)S(1)} %get-tuple-element.1353), channel_id=1, source_target_pairs={{16,0},{32,16},{48,32},{64,48},{80,64},{96,80},{112,96},{17,1},{33... | collective-permute-start | bytes 1572872 | tf_op jit(solution)/shard_map/ppermute | solution.py:27
  413.1 1.7 copy-start.15
  414.8 21.6 %collective-permute-start.10 = (f32[2,2,512,128]{3,2,1,0:T(8,128)}, f32[2,2,512,128]{3,2,1,0:T(8,128)}, u32[]{:S(2)}, u32[]{:S(2)}) collective-permute-start(f32[2,2,512,128]{3,2,1,0:T(8,128)} %get-tuple-element.1344), channel_id=1, source_target_pairs={{0,1},{1,2},{2,3},{3,4},{4,5},{5,6},{6,7},{7,8},{8,9},{9,10},{10,1... | collective-permute-start | bytes 3145736 | tf_op jit(solution)/shard_map/ppermute | solution.py:26
  424.4 16.4 %collective-permute-start.11 = (f32[2,2,512,128]{3,2,1,0:T(8,128)}, f32[2,2,512,128]{3,2,1,0:T(8,128)}, u32[]{:S(2)}, u32[]{:S(2)}) collective-permute-start(f32[2,2,512,128]{3,2,1,0:T(8,128)} %get-tuple-element.1345), channel_id=1, source_target_pairs={{1,0},{2,1},{3,2},{4,3},{5,4},{6,5},{7,6},{8,7},{9,8},{10,9},{11,1... | collective-permute-start | bytes 3145736 | tf_op jit(solution)/shard_map/ppermute | solution.py:27
  444.9 2.6 copy-start.18
  444.9 2.6 copy-start.19
  722.0 8.6 copy-start.1
  725.1 9.9 %copy-start.2 = (f32[2,2,256,256]{2,3,1,0:T(8,128)S(1)}, f32[2,2,256,256]{2,3,1,0:T(8,128)}, u32[]{:S(2)}) copy-start(f32[2,2,256,256]{2,3,1,0:T(8,128)} %get-tuple-element.843) | copy-start | bytes 3145732
  725.2 14.3 %collective-permute-start.12 = (f32[2,2,512,128]{3,2,1,0:T(8,128)}, f32[2,2,512,128]{3,2,1,0:T(8,128)}, u32[]{:S(2)}, u32[]{:S(2)}) collective-permute-start(f32[2,2,512,128]{3,2,1,0:T(8,128)} %get-tuple-element.1339), channel_id=1, source_target_pairs={{0,1},{1,2},{2,3},{3,4},{4,5},{5,6},{6,7},{7,8},{8,9},{9,10},{10,1... | collective-permute-start | bytes 3145736 | tf_op jit(solution)/shard_map/ppermute | solution.py:16
  727.4 16.4 %collective-permute-start.13 = (f32[2,2,512,128]{3,2,1,0:T(8,128)}, f32[2,2,512,128]{3,2,1,0:T(8,128)}, u32[]{:S(2)}, u32[]{:S(2)}) collective-permute-start(f32[2,2,512,128]{3,2,1,0:T(8,128)} %get-tuple-element.1338), channel_id=1, source_target_pairs={{1,0},{2,1},{3,2},{4,3},{5,4},{6,5},{7,6},{8,7},{9,8},{10,9},{11,1... | collective-permute-start | bytes 3145736 | tf_op jit(solution)/shard_map/ppermute | solution.py:16
  731.9 4.5 copy-start.10
  736.4 3.1 copy-start.5
  746.4 152.5 %collective-permute-start.14 = (f32[2,2,128,256]{3,2,1,0:T(8,128)}, f32[2,2,128,256]{3,2,1,0:T(8,128)}, u32[]{:S(2)}, u32[]{:S(2)}) collective-permute-start(f32[2,2,128,256]{3,2,1,0:T(8,128)} %get-tuple-element.1343), channel_id=1, source_target_pairs={{0,16},{16,32},{32,48},{48,64},{64,80},{80,96},{96,112},{1,17},{17... | collective-permute-start | bytes 1572872 | tf_op jit(solution)/shard_map/ppermute | solution.py:16
  751.3 149.8 %copy-start.4 = (f32[2,2,256,256]{3,2,1,0:T(8,128)S(1)}, f32[2,2,256,256]{3,2,1,0:T(8,128)}, u32[]{:S(2)}) copy-start(f32[2,2,256,256]{3,2,1,0:T(8,128)} %copy-done.3) | copy-start | bytes 3145732
  751.3 148.7 %collective-permute-start.15 = (f32[2,2,128,256]{3,2,1,0:T(8,128)}, f32[2,2,128,256]{3,2,1,0:T(8,128)}, u32[]{:S(2)}, u32[]{:S(2)}) collective-permute-start(f32[2,2,128,256]{3,2,1,0:T(8,128)} %get-tuple-element.1342), channel_id=1, source_target_pairs={{16,0},{32,16},{48,32},{64,48},{80,64},{96,80},{112,96},{17,1},{33... | collective-permute-start | bytes 1572872 | tf_op jit(solution)/shard_map/ppermute | solution.py:16
Sparse Core Ops, SparseCore 0:
  739.0 157.0 all-reduce.1
where the time goes:
time: 916 us; the launch traced here: 909 us
  matrix products  358 us (39%)
  waiting for transfers between devices  246 us (27%)
  local copies, waits for them, and re-layouts  141 us (15%)
  other arithmetic  62.3 us (7%)
  starting transfers between devices  52.4 us (6%)
  loops' own time  34.4 us (4%)
  between operations  14.7 us (2%)
    dot_general x288, matrix products, contract(): return jnp.einsum(form, left, right, preferred_element_type=jnp.float32)  358 us
    psum x1, waiting for transfers between devices, body(): probe_total = probe_total + lax.psum(probe_part, ('row', 'col'))  143 us
    dynamic_update_slice x12, local copies, waits for them, and re-layouts, accumulate(): gradient = lax.dynamic_update_slice(gradient, window + object_stack, anchor)  80.6 us
    ppermute x4, waiting for transfers between devices, with_halo(): after = lax.ppermute(leading, axis, down)  38.4 us
    ppermute x8, waiting for transfers between devices, from_behind(): lax.ppermute(value, axis, [(source, source + steps) for source in range(l...  36.1 us
    another operation x2, loops' own time, body(): running = lax.fori_loop(0, slot_count, visit_masked, running)  34.4 us
    ppermute x4, waiting for transfers between devices, with_halo(): before = lax.ppermute(last, axis, up)  27.9 us
    ppermute x8, starting transfers between devices, from_behind(): lax.ppermute(value, axis, [(source, source + steps) for source in range(l...  22.9 us
  transfers between devices with their start and end apart: 17, of which 15 were waited for; matrix products, arithmetic and copies ran while one was open for 3% of the time, Pallas kernels for 0%

commit v1 on v0

v1 whole, which is shorter than its diff:
```python
import math

import jax
import jax.numpy as jnp
import numpy as np
from jax import lax
from jax.experimental import pallas as pl
from jax.experimental.pallas import tpu as pltpu
from jax.sharding import PartitionSpec as P

AMPLITUDE_FLOOR = 0.5
OBJECT_STEP = 0.25
PROBE_STEP = 0.125
SIDE = 256
HALF = SIDE // 2
MODES = 2
CHUNK = 16


def real_form(table):
    re, im = table.real, table.imag
    return np.block([[re, im], [-im, re]]).astype(jnp.bfloat16)


def make_tables():
    index = np.arange(SIDE)
    angles = (index[:, None] * index[None, :] % SIDE).astype(np.float32) * np.float32(2.0 * math.pi / SIDE)
    scale = np.float32(1.0 / math.sqrt(SIDE))
    rounded = lambda v: (v * scale).astype(jnp.bfloat16).astype(np.float64)
    forward = rounded(np.cos(angles)) - 1j * rounded(np.sin(angles))
    frequency = np.where(index < HALF, index, index - SIDE).astype(np.float64)
    chirp = np.exp(-2j * math.pi * (frequency * frequency % (16 * SIDE)) / (16 * SIDE))
    spread = (forward.conj() * chirp[None, :]) @ forward
    same = 0.25 * (spread[:HALF, :HALF] + spread[HALF:, HALF:] + spread[:HALF, HALF:] + spread[HALF:, :HALF])
    other = 0.25 * (spread[:HALF, :HALF] + spread[HALF:, HALF:] - spread[:HALF, HALF:] - spread[HALF:, :HALF])
    same = 0.5 * (same + same.T)
    other = 0.5 * (other + other.T)
    even = forward[:HALF, 0::2]
    odd = forward[:HALF, 1::2]
    rows = []
    for table in (same, other, even, odd):
        matrix = real_form(table)
        rows += [matrix, np.ascontiguousarray(matrix.T)]
    order = np.zeros((SIDE, SIDE), np.float32)
    order[0::2, :HALF] = np.eye(HALF)
    order[1::2, HALF:] = np.eye(HALF)
    return np.stack(rows), order.astype(jnp.bfloat16)


TABLES, ORDER = make_tables()
(SUM_R, SUM_L, DIF_R, DIF_L, EVEN_R, EVEN_L, ODD_R, ODD_L) = range(8)


def dot(left, right):
    return jnp.dot(left, right, preferred_element_type=jnp.float32)


def three_parts(value):
    high = value.astype(jnp.bfloat16)
    rest = value - high.astype(jnp.float32)
    middle = rest.astype(jnp.bfloat16)
    return high, middle, (rest - middle.astype(jnp.float32)).astype(jnp.bfloat16)


def reorder_kernel(amp_ref, order_ref, turn_ref, out_ref):
    def one(slot, carry):
        high, middle, low = [dot(part, order_ref[...]) for part in three_parts(amp_ref[slot])]
        high, middle, low = [dot(turn_ref[...], part) for part in three_parts(high + (middle + low))]
        out_ref[slot] = high + (middle + low)
        return carry

    lax.fori_loop(0, amp_ref.shape[0], one, 0)


def reorder(amplitudes):
    slots = amplitudes.shape[0]
    spec = pl.BlockSpec(memory_space=pltpu.VMEM)
    return pl.pallas_call(
        reorder_kernel,
        out_shape=jax.ShapeDtypeStruct((slots, SIDE, SIDE), jnp.float32),
        in_specs=[spec, spec, spec],
        out_specs=spec,
        compiler_params=pltpu.CompilerParams(vmem_limit_bytes=16 << 20),
        cost_estimate=pl.CostEstimate(flops=slots * 12 * SIDE**3, bytes_accessed=slots * 8 * SIDE * SIDE, transcendentals=0),
    )(amplitudes, jnp.asarray(ORDER), jnp.asarray(ORDER.T))


def batch_kernel(
    offset_ref, count_ref, ext_ref, probe_ref, amp_ref, table_ref, grad_ref, probe_grad_ref,
    obj, psi, right_a, right_b, yield_a, yield_b, left_a, left_b, out_a, out_b,
):
    lanes = lax.broadcasted_iota(jnp.int32, (CHUNK, HALF), 1)
    lo, hi = pl.ds(0, HALF), pl.ds(HALF, HALF)

    def chunks(total, body):
        def step(index, carry):
            body(pl.multiple_of(index * CHUNK, CHUNK))
            return carry

        lax.fori_loop(0, total // CHUNK, step, 0)

    def bf(value):
        return value.astype(jnp.bfloat16)

    def zero_grad(row):
        for part in range(2):
            for layer in range(2):
                for block in range(4):
                    grad_ref[part, layer, block, pl.ds(row, CHUNK), :] = jnp.zeros((CHUNK, HALF), jnp.float32)

    chunks(2 * SIDE, zero_grad)

    def zero_probe(row):
        for part in range(2):
            for mode in range(MODES):
                probe_grad_ref[part, mode, pl.ds(row, CHUNK), :] = jnp.zeros((CHUNK, SIDE), jnp.float32)

    chunks(SIDE, zero_probe)

    def right(table_a, table_b):
        yield_a[...] = dot(right_a[...], table_ref[table_a])
        yield_b[...] = dot(right_b[...], table_ref[table_b])

    def left(table_a, table_b):
        out_a[...] = dot(table_ref[table_a], left_a[...])
        out_b[...] = dot(table_ref[table_b], left_b[...])

    def put_split(mode, row, re, im):
        at = pl.ds(mode * SIDE + row, CHUNK)
        right_a[at, lo] = bf(re[0] + re[1])
        right_a[at, hi] = bf(im[0] + im[1])
        right_b[at, lo] = bf(re[0] - re[1])
        right_b[at, hi] = bf(im[0] - im[1])

    def columns(ref, mode):
        return pl.ds(mode * SIDE, HALF), pl.ds(mode * SIDE + HALF, HALF)

    def middle_spread(row):
        for mode in range(MODES):
            here = columns(left_a, mode)
            for part, lane in ((0, lo), (1, hi)):
                top = pl.ds(mode * SIDE + row, CHUNK)
                low = pl.ds(mode * SIDE + HALF + row, CHUNK)
                at, ab = yield_a[top, lane], yield_a[low, lane]
                bt, bb = yield_b[top, lane], yield_b[low, lane]
                to = pl.ds(part * HALF + row, CHUNK)
                a_sum, a_dif = at + ab, at - ab
                b_sum, b_dif = bt + bb, bt - bb
                left_a[to, here[0]] = bf(a_sum + b_sum)
                left_a[to, here[1]] = bf(a_sum - b_sum)
                left_b[to, here[0]] = bf(a_dif + b_dif)
                left_b[to, here[1]] = bf(a_dif - b_dif)

    def middle_forward(row):
        for mode in range(MODES):
            here = columns(left_a, mode)
            for part, lane in ((0, lo), (1, hi)):
                top = pl.ds(mode * SIDE + row, CHUNK)
                low = pl.ds(mode * SIDE + HALF + row, CHUNK)
                to = pl.ds(part * HALF + row, CHUNK)
                for source, at in ((yield_a, here[0]), (yield_b, here[1])):
                    upper, lower = source[top, lane], source[low, lane]
                    left_a[to, at] = bf(upper + lower)
                    left_b[to, at] = bf(upper - lower)

    def middle_backward(row):
        for mode in range(MODES):
            here = columns(left_a, mode)
            for part, lane in ((0, lo), (1, hi)):
                to = pl.ds(part * HALF + row, CHUNK)
                for base, target in ((0, left_a), (HALF, left_b)):
                    at = pl.ds(mode * SIDE + base + row, CHUNK)
                    even, odd = yield_a[at, lane], yield_b[at, lane]
                    target[to, here[0]] = bf(even + odd)
                    target[to, here[1]] = bf(even - odd)

    def joined(mode, row):
        result = []
        for sign in (1, -1):
            pair = []
            for part in range(2):
                at = pl.ds(part * HALF + row, CHUNK)
                halves = []
                for lane in columns(out_a, mode):
                    a, b = out_a[at, lane], out_b[at, lane]
                    halves.append(a + b if sign > 0 else a - b)
                pair.append(halves)
            result.append(pair)
        return result

    def pair_of(ref, first, second, row):
        return [ref[first, second, pl.ds(row, CHUNK), lane] for lane in (lo, hi)]

    def one_slot(slot, carry):
        start_row = offset_ref[0, slot]
        start_col = offset_ref[1, slot]
        base = start_col // HALF
        shift = start_col % HALF
        take_left = lanes < HALF - shift
        put_right = lanes >= shift
        back = lax.rem(HALF - shift, HALF)

        def fetch(row):
            for part in range(2):
                for layer in range(2):
                    at = pl.ds(start_row + row, CHUNK)
                    turned = [pltpu.roll(ext_ref[part, layer, base + k, at, :], back, 1) for k in range(3)]
                    obj[part, layer, pl.ds(row, CHUNK), lo] = jnp.where(take_left, turned[0], turned[1])
                    obj[part, layer, pl.ds(row, CHUNK), hi] = jnp.where(take_left, turned[1], turned[2])

        chunks(SIDE, fetch)

        def enter(row):
            o_re, o_im = pair_of(obj, 0, 0, row), pair_of(obj, 1, 0, row)
            for mode in range(MODES):
                p_re, p_im = pair_of(probe_ref, 0, mode, row), pair_of(probe_ref, 1, mode, row)
                re = [p_re[k] * o_re[k] - p_im[k] * o_im[k] for k in range(2)]
                im = [p_re[k] * o_im[k] + p_im[k] * o_re[k] for k in range(2)]
                put_split(mode, row, re, im)

        chunks(SIDE, enter)
        right(SUM_R, DIF_R)
        chunks(HALF, middle_spread)
        left(SUM_L, DIF_L)

        def second_slice(row):
            for side in range(2):
                at = row + side * HALF
                o_re, o_im = pair_of(obj, 0, 1, at), pair_of(obj, 1, 1, at)
                for mode in range(MODES):
                    w_re, w_im = joined(mode, row)[side]
                    for k, lane in ((0, lo), (1, hi)):
                        psi[0, mode, pl.ds(at, CHUNK), lane] = w_re[k]
                        psi[1, mode, pl.ds(at, CHUNK), lane] = w_im[k]
                    re = [w_re[k] * o_re[k] - w_im[k] * o_im[k] for k in range(2)]
                    im = [w_re[k] * o_im[k] + w_im[k] * o_re[k] for k in range(2)]
                    put_split(mode, at, re, im)

        chunks(HALF, second_slice)
        right(EVEN_R, ODD_R)
        chunks(HALF, middle_forward)
        left(EVEN_L, ODD_L)

        def compare(row):
            for base_row, source in ((0, out_a), (HALF, out_b)):
                waves = []
                for mode in range(MODES):
                    here = columns(source, mode)
                    re = [source[pl.ds(row, CHUNK), lane] for lane in here]
                    im = [source[pl.ds(HALF + row, CHUNK), lane] for lane in here]
                    waves.append((re, im))
                for k, lane in ((0, lo), (1, hi)):
                    intensity = waves[0][0][k] * waves[0][0][k] + waves[0][1][k] * waves[0][1][k]
                    for re, im in waves[1:]:
                        intensity = intensity + (re[k] * re[k] + im[k] * im[k])
                    amplitude = amp_ref[slot, pl.ds(base_row + row, CHUNK), lane]
                    ratio = 1.0 - amplitude * lax.rsqrt(jnp.maximum(intensity, AMPLITUDE_FLOOR**2))
                    target = right_a if k == 0 else right_b
                    for mode, (re, im) in enumerate(waves):
                        at = pl.ds(mode * SIDE + base_row + row, CHUNK)
                        target[at, lo] = bf(re[k] * ratio)
                        target[at, hi] = bf(im[k] * ratio)

        chunks(HALF, compare)
        right(EVEN_L, ODD_L)
        chunks(HALF, middle_backward)
        left(EVEN_R, ODD_R)

        def add_term(part, layer, row, term):
            turned = [pltpu.roll(value, shift, 1) for value in term]
            zero = jnp.zeros_like(turned[0])
            spread = [
                jnp.where(put_right, turned[0], zero),
                jnp.where(put_right, turned[1], turned[0]),
                jnp.where(put_right, zero, turned[1]),
            ]
            at = pl.ds(start_row + row, CHUNK)
            for k in range(3):
                grad_ref[part, layer, base + k, at, :] = grad_ref[part, layer, base + k, at, :] + spread[k]

        def object_term(layer, row, waves, backs):
            re, im = [], []
            for k in range(2):
                re.append(sum(w[0][k] * b[0][k] + w[1][k] * b[1][k] for w, b in zip(waves, backs)))
                im.append(sum(w[0][k] * b[1][k] - w[1][k] * b[0][k] for w, b in zip(waves, backs)))
            add_term(0, layer, row, re)
            add_term(1, layer, row, im)

        def last_back(row):
            for side in range(2):
                at = row + side * HALF
                backs = [joined(mode, row)[side] for mode in range(MODES)]
                waves = [(pair_of(psi, 0, mode, at), pair_of(psi, 1, mode, at)) for mode in range(MODES)]
                o_re, o_im = pair_of(obj, 0, 1, at), pair_of(obj, 1, 1, at)
                for mode, (b_re, b_im) in enumerate(backs):
                    re = [o_re[k] * b_re[k] + o_im[k] * b_im[k] for k in range(2)]
                    im = [o_re[k] * b_im[k] - o_im[k] * b_re[k] for k in range(2)]
                    put_split(mode, at, re, im)
                object_term(1, at, waves, backs)

        chunks(HALF, last_back)
        right(SUM_L, DIF_L)
        chunks(HALF, middle_spread)
        left(SUM_R, DIF_R)

        def first_back(row):
            for side in range(2):
                at = row + side * HALF
                backs = [joined(mode, row)[side] for mode in range(MODES)]
                waves = [(pair_of(probe_ref, 0, mode, at), pair_of(probe_ref, 1, mode, at)) for mode in range(MODES)]
                o_re, o_im = pair_of(obj, 0, 0, at), pair_of(obj, 1, 0, at)
                for mode, (b_re, b_im) in enumerate(backs):
                    for k, lane in ((0, lo), (1, hi)):
                        spot = (mode, pl.ds(at, CHUNK), lane)
                        probe_grad_ref[(0, *spot)] = probe_grad_ref[(0, *spot)] + (o_re[k] * b_re[k] + o_im[k] * b_im[k])
                        probe_grad_ref[(1, *spot)] = probe_grad_ref[(1, *spot)] + (o_re[k] * b_im[k] - o_im[k] * b_re[k])
                object_term(0, at, waves, backs)

        chunks(HALF, first_back)
        return carry

    lax.fori_loop(0, count_ref[0], one_slot, 0)


def batch_terms(extended, probe_modes, amplitudes, offsets, counts, table):
    vmem = pl.BlockSpec(memory_space=pltpu.VMEM)
    smem = pl.BlockSpec(memory_space=pltpu.SMEM)
    field = pltpu.VMEM((2, 2, SIDE, SIDE), jnp.float32)
    return pl.pallas_call(
        batch_kernel,
        out_shape=(
            jax.ShapeDtypeStruct((2, 2, 4, 2 * SIDE, HALF), jnp.float32),
            jax.ShapeDtypeStruct((2, MODES, SIDE, SIDE), jnp.float32),
        ),
        in_specs=[smem, smem, vmem, vmem, vmem, vmem],
        out_specs=(vmem, vmem),
        scratch_shapes=[
            field,
            field,
            pltpu.VMEM((MODES * SIDE, SIDE), jnp.bfloat16),
            pltpu.VMEM((MODES * SIDE, SIDE), jnp.bfloat16),
            pltpu.VMEM((MODES * SIDE, SIDE), jnp.float32),
            pltpu.VMEM((MODES * SIDE, SIDE), jnp.float32),
            pltpu.VMEM((SIDE, MODES * SIDE), jnp.bfloat16),
            pltpu.VMEM((SIDE, MODES * SIDE), jnp.bfloat16),
            pltpu.VMEM((SIDE, MODES * SIDE), jnp.float32),
            pltpu.VMEM((SIDE, MODES * SIDE), jnp.float32),
        ],
        compiler_params=pltpu.CompilerParams(vmem_limit_bytes=40 << 20),
        cost_estimate=pl.CostEstimate(flops=3 * 64 * SIDE**3, bytes_accessed=12 << 20, transcendentals=0),
    )(offsets, counts, extended, probe_modes, amplitudes, table)


def from_behind(value, axis, steps):
    count = lax.axis_size(axis)
    leading, last = (max(0, -steps), min(count, count - steps))
    return lax.ppermute(value, axis, [(source, source + steps) for source in range(leading, last)])


def with_halo(array, sides, width):
    for axis, dim in sides:
        length = array.shape[dim]
        last = lax.slice_in_dim(array, length - width, length, axis=dim)
        leading = lax.slice_in_dim(array, 0, width, axis=dim)
        before = from_behind(last, axis, 1)
        after = from_behind(leading, axis, -1)
        array = jnp.concatenate([before, array, after], axis=dim)
    return array


def return_sectioned(gradient, rim_width, tile_cells):
    rim_start = rim_width + tile_cells
    rim_end = tile_cells - rim_width
    from_left = from_behind(gradient[:, :, :, rim_start:], "col", 1)
    from_right = from_behind(gradient[:, :, :, :rim_width], "col", -1)
    middle = gradient[:, :, :, rim_width:rim_start]
    middle = middle.at[:, :, :, :rim_width].add(from_left)
    middle = middle.at[:, :, :, rim_end:].add(from_right)
    from_above = from_behind(middle[:, :, rim_start:, :], "row", 1)
    from_below = from_behind(middle[:, :, :rim_width, :], "row", -1)
    tile_grad = middle[:, :, rim_width:rim_start, :]
    tile_grad = tile_grad.at[:, :, :rim_width, :].add(from_above)
    tile_grad = tile_grad.at[:, :, rim_end:, :].add(from_below)
    return tile_grad


def body(object_field, probe_modes, amplitudes, offsets, counts):
    batches, slots = amplitudes.shape[:2]
    table = jnp.asarray(TABLES)
    ordered = reorder(amplitudes.reshape(batches * slots, SIDE, SIDE)).reshape(batches, slots, SIDE, SIDE)
    current = object_field
    probe_total = None
    for batch in range(batches):
        extended = with_halo(current, (("row", 2), ("col", 3)), HALF)
        extended = extended.reshape(2, 2, 2 * SIDE, 4, HALF).transpose(0, 1, 3, 2, 4)
        gradient, probe_part = batch_terms(
            extended, probe_modes, ordered[batch], offsets[batch, :, :, 0], counts[batch, 0], table
        )
        gradient = gradient.transpose(0, 1, 3, 2, 4).reshape(2, 2, 2 * SIDE, 2 * SIDE)
        current = current - OBJECT_STEP * return_sectioned(gradient, HALF, SIDE)
        probe_total = probe_part if probe_total is None else probe_total + probe_part
    return (current, probe_modes - PROBE_STEP * lax.psum(probe_total, ("row", "col")))


def solution(mesh):
    return jax.shard_map(
        body,
        mesh=mesh,
        in_specs=(
            P(None, None, "row", "col"),
            P(),
            P(None, "row", "col", None, None),
            P(None, None, "row", "col"),
            P(None, "row", "col"),
        ),
        out_specs=(P(None, None, "row", "col"), P()),
        check_vma=False,
    )
```

time: 916 us -> 423 us (0.46)
  matrix products: 358 us -> 0 us
  local copies, waits for them, and re-layouts: 141 us -> 47.6 us
  other arithmetic: 62.3 us -> 17.6 us
  Pallas kernels: 0 us -> 35.8 us
  loops' own time: 34.4 us -> 0 us
  starting transfers between devices: 52.4 us -> 64.8 us
    dot_general x288 -> x0, matrix products: 358 us -> none  [contract(): return jnp.einsum(form, left, right, preferred_element_type=jnp.float32)]
    dynamic_update_slice x12 -> x0, local copies, waits for them, and re-layouts: 80.6 us -> none  [accumulate(): gradient = lax.dynamic_update_slice(gradient, window + object_stack, anchor)]
    ppermute x8 -> x0, waiting for transfers between devices: 66.3 us -> none  [the longest x4 38.4 us: with_halo(): after = lax.ppermute(leading, axis, down)]
    ppermute x8 -> x16, waiting for transfers between devices: 36.1 us -> 94.7 us  [from_behind(): lax.ppermute(value, axis, [(source, source + steps) for source in range(l...]
    ppermute x8 -> x16, starting transfers between devices: 22.9 us -> 64.8 us  [from_behind(): lax.ppermute(value, axis, [(source, source + steps) for source in range(l...]
    pallas_call x0 -> x3, Pallas kernels: none -> 35.8 us  [the longest x2 31.8 us: batch_terms(): pl.pallas_call(batch_kernel, out_shape=(jax.ShapeDtypeStruct((2, 2, 4, 2...]
    another operation x2 -> x0, loops' own time: 34.4 us -> none  [body(): running = lax.fori_loop(0, slot_count, visit_masked, running)]
    ppermute x8 -> x0, starting transfers between devices: 29.4 us -> none  [the longest x4 22.7 us: with_halo(): before = lax.ppermute(last, axis, up)]
  transfers between devices with their start and end apart: 17 -> 17, of which waited for: 15 -> 15; matrix products, arithmetic and copies ran while one was open for 3% -> 4% of each run, Pallas kernels for 0% -> 1%
where the time goes in v1:
time: 423 us; the launch traced here: 421 us
  waiting for transfers between devices  241 us (57%)
  starting transfers between devices  64.8 us (15%)
  local copies, waits for them, and re-layouts  47.6 us (11%)
  Pallas kernels  35.8 us (8%)
  other arithmetic  17.6 us (4%)
  between operations  14.5 us (3%)
    psum x1, waiting for transfers between devices, body(): lax.psum(probe_total, ('row', 'col'))  146 us
    ppermute x16, waiting for transfers between devices, from_behind(): lax.ppermute(value, axis, [(source, source + steps) for source in range(l...  94.7 us
    ppermute x16, starting transfers between devices, from_behind(): lax.ppermute(value, axis, [(source, source + steps) for source in range(l...  64.8 us
    pallas_call x2, Pallas kernels, batch_terms(): pl.pallas_call(batch_kernel, out_shape=(jax.ShapeDtypeStruct((2, 2, 4, 2...  31.8 us
    unnamed x42, local copies, waits for them, and re-layouts  14.9 us
    reshape x2, local copies, waits for them, and re-layouts, body(): extended.reshape(2, 2, 2 * SIDE, 4, HALF).transpose(0, 1, 3, 2, 4)  10.7 us
    transpose x2, local copies, waits for them, and re-layouts, body(): gradient.transpose(0, 1, 3, 2, 4).reshape(2, 2, 2 * SIDE, 2 * SIDE)  10.5 us
  transfers between devices with their start and end apart: 17, of which 15 were waited for; matrix products, arithmetic and copies ran while one was open for 4% of the time, Pallas kernels for 1%

profile of v1, /device:TPU:1, one launch (start us, length us, event | category | flops | bytes accessed | tf_op | source)
XLA Modules:
  0.0 421.2 jit_solution(6613166856087010052)
XLA Ops:
  7.2 1.6 copy.15
  8.9 5.7 %collective-permute-start = (f32[2,2,128,256]{2,3,1,0:T(8,128)S(1)}, f32[2,2,128,256]{2,3,1,0:T(8,128)S(1)}, u32[]{:S(2)}, u32[]{:S(2)}) collective-permute-start(f32[2,2,128,256]{2,3,1,0:T(8,128)S(1)} %get-tuple-element.124), channel_id=1, source_target_pairs={{0,16},{16,32},{32,48},{48,64},{64,80},{80,96},{96,112},{1,17},{17... | collective-permute-start | bytes 1572872 | tf_op jit(solution)/shard_map/ppermute | solution.py:357
  14.5 1.3 collective-permute-start.1
  15.8 9.2 %collective-permute-done = f32[2,2,128,256]{2,3,1,0:T(8,128)S(1)} collective-permute-done((f32[2,2,128,256]{2,3,1,0:T(8,128)S(1)}, f32[2,2,128,256]{2,3,1,0:T(8,128)S(1)}, u32[]{:S(2)}, u32[]{:S(2)}) %collective-permute-start) | collective-permute-done | bytes 524320 | tf_op jit(solution)/shard_map/ppermute | solution.py:357
  25.1 13.4 %collective-permute-done.1 = f32[2,2,128,256]{2,3,1,0:T(8,128)S(1)} collective-permute-done((f32[2,2,128,256]{2,3,1,0:T(8,128)S(1)}, f32[2,2,128,256]{2,3,1,0:T(8,128)S(1)}, u32[]{:S(2)}, u32[]{:S(2)}) %collective-permute-start.1) | collective-permute-done | bytes 524320 | tf_op jit(solution)/shard_map/ppermute | solution.py:357
  38.5 0.2 pad_maximum_fusion.2
  38.9 4.7 %collective-permute-start.2 = (f32[2,2,512,128]{2,3,1,0:T(8,128)S(1)}, f32[2,2,512,128]{2,3,1,0:T(8,128)S(1)}, u32[]{:S(2)}, u32[]{:S(2)}) collective-permute-start(f32[2,2,512,128]{2,3,1,0:T(8,128)S(1)} %get-tuple-element.118), channel_id=1, source_target_pairs={{0,1},{1,2},{2,3},{3,4},{4,5},{5,6},{6,7},{7,8},{8,9},{9,10},{10,1... | collective-permute-start | bytes 3145736 | tf_op jit(solution)/shard_map/ppermute | solution.py:357
  43.6 1.9 collective-permute-start.3
  45.6 0.7 fusion.18
  46.3 4.1 shard_map.95
  50.4 1.1 fusion.14
  51.4 3.9 collective-permute-done.2
  55.4 4.4 %collective-permute-done.3 = f32[2,2,512,128]{2,3,1,0:T(8,128)S(1)} collective-permute-done((f32[2,2,512,128]{2,3,1,0:T(8,128)S(1)}, f32[2,2,512,128]{2,3,1,0:T(8,128)S(1)}, u32[]{:S(2)}, u32[]{:S(2)}) %collective-permute-start.3) | collective-permute-done | bytes 1048608 | tf_op jit(solution)/shard_map/ppermute | solution.py:357
  59.8 2.4 pad_maximum_fusion
  62.2 5.4 %copy.13 = f32[2,2,512,4,128]{4,2,3,1,0:T(8,128)} copy(f32[2,2,512,4,128]{2,4,3,1,0:T(8,128)} %bitcast.26) | data formatting | bytes 8388608 | tf_op jit(solution)/shard_map/reshape | solution.py:395
  67.5 2.2 copy-done.2
  69.7 1.2 copy-done.7
  71.0 23.0 %shard_map.96 = (f32[2,2,4,512,128]{4,3,2,1,0:T(8,128)S(1)}, f32[2,2,256,256]{3,2,1,0:T(8,128)S(1)}) custom-call(s32[2,3]{1,0:T(2,128)S(1)} %bitcast.18, s32[1]{0:T(128)} %bitcast.1.count_ref, f32[2,2,4,512,128]{4,3,2,1,0:T(8,128)S(1)} %bitcast.15, f32[2,2,256,256]{3,2,1,0:T(8,128)S(1)} %copy-done.4, f32[3,256,256]{2,1,0:T(8,128)S(1)} %get-tuple-element.121.amp_ref, ...), custom_call_target="tpu_custom_call" | custom-call | flops 3221225472 | bytes 12582912 | tf_op jit(solution)/shard_map/pallas_call | solution.py:329
  93.9 1.9 copy-done.3
  95.9 5.3 %copy.14 = f32[2,2,512,4,128]{2,4,3,1,0:T(8,128)} copy(f32[2,2,512,4,128]{4,2,3,1,0:T(8,128)} %bitcast.16) | data formatting | bytes 8388608 | tf_op jit(solution)/shard_map/transpose | solution.py:399
  101.2 1.9 fusion.9
  103.1 1.9 collective-permute-start.4
  105.0 2.5 collective-permute-start.5
  107.7 9.1 %collective-permute-done.4 = f32[2,2,512,128]{2,3,1,0:T(8,128)S(1)} collective-permute-done((f32[2,2,512,128]{2,3,1,0:T(8,128)S(1)}, f32[2,2,512,128]{2,3,1,0:T(8,128)S(1)}, u32[]{:S(2)}, u32[]{:S(2)}) %collective-permute-start.4) | collective-permute-done | bytes 1048608 | tf_op jit(solution)/shard_map/ppermute | solution.py:357
  117.0 4.2 collective-permute-done.5
  121.2 0.3 fusion.2
  121.5 1.3 collective-permute-start.6
  122.8 1.3 collective-permute-start.7
  124.3 4.7 %collective-permute-done.6 = f32[2,2,128,256]{2,3,1,0:T(8,128)S(1)} collective-permute-done((f32[2,2,128,256]{2,3,1,0:T(8,128)S(1)}, f32[2,2,128,256]{2,3,1,0:T(8,128)S(1)}, u32[]{:S(2)}, u32[]{:S(2)}) %collective-permute-start.6) | collective-permute-done | bytes 524320 | tf_op jit(solution)/shard_map/ppermute | solution.py:357
  129.0 11.6 %collective-permute-done.7 = f32[2,2,128,256]{2,3,1,0:T(8,128)S(1)} collective-permute-done((f32[2,2,128,256]{2,3,1,0:T(8,128)S(1)}, f32[2,2,128,256]{2,3,1,0:T(8,128)S(1)}, u32[]{:S(2)}, u32[]{:S(2)}) %collective-permute-start.7) | collective-permute-done | bytes 524320 | tf_op jit(solution)/shard_map/ppermute | solution.py:357
  141.0 12.2 %collective-permute-start.8 = (f32[2,2,128,256]{2,3,1,0:T(8,128)S(1)}, f32[2,2,128,256]{2,3,1,0:T(8,128)S(1)}, u32[]{:S(2)}, u32[]{:S(2)}) collective-permute-start(f32[2,2,128,256]{2,3,1,0:T(8,128)S(1)} %get-tuple-element.122), channel_id=1, source_target_pairs={{0,16},{16,32},{32,48},{48,64},{64,80},{80,96},{96,112},{1,17},{17... | collective-permute-start | bytes 1572872 | tf_op jit(solution)/shard_map/ppermute | solution.py:357
  153.1 1.3 collective-permute-start.9
  154.4 4.8 %collective-permute-done.8 = f32[2,2,128,256]{2,3,1,0:T(8,128)S(1)} collective-permute-done((f32[2,2,128,256]{2,3,1,0:T(8,128)S(1)}, f32[2,2,128,256]{2,3,1,0:T(8,128)S(1)}, u32[]{:S(2)}, u32[]{:S(2)}) %collective-permute-start.8) | collective-permute-done | bytes 524320 | tf_op jit(solution)/shard_map/ppermute | solution.py:357
  159.2 9.3 %collective-permute-done.9 = f32[2,2,128,256]{2,3,1,0:T(8,128)S(1)} collective-permute-done((f32[2,2,128,256]{2,3,1,0:T(8,128)S(1)}, f32[2,2,128,256]{2,3,1,0:T(8,128)S(1)}, u32[]{:S(2)}, u32[]{:S(2)}) %collective-permute-start.9) | collective-permute-done | bytes 524320 | tf_op jit(solution)/shard_map/ppermute | solution.py:357
  168.5 0.2 pad_maximum_fusion.3
  168.9 10.7 %collective-permute-start.10 = (f32[2,2,512,128]{2,3,1,0:T(8,128)S(1)}, f32[2,2,512,128]{2,3,1,0:T(8,128)S(1)}, u32[]{:S(2)}, u32[]{:S(2)}) collective-permute-start(f32[2,2,512,128]{2,3,1,0:T(8,128)S(1)} %get-tuple-element.114), channel_id=1, source_target_pairs={{0,1},{1,2},{2,3},{3,4},{4,5},{5,6},{6,7},{7,8},{8,9},{9,10},{10,1... | collective-permute-start | bytes 3145736 | tf_op jit(solution)/shard_map/ppermute | solution.py:357
  179.7 1.9 collective-permute-start.11
  181.6 9.8 %collective-permute-done.10 = f32[2,2,512,128]{2,3,1,0:T(8,128)S(1)} collective-permute-done((f32[2,2,512,128]{2,3,1,0:T(8,128)S(1)}, f32[2,2,512,128]{2,3,1,0:T(8,128)S(1)}, u32[]{:S(2)}, u32[]{:S(2)}) %collective-permute-start.10) | collective-permute-done | bytes 1048608 | tf_op jit(solution)/shard_map/ppermute | solution.py:357
  191.4 4.4 %collective-permute-done.11 = f32[2,2,512,128]{2,3,1,0:T(8,128)S(1)} collective-permute-done((f32[2,2,512,128]{2,3,1,0:T(8,128)S(1)}, f32[2,2,512,128]{2,3,1,0:T(8,128)S(1)}, u32[]{:S(2)}, u32[]{:S(2)}) %collective-permute-start.11) | collective-permute-done | bytes 1048608 | tf_op jit(solution)/shard_map/ppermute | solution.py:357
  195.8 2.4 pad_maximum_fusion.1
  198.3 5.3 %copy.16 = f32[2,2,512,4,128]{4,2,3,1,0:T(8,128)} copy(f32[2,2,512,4,128]{2,4,3,1,0:T(8,128)} %bitcast.27) | data formatting | bytes 8388608 | tf_op jit(solution)/shard_map/reshape | solution.py:395
  203.5 2.2 copy-done
  205.7 1.1 copy-done.5
  206.9 1.2 copy-done.8
  208.1 8.8 %shard_map.97 = (f32[2,2,4,512,128]{4,3,2,1,0:T(8,128)S(1)}, f32[2,2,256,256]{3,2,1,0:T(8,128)S(1)}) custom-call(s32[2,3]{1,0:T(2,128)S(1)} %bitcast.17, s32[1]{0:T(128)} %bitcast.8.count_ref, f32[2,2,4,512,128]{4,3,2,1,0:T(8,128)S(1)} %bitcast.13, f32[2,2,256,256]{3,2,1,0:T(8,128)S(1)} %copy-done.4, f32[3,256,256]{2,1,0:T(8,128)S(1)} %copy-done.5, ...), custom_call_target="tpu_custom_call" | custom-call | flops 3221225472 | bytes 12582912 | tf_op jit(solution)/shard_map/pallas_call | solution.py:329
  216.9 2.0 copy-done.1
  218.9 5.2 %copy.17 = f32[2,2,512,4,128]{2,4,3,1,0:T(8,128)} copy(f32[2,2,512,4,128]{4,2,3,1,0:T(8,128)} %bitcast.14) | data formatting | bytes 8388608 | tf_op jit(solution)/shard_map/transpose | solution.py:399
  224.2 3.2 fusion.8
  227.3 1.9 collective-permute-start.12
  229.3 5.0 %collective-permute-start.13 = (f32[2,2,512,128]{2,3,1,0:T(8,128)}, f32[2,2,512,128]{2,3,1,0:T(8,128)}, u32[]{:S(2)}, u32[]{:S(2)}) collective-permute-start(f32[2,2,512,128]{2,3,1,0:T(8,128)} %get-tuple-element.108), channel_id=1, source_target_pairs={{1,0},{2,1},{3,2},{4,3},{5,4},{6,5},{7,6},{8,7},{9,8},{10,9},{11,1... | collective-permute-start | bytes 3145736 | tf_op jit(solution)/shard_map/ppermute | solution.py:357
  234.2 1.5 slice.370
  235.8 1.2 add.69
  237.0 4.3 %collective-permute-done.12 = f32[2,2,512,128]{2,3,1,0:T(8,128)} collective-permute-done((f32[2,2,512,128]{2,3,1,0:T(8,128)}, f32[2,2,512,128]{2,3,1,0:T(8,128)}, u32[]{:S(2)}, u32[]{:S(2)}) %collective-permute-start.12) | collective-permute-done | bytes 1048608 | tf_op jit(solution)/shard_map/ppermute | solution.py:357
  241.3 2.7 fusion.1
  244.1 1.6 collective-permute-done.13
  245.7 2.8 fusion
  248.5 2.3 fusion.10
  250.7 9.9 %collective-permute-start.14 = (f32[2,2,128,256]{2,3,1,0:T(8,128)}, f32[2,2,128,256]{2,3,1,0:T(8,128)}, u32[]{:S(2)}, u32[]{:S(2)}) collective-permute-start(f32[2,2,128,256]{2,3,1,0:T(8,128)} %get-tuple-element.113), channel_id=1, source_target_pairs={{0,16},{16,32},{32,48},{48,64},{64,80},{80,96},{96,112},{1,17},{17... | collective-permute-start | bytes 1572872 | tf_op jit(solution)/shard_map/ppermute | solution.py:357
  260.6 1.3 collective-permute-start.15
  261.9 146.1 %all-reduce.2.cloned.1.call-done = f32[2,2,256,256]{3,2,1,0:T(8,128)} async-done(((f32[2,2,256,256]{3,2,1,0:T(8,128)}), f32[2,2,256,256]{3,2,1,0:T(8,128)}) %all-reduce.2.cloned.1.call-update) | async-done | bytes 1048592 | tf_op jit(solution)/shard_map/psum | solution.py:402
  408.1 2.3 multiply_subtract_fusion
  410.5 1.2 fusion.5
  411.8 1.2 fusion.4
  413.1 1.3 copy.18
  (51 shorter events, 1.8 us)
Async XLA Ops:
  7.2 400.9 %all-reduce.2.cloned.1.call-start = ((), (), s32[]{:S(2)}) async-start(), calls=%async_computation | async-start | bytes 2097152 | tf_op jit(solution)/shard_map/psum | solution.py:402
  8.8 51.0 %copy-start.13 = (f32[2,2,256,256]{2,3,1,0:T(8,128)}, f32[2,2,256,256]{2,3,1,0:T(8,128)S(1)}, u32[]{:S(2)}) copy-start(f32[2,2,256,256]{2,3,1,0:T(8,128)S(1)} %copy.15) | copy-start | bytes 3145732
  8.9 16.2 %collective-permute-start = (f32[2,2,128,256]{2,3,1,0:T(8,128)S(1)}, f32[2,2,128,256]{2,3,1,0:T(8,128)S(1)}, u32[]{:S(2)}, u32[]{:S(2)}) collective-permute-start(f32[2,2,128,256]{2,3,1,0:T(8,128)S(1)} %get-tuple-element.124), channel_id=1, source_target_pairs={{0,16},{16,32},{32,48},{48,64},{64,80},{80,96},{96,112},{1,17},{17... | collective-permute-start | bytes 1572872 | tf_op jit(solution)/shard_map/ppermute | solution.py:357
  14.5 23.9 %collective-permute-start.1 = (f32[2,2,128,256]{2,3,1,0:T(8,128)S(1)}, f32[2,2,128,256]{2,3,1,0:T(8,128)S(1)}, u32[]{:S(2)}, u32[]{:S(2)}) collective-permute-start(f32[2,2,128,256]{2,3,1,0:T(8,128)S(1)} %get-tuple-element.125), channel_id=1, source_target_pairs={{16,0},{32,16},{48,32},{64,48},{80,64},{96,80},{112,96},{17,1},{33... | collective-permute-start | bytes 1572872 | tf_op jit(solution)/shard_map/ppermute | solution.py:357
  38.7 6.9 %copy-start.19 = (s32[2,1,1]{0,2,1:T(1,128)S(1)}, s32[2,1,1]{0,2,1:T(1,128)}, u32[]{:S(2)}) copy-start(s32[2,1,1]{0,2,1:T(1,128)} %param.28) | copy-start | bytes 28
  38.7 7.5 %copy-start.6 = (f32[2,3,1,256,256]{4,3,2,1,0:T(8,128)S(1)}, f32[2,3,1,256,256]{4,3,2,1,0:T(8,128)}, u32[]{:S(2)}) copy-start(f32[2,3,1,256,256]{4,3,2,1,0:T(8,128)} %param.26) | copy-start | bytes 4718596
  38.7 7.5 %copy-start.9 = (bf16[256,256]{1,0:T(8,128)(2,1)S(1)}, bf16[256,256]{1,0:T(8,128)(2,1)}, u32[]{:S(2)}) copy-start(bf16[256,256]{1,0:T(8,128)(2,1)} %constant.198.clone.turn_ref) | copy-start | bytes 393220
  38.8 7.5 %copy-start.10 = (bf16[256,256]{1,0:T(8,128)(2,1)S(1)}, bf16[256,256]{1,0:T(8,128)(2,1)}, u32[]{:S(2)}) copy-start(bf16[256,256]{1,0:T(8,128)(2,1)} %constant.197.clone.order_ref) | copy-start | bytes 393220
  38.9 16.4 %collective-permute-start.2 = (f32[2,2,512,128]{2,3,1,0:T(8,128)S(1)}, f32[2,2,512,128]{2,3,1,0:T(8,128)S(1)}, u32[]{:S(2)}, u32[]{:S(2)}) collective-permute-start(f32[2,2,512,128]{2,3,1,0:T(8,128)S(1)} %get-tuple-element.118), channel_id=1, source_target_pairs={{0,1},{1,2},{2,3},{3,4},{4,5},{5,6},{6,7},{7,8},{8,9},{9,10},{10,1... | collective-permute-start | bytes 3145736 | tf_op jit(solution)/shard_map/ppermute | solution.py:357
  43.6 16.1 %collective-permute-start.3 = (f32[2,2,512,128]{2,3,1,0:T(8,128)S(1)}, f32[2,2,512,128]{2,3,1,0:T(8,128)S(1)}, u32[]{:S(2)}, u32[]{:S(2)}) collective-permute-start(f32[2,2,512,128]{2,3,1,0:T(8,128)S(1)} %get-tuple-element.119), channel_id=1, source_target_pairs={{1,0},{2,1},{3,2},{4,3},{5,4},{6,5},{7,6},{8,7},{9,8},{10,9},{11,1... | collective-permute-start | bytes 3145736 | tf_op jit(solution)/shard_map/ppermute | solution.py:357
  46.2 4.1 copy-start.18
  62.2 5.4 %copy-start.4 = (f32[2,2,256,256]{3,2,1,0:T(8,128)S(1)}, f32[2,2,256,256]{3,2,1,0:T(8,128)}, u32[]{:S(2)}) copy-start(f32[2,2,256,256]{3,2,1,0:T(8,128)} %probe_ref.3) | copy-start | bytes 3145732
  67.5 2.2 copy-start.2
  69.7 1.2 copy-start.7
  93.9 2.0 copy-start.3
  101.2 6.3 %copy-start.16 = (f32[2,2,512,4,128]{2,4,3,1,0:T(8,128)S(1)}, f32[2,2,512,4,128]{2,4,3,1,0:T(8,128)}, u32[]{:S(2)}) copy-start(f32[2,2,512,4,128]{2,4,3,1,0:T(8,128)} %copy.14) | copy-start | bytes 12582916
  103.1 13.7 %collective-permute-start.4 = (f32[2,2,512,128]{2,3,1,0:T(8,128)S(1)}, f32[2,2,512,128]{2,3,1,0:T(8,128)S(1)}, u32[]{:S(2)}, u32[]{:S(2)}) collective-permute-start(f32[2,2,512,128]{2,3,1,0:T(8,128)S(1)} %get-tuple-element.111), channel_id=1, source_target_pairs={{0,1},{1,2},{2,3},{3,4},{4,5},{5,6},{6,7},{7,8},{8,9},{9,10},{10,1... | collective-permute-start | bytes 3145736 | tf_op jit(solution)/shard_map/ppermute | solution.py:357
  105.0 16.1 %collective-permute-start.5 = (f32[2,2,512,128]{2,3,1,0:T(8,128)S(1)}, f32[2,2,512,128]{2,3,1,0:T(8,128)S(1)}, u32[]{:S(2)}, u32[]{:S(2)}) collective-permute-start(f32[2,2,512,128]{2,3,1,0:T(8,128)S(1)} %get-tuple-element.110), channel_id=1, source_target_pairs={{1,0},{2,1},{3,2},{4,3},{5,4},{6,5},{7,6},{8,7},{9,8},{10,9},{11,1... | collective-permute-start | bytes 3145736 | tf_op jit(solution)/shard_map/ppermute | solution.py:357
  121.5 7.4 %collective-permute-start.6 = (f32[2,2,128,256]{2,3,1,0:T(8,128)S(1)}, f32[2,2,128,256]{2,3,1,0:T(8,128)S(1)}, u32[]{:S(2)}, u32[]{:S(2)}) collective-permute-start(f32[2,2,128,256]{2,3,1,0:T(8,128)S(1)} %get-tuple-element.117), channel_id=1, source_target_pairs={{0,16},{16,32},{32,48},{48,64},{64,80},{80,96},{96,112},{1,17},{17... | collective-permute-start | bytes 1572872 | tf_op jit(solution)/shard_map/ppermute | solution.py:357
  122.8 17.8 %collective-permute-start.7 = (f32[2,2,128,256]{2,3,1,0:T(8,128)S(1)}, f32[2,2,128,256]{2,3,1,0:T(8,128)S(1)}, u32[]{:S(2)}, u32[]{:S(2)}) collective-permute-start(f32[2,2,128,256]{2,3,1,0:T(8,128)S(1)} %get-tuple-element.116), channel_id=1, source_target_pairs={{16,0},{32,16},{48,32},{64,48},{80,64},{96,80},{112,96},{17,1},{33... | collective-permute-start | bytes 1572872 | tf_op jit(solution)/shard_map/ppermute | solution.py:357
  124.3 16.5 %copy-start.14 = (f32[2,2,256,256]{2,3,1,0:T(8,128)S(1)}, f32[2,2,256,256]{2,3,1,0:T(8,128)}, u32[]{:S(2)}) copy-start(f32[2,2,256,256]{2,3,1,0:T(8,128)} %copy-done.13) | copy-start | bytes 3145732
  140.9 54.9 %copy-start.11 = (f32[2,2,256,256]{2,3,1,0:T(8,128)}, f32[2,2,256,256]{2,3,1,0:T(8,128)S(1)}, u32[]{:S(2)}) copy-start(f32[2,2,256,256]{2,3,1,0:T(8,128)S(1)} %multiply_subtract_fusion.2) | copy-start | bytes 3145732
  141.0 18.3 %collective-permute-start.8 = (f32[2,2,128,256]{2,3,1,0:T(8,128)S(1)}, f32[2,2,128,256]{2,3,1,0:T(8,128)S(1)}, u32[]{:S(2)}, u32[]{:S(2)}) collective-permute-start(f32[2,2,128,256]{2,3,1,0:T(8,128)S(1)} %get-tuple-element.122), channel_id=1, source_target_pairs={{0,16},{16,32},{32,48},{48,64},{64,80},{80,96},{96,112},{1,17},{17... | collective-permute-start | bytes 1572872 | tf_op jit(solution)/shard_map/ppermute | solution.py:357
  153.1 15.4 %collective-permute-start.9 = (f32[2,2,128,256]{2,3,1,0:T(8,128)S(1)}, f32[2,2,128,256]{2,3,1,0:T(8,128)S(1)}, u32[]{:S(2)}, u32[]{:S(2)}) collective-permute-start(f32[2,2,128,256]{2,3,1,0:T(8,128)S(1)} %get-tuple-element.123), channel_id=1, source_target_pairs={{16,0},{32,16},{48,32},{64,48},{80,64},{96,80},{112,96},{17,1},{33... | collective-permute-start | bytes 1572872 | tf_op jit(solution)/shard_map/ppermute | solution.py:357
  168.9 22.5 %collective-permute-start.10 = (f32[2,2,512,128]{2,3,1,0:T(8,128)S(1)}, f32[2,2,512,128]{2,3,1,0:T(8,128)S(1)}, u32[]{:S(2)}, u32[]{:S(2)}) collective-permute-start(f32[2,2,512,128]{2,3,1,0:T(8,128)S(1)} %get-tuple-element.114), channel_id=1, source_target_pairs={{0,1},{1,2},{2,3},{3,4},{4,5},{5,6},{6,7},{7,8},{8,9},{9,10},{10,1... | collective-permute-start | bytes 3145736 | tf_op jit(solution)/shard_map/ppermute | solution.py:357
  179.7 16.1 %collective-permute-start.11 = (f32[2,2,512,128]{2,3,1,0:T(8,128)S(1)}, f32[2,2,512,128]{2,3,1,0:T(8,128)S(1)}, u32[]{:S(2)}, u32[]{:S(2)}) collective-permute-start(f32[2,2,512,128]{2,3,1,0:T(8,128)S(1)} %get-tuple-element.115), channel_id=1, source_target_pairs={{1,0},{2,1},{3,2},{4,3},{5,4},{6,5},{7,6},{8,7},{9,8},{10,9},{11,1... | collective-permute-start | bytes 3145736 | tf_op jit(solution)/shard_map/ppermute | solution.py:357
  203.5 2.2 copy-start
  205.7 1.1 copy-start.5
  206.9 1.2 copy-start.8
  216.9 2.0 copy-start.1
  224.2 10.1 %copy-start.15 = (f32[2,2,512,4,128]{2,4,3,1,0:T(8,128)S(1)}, f32[2,2,512,4,128]{2,4,3,1,0:T(8,128)}, u32[]{:S(2)}) copy-start(f32[2,2,512,4,128]{2,4,3,1,0:T(8,128)} %copy.17) | copy-start | bytes 12582916
  227.3 14.0 %collective-permute-start.12 = (f32[2,2,512,128]{2,3,1,0:T(8,128)}, f32[2,2,512,128]{2,3,1,0:T(8,128)}, u32[]{:S(2)}, u32[]{:S(2)}) collective-permute-start(f32[2,2,512,128]{2,3,1,0:T(8,128)} %get-tuple-element.109), channel_id=1, source_target_pairs={{0,1},{1,2},{2,3},{3,4},{4,5},{5,6},{6,7},{7,8},{8,9},{9,10},{10,1... | collective-permute-start | bytes 3145736 | tf_op jit(solution)/shard_map/ppermute | solution.py:357
  229.3 16.4 %collective-permute-start.13 = (f32[2,2,512,128]{2,3,1,0:T(8,128)}, f32[2,2,512,128]{2,3,1,0:T(8,128)}, u32[]{:S(2)}, u32[]{:S(2)}) collective-permute-start(f32[2,2,512,128]{2,3,1,0:T(8,128)} %get-tuple-element.108), channel_id=1, source_target_pairs={{1,0},{2,1},{3,2},{4,3},{5,4},{6,5},{7,6},{8,7},{9,8},{10,9},{11,1... | collective-permute-start | bytes 3145736 | tf_op jit(solution)/shard_map/ppermute | solution.py:357
  250.7 159.7 %copy-start.17 = (f32[2,2,512,256]{2,3,1,0:T(8,128)S(1)}, f32[2,2,512,256]{2,3,1,0:T(8,128)}, u32[]{:S(2)}) copy-start(f32[2,2,512,256]{2,3,1,0:T(8,128)} %fusion) | copy-start | bytes 6291460
  250.7 159.8 %collective-permute-start.14 = (f32[2,2,128,256]{2,3,1,0:T(8,128)}, f32[2,2,128,256]{2,3,1,0:T(8,128)}, u32[]{:S(2)}, u32[]{:S(2)}) collective-permute-start(f32[2,2,128,256]{2,3,1,0:T(8,128)} %get-tuple-element.113), channel_id=1, source_target_pairs={{0,16},{16,32},{32,48},{48,64},{64,80},{80,96},{96,112},{1,17},{17... | collective-permute-start | bytes 1572872 | tf_op jit(solution)/shard_map/ppermute | solution.py:357
  260.6 151.1 %collective-permute-start.15 = (f32[2,2,128,256]{2,3,1,0:T(8,128)}, f32[2,2,128,256]{2,3,1,0:T(8,128)}, u32[]{:S(2)}, u32[]{:S(2)}) collective-permute-start(f32[2,2,128,256]{2,3,1,0:T(8,128)} %get-tuple-element.112), channel_id=1, source_target_pairs={{16,0},{32,16},{48,32},{64,48},{80,64},{96,80},{112,96},{17,1},{33... | collective-permute-start | bytes 1572872 | tf_op jit(solution)/shard_map/ppermute | solution.py:357
  410.5 2.4 copy-start.12
Sparse Core Ops, SparseCore 0:
  237.1 170.9 all-reduce.1

commit v2 on v1

--- a/solution.py
+++ b/solution.py
@@ -15,6 +15,9 @@
 HALF = SIDE // 2
 MODES = 2
 CHUNK = 16
+MESH = pl.DeviceIdType.MESH
+SIDES = ("up", "down", "left", "right")
+OPPOSITE = {"up": "down", "down": "up", "left": "right", "right": "left"}
 
 
 def real_form(table):
@@ -62,27 +65,430 @@
     return high, middle, (rest - middle.astype(jnp.float32)).astype(jnp.bfloat16)
 
 
-def reorder_kernel(amp_ref, order_ref, turn_ref, out_ref):
-    def one(slot, carry):
-        high, middle, low = [dot(part, order_ref[...]) for part in three_parts(amp_ref[slot])]
-        high, middle, low = [dot(turn_ref[...], part) for part in three_parts(high + (middle + low))]
-        out_ref[slot] = high + (middle + low)
+def reorder_plane(plane, order, turn):
+    high, middle, low = [dot(part, order) for part in three_parts(plane)]
+    high, middle, low = [dot(turn, part) for part in three_parts(high + (middle + low))]
+    return high + (middle + low)
+
+
+class Links:
+    def __init__(self, send_sems, recv_sems):
+        self.row, self.col = lax.axis_index("row"), lax.axis_index("col")
+        rows, cols = lax.axis_size("row"), lax.axis_size("col")
+        self.has = {
+            "up": self.row > 0,
+            "down": self.row < rows - 1,
+            "left": self.col > 0,
+            "right": self.col < cols - 1,
+        }
+        self.at = {
+            "up": (self.row - 1, self.col),
+            "down": (self.row + 1, self.col),
+            "left": (self.row, self.col - 1),
+            "right": (self.row, self.col + 1),
+        }
+        self.send_sems, self.recv_sems = send_sems, recv_sems
+        self.used = 0
+        self.sent = []
+
+    def greet(self, peers=()):
+        barrier = pltpu.get_barrier_semaphore()
+        for side in SIDES:
+
+            @pl.when(self.has[side])
+            def _():
+                pl.semaphore_signal(barrier, inc=1, device_id=self.at[side], device_id_type=MESH)
+
+        for peer in peers:
+            pl.semaphore_signal(barrier, inc=1, device_id=peer, device_id_type=MESH)
+        pl.semaphore_wait(barrier, len(peers) + sum(self.has[side].astype(jnp.int32) for side in SIDES))
+
+    def copy(self, source, target, device):
+        index = self.used
+        self.used += 1
+        return pltpu.make_async_remote_copy(
+            src_ref=source,
+            dst_ref=target,
+            send_sem=self.send_sems.at[index],
+            recv_sem=self.recv_sems.at[index],
+            device_id=device,
+            device_id_type=MESH,
+        )
+
+    def send(self, source, target, side, also=None):
+        item = self.copy(source, target, self.at[side])
+        condition = self.has[side] if also is None else jnp.logical_and(self.has[side], also)
+
+        @pl.when(condition)
+        def _():
+            item.start()
+
+        self.sent.append((item, condition))
+        source_side = self.has[OPPOSITE[side]]
+        arrives = source_side if also is None else jnp.logical_and(source_side, also)
+
+        def arrived():
+            @pl.when(arrives)
+            def _():
+                item.wait_recv()
+
+        return arrived
+
+    def finish(self):
+        for item, condition in self.sent:
+
+            @pl.when(condition)
+            def _():
+                item.wait_send()
+
+
+def by_rows(start, stop, step, body):
+    def one(index, carry):
+        body(pl.ds(pl.multiple_of(start + index * step, 8), step))
         return carry
 
-    lax.fori_loop(0, amp_ref.shape[0], one, 0)
-
-
-def reorder(amplitudes):
+    lax.fori_loop(0, (stop - start) // step, one, 0)
+
+
+def first_kernel(tile_ref, amp_ref, order_ref, turn_ref, ext_ref, ordered_ref, send_sems, recv_sems):
+    links = Links(send_sems, recv_sems)
+    links.greet()
+    upper, lower, own = pl.ds(0, HALF), pl.ds(3 * HALF, HALF), pl.ds(HALF, SIDE)
+    waits, col_waits, corner_waits = [], [], []
+    for layer in range(2):
+        arrivals = []
+        for block in range(2):
+            lane = pl.ds(block * HALF, HALF)
+            arrivals.append(
+                links.send(tile_ref.at[:, layer, pl.ds(0, HALF), lane], ext_ref.at[:, layer, 1 + block, lower], "up")
+            )
+            arrivals.append(
+                links.send(tile_ref.at[:, layer, pl.ds(HALF, HALF), lane], ext_ref.at[:, layer, 1 + block, upper], "down")
+            )
+        waits.append(arrivals)
+    for layer in range(2):
+        col_waits.append(links.send(tile_ref.at[:, layer, :, pl.ds(0, HALF)], ext_ref.at[:, layer, 3, own], "left"))
+        col_waits.append(links.send(tile_ref.at[:, layer, :, pl.ds(HALF, HALF)], ext_ref.at[:, layer, 0, own], "right"))
+
+    def clear(side, blocks, rows):
+        @pl.when(jnp.logical_not(links.has[side]))
+        def _():
+            for part in range(2):
+                for layer in range(2):
+                    for block in blocks:
+                        ext_ref[part, layer, block, rows, :] = jnp.zeros((rows.size, HALF), jnp.float32)
+
+    clear("up", (1, 2), upper)
+    clear("down", (1, 2), lower)
+    clear("left", (0,), own)
+    clear("right", (3,), own)
+    for rows, side in ((upper, "up"), (lower, "down")):
+        for block, other in ((0, "left"), (3, "right")):
+
+            @pl.when(jnp.logical_not(jnp.logical_and(links.has[side], links.has[other])))
+            def _():
+                for part in range(2):
+                    for layer in range(2):
+                        ext_ref[part, layer, block, rows, :] = jnp.zeros((HALF, HALF), jnp.float32)
+
+    for part in range(2):
+        for layer in range(2):
+            for block in range(2):
+                ext_ref[part, layer, 1 + block, own, :] = tile_ref[part, layer, :, block * HALF : (block + 1) * HALF]
+
+    def one_plane(index, carry):
+        ordered_ref[index] = reorder_plane(amp_ref[index], order_ref[...], turn_ref[...])
+        return carry
+
+    lax.fori_loop(0, amp_ref.shape[0], one_plane, 0)
+    for layer in range(2):
+        for arrived in waits[layer]:
+            arrived()
+        for rows, side in ((upper, "up"), (lower, "down")):
+            for block, to, target in ((1, "left", 3), (2, "right", 0)):
+                corner_waits.append(
+                    links.send(
+                        ext_ref.at[:, layer, block, rows], ext_ref.at[:, layer, target, rows], to, also=links.has[side]
+                    )
+                )
+    for arrived in col_waits + corner_waits:
+        arrived()
+    links.finish()
+
+
+def collect_columns(links, grad_ref, from_left, from_right, total, order):
+    for side, buffer in (("left", from_left), ("right", from_right)):
+
+        @pl.when(jnp.logical_not(links.has[side]))
+        def _():
+            for part, layer in order:
+                buffer[part, layer] = jnp.zeros((2 * SIDE, HALF), jnp.float32)
+
+    arrivals = []
+    for part, layer in order:
+        arrivals.append(
+            (
+                links.send(grad_ref.at[part, layer, 0], from_right.at[part, layer], "left"),
+                links.send(grad_ref.at[part, layer, 3], from_left.at[part, layer], "right"),
+            )
+        )
+
+    def finish(index):
+        part, layer = order[index]
+        for arrived in arrivals[index]:
+            arrived()
+
+        def add(rows):
+            total[part, layer, 0, rows, :] = grad_ref[part, layer, 1, rows, :] + from_left[part, layer, rows, :]
+            total[part, layer, 1, rows, :] = grad_ref[part, layer, 2, rows, :] + from_right[part, layer, rows, :]
+
+        by_rows(0, 2 * SIDE, 64, add)
+
+    return finish
+
+
+PLANES = [(part, layer) for layer in range(2) for part in range(2)]
+
+
+def middle_kernel(ext_ref, grad_ref, out_ref, from_left, from_right, from_up, from_down, total, send_sems, recv_sems):
+    links = Links(send_sems, recv_sems)
+    links.greet()
+    finish_columns = collect_columns(links, grad_ref, from_left, from_right, total, PLANES)
+    for side, buffer in (("up", from_up), ("down", from_down)):
+
+        @pl.when(jnp.logical_not(links.has[side]))
+        def _():
+            for part, layer in PLANES:
+                buffer[part, layer] = jnp.zeros((2, SIDE, HALF), jnp.float32)
+
+    for side, block in (("left", 0), ("right", 3)):
+
+        @pl.when(jnp.logical_not(links.has[side]))
+        def _():
+            for part, layer in PLANES:
+                out_ref[part, layer, block] = jnp.zeros((2 * SIDE, HALF), jnp.float32)
+
+    arrivals = []
+    for index, (part, layer) in enumerate(PLANES):
+        finish_columns(index)
+        arrivals.append(
+            (
+                links.send(total.at[part, layer, :, pl.ds(0, SIDE)], from_down.at[part, layer], "up"),
+                links.send(total.at[part, layer, :, pl.ds(SIDE, SIDE)], from_up.at[part, layer], "down"),
+            )
+        )
+    step_up = jnp.where(links.has["up"], OBJECT_STEP, 0.0).astype(jnp.float32)
+    step_down = jnp.where(links.has["down"], OBJECT_STEP, 0.0).astype(jnp.float32)
+    halos = []
+    for index, (part, layer) in enumerate(PLANES):
+        for arrived in arrivals[index]:
+            arrived()
+        for block in range(2):
+            for start, buffer, offset, step in (
+                (0, from_up, 0, step_up),
+                (HALF, from_up, 0, OBJECT_STEP),
+                (SIDE, from_down, SIDE, OBJECT_STEP),
+                (3 * HALF, from_down, SIDE, step_down),
+            ):
+                for row in range(start, start + HALF, 64):
+                    rows, near = pl.ds(row, 64), pl.ds(row - offset, 64)
+                    gradient = total[part, layer, block, rows, :] + buffer[part, layer, block, near, :]
+                    out_ref[part, layer, 1 + block, rows, :] = ext_ref[part, layer, 1 + block, rows, :] - step * gradient
+        halos.append(links.send(out_ref.at[part, layer, 1], out_ref.at[part, layer, 3], "left"))
+        halos.append(links.send(out_ref.at[part, layer, 2], out_ref.at[part, layer, 0], "right"))
+    for arrived in halos:
+        arrived()
+    links.finish()
+
+
+def last_kernel(
+    ext_ref, grad_ref, first_probe_ref, second_probe_ref, probe_ref, object_ref, new_probe_ref,
+    from_left, from_right, from_up, from_down, total, partial, pair, quarters, sums, gathered, send_sems, recv_sems,
+):
+    links = Links(send_sems, recv_sems)
+    row, col = links.row, links.col
+    core, x, y_low = lax.rem(col, 2), lax.rem(col // 2, 4), col // 8
+    y_high, z = lax.rem(row, 2), row // 2
+    y = y_high * 2 + y_low
+    partner = (row, col + 1 - 2 * core)
+    groups = [
+        (z, lambda k: (k * 2 + y_high, col)),
+        (x, lambda k: (row, y_low * 8 + k * 2 + core)),
+        (y, lambda k: (z * 2 + k // 2, lax.rem(k, 2) * 8 + x * 2 + core)),
+    ]
+    peers = [partner]
+    for place, device in groups:
+        peers += [device(lax.rem(place + k, 4)) for k in range(1, 4)]
+    links.greet(peers)
+    finish_columns = collect_columns(links, grad_ref, from_left, from_right, total, PLANES)
+    count = 4 * SIDE
+    half = count // 2
+
+    def rows_at(start, size):
+        return pl.ds(pl.multiple_of(start, 8), size)
+
+    def start(source, target, device):
+        item = links.copy(source, target, device)
+        item.start()
+        return item
+
+    def add_probe(rows):
+        partial[rows, :] = first_probe_ref[rows, :] + second_probe_ref[rows, :]
+
+    by_rows(0, count, 64, add_probe)
+    swap = start(partial.at[rows_at((1 - core) * half, half)], pair, partner)
+    for side, buffer in (("up", from_up), ("down", from_down)):
+
+        @pl.when(jnp.logical_not(links.has[side]))
+        def _():
+            for part, layer in PLANES:
+                buffer[part, layer] = jnp.zeros((2, HALF, HALF), jnp.float32)
+
+    arrivals = []
+    for index, (part, layer) in enumerate(PLANES):
+        finish_columns(index)
+        arrivals.append(
+            (
+                links.send(total.at[part, layer, :, pl.ds(0, HALF)], from_down.at[part, layer], "up"),
+                links.send(total.at[part, layer, :, pl.ds(3 * HALF, HALF)], from_up.at[part, layer], "down"),
+            )
+        )
+    swap.wait_recv()
+    base = core * half
+
+    def add_pair(index, carry):
+        near = pl.ds(pl.multiple_of(index * 64, 64), 64)
+        mine = rows_at(base + index * 64, 64)
+        sums[mine, :] = partial[mine, :] + pair[near, :]
+        return carry
+
+    lax.fori_loop(0, half // 64, add_pair, 0)
+    size = half
+    places = []
+    for number, (place, device) in enumerate(groups):
+        size = size // 4
+        landing = quarters[number]
+        items = []
+        for k in range(1, 4):
+            other = lax.rem(place + k, 4)
+            items.append(start(sums.at[rows_at(base + other * size, size)], landing.at[k - 1], device(other)))
+        places.append((place, device, base, size))
+        base = base + place * size
+        for item in items:
+            item.wait_recv()
+        for item in items:
+            item.wait_send()
+        for begin in range(0, size, 32):
+            step = min(32, size)
+            mine = rows_at(base + begin, step)
+            value = sums[mine, :]
+            for k in range(3):
+                value = value + landing[k, pl.ds(begin, step), :]
+            (gathered if number == 2 else sums)[mine, :] = value
+    gathers = [swap]
+    for place, device, group_base, size in reversed(places):
+        mine = rows_at(group_base + place * size, size)
+        items = [start(gathered.at[mine], gathered.at[mine], device(lax.rem(place + k, 4))) for k in range(1, 4)]
+        gathers += items
+        for item in items:
+            item.wait_recv()
+    mine = rows_at(core * half, half)
+    swap_back = start(gathered.at[mine], gathered.at[mine], partner)
+    for index, (part, layer) in enumerate(PLANES):
+        for arrived in arrivals[index]:
+            arrived()
+        for block in range(2):
+            lane = pl.ds(block * HALF, HALF)
+            for begin, buffer in ((HALF, from_up), (SIDE, from_down)):
+                for offset in range(0, HALF, 64):
+                    rows, near = pl.ds(begin + offset, 64), pl.ds(offset, 64)
+                    gradient = total[part, layer, block, rows, :] + buffer[part, layer, block, near, :]
+                    target = pl.ds(begin - HALF + offset, 64)
+                    object_ref[part, layer, target, lane] = (
+                        ext_ref[part, layer, 1 + block, rows, :] - OBJECT_STEP * gradient
+                    )
+    swap_back.wait_recv()
+
+    def finish_probe(rows):
+        new_probe_ref[rows, :] = probe_ref[rows, :] - PROBE_STEP * gathered[rows, :]
+
+    by_rows(0, count, 64, finish_probe)
+    for item in gathers + [swap_back]:
+        item.wait_send()
+    links.finish()
+
+
+def vmem_specs(count):
+    return [pl.BlockSpec(memory_space=pltpu.VMEM)] * count
+
+
+def comm_params(identity):
+    return pltpu.CompilerParams(collective_id=identity, has_side_effects=True, vmem_limit_bytes=48 << 20)
+
+
+def semaphores(count):
+    return [pltpu.SemaphoreType.DMA((count,)), pltpu.SemaphoreType.DMA((count,))]
+
+
+EXTENDED = jax.ShapeDtypeStruct((2, 2, 4, 2 * SIDE, HALF), jnp.float32)
+
+
+def first_exchange(tile, amplitudes):
     slots = amplitudes.shape[0]
-    spec = pl.BlockSpec(memory_space=pltpu.VMEM)
     return pl.pallas_call(
-        reorder_kernel,
-        out_shape=jax.ShapeDtypeStruct((slots, SIDE, SIDE), jnp.float32),
-        in_specs=[spec, spec, spec],
-        out_specs=spec,
-        compiler_params=pltpu.CompilerParams(vmem_limit_bytes=16 << 20),
-        cost_estimate=pl.CostEstimate(flops=slots * 12 * SIDE**3, bytes_accessed=slots * 8 * SIDE * SIDE, transcendentals=0),
-    )(amplitudes, jnp.asarray(ORDER), jnp.asarray(ORDER.T))
+        first_kernel,
+        out_shape=(EXTENDED, jax.ShapeDtypeStruct((slots, SIDE, SIDE), jnp.float32)),
+        in_specs=vmem_specs(4),
+        out_specs=tuple(vmem_specs(2)),
+        scratch_shapes=semaphores(20),
+        compiler_params=comm_params(0),
+    )(tile, amplitudes, jnp.asarray(ORDER), jnp.asarray(ORDER.T))
+
+
+def columns_buffers():
+    return [pltpu.VMEM((2, 2, 2 * SIDE, HALF), jnp.float32)] * 2
+
+
+def middle_exchange(extended, gradient):
+    return pl.pallas_call(
+        middle_kernel,
+        out_shape=EXTENDED,
+        in_specs=vmem_specs(2),
+        out_specs=vmem_specs(1)[0],
+        scratch_shapes=[
+            *columns_buffers(),
+            *[pltpu.VMEM((2, 2, 2, SIDE, HALF), jnp.float32)] * 2,
+            pltpu.VMEM((2, 2, 2, 2 * SIDE, HALF), jnp.float32),
+            *semaphores(24),
+        ],
+        compiler_params=comm_params(1),
+    )(extended, gradient)
+
+
+def last_exchange(extended, gradient, first_probe, second_probe, probe_modes):
+    flat = (4 * SIDE, SIDE)
+    new_object, new_probe = pl.pallas_call(
+        last_kernel,
+        out_shape=(
+            jax.ShapeDtypeStruct((2, 2, SIDE, SIDE), jnp.float32),
+            jax.ShapeDtypeStruct(flat, jnp.float32),
+        ),
+        in_specs=vmem_specs(5),
+        out_specs=tuple(vmem_specs(2)),
+        scratch_shapes=[
+            *columns_buffers(),
+            *[pltpu.VMEM((2, 2, 2, HALF, HALF), jnp.float32)] * 2,
+            pltpu.VMEM((2, 2, 2, 2 * SIDE, HALF), jnp.float32),
+            pltpu.VMEM(flat, jnp.float32),
+            pltpu.VMEM((2 * SIDE, SIDE), jnp.float32),
+            [pltpu.VMEM((3, 2 * SIDE // 4**k, SIDE), jnp.float32) for k in (1, 2, 3)],
+            pltpu.VMEM(flat, jnp.float32),
+            pltpu.VMEM(flat, jnp.float32),
+            *semaphores(36),
+        ],
+        compiler_params=comm_params(2),
+    )(extended, gradient, first_probe.reshape(flat), second_probe.reshape(flat), probe_modes.reshape(flat))
+    return new_object, new_probe.reshape(probe_modes.shape)
 
 
 def batch_kernel(
@@ -351,55 +757,18 @@
     )(offsets, counts, extended, probe_modes, amplitudes, table)
 
 
-def from_behind(value, axis, steps):
-    count = lax.axis_size(axis)
-    leading, last = (max(0, -steps), min(count, count - steps))
-    return lax.ppermute(value, axis, [(source, source + steps) for source in range(leading, last)])
-
-
-def with_halo(array, sides, width):
-    for axis, dim in sides:
-        length = array.shape[dim]
-        last = lax.slice_in_dim(array, length - width, length, axis=dim)
-        leading = lax.slice_in_dim(array, 0, width, axis=dim)
-        before = from_behind(last, axis, 1)
-        after = from_behind(leading, axis, -1)
-        array = jnp.concatenate([before, array, after], axis=dim)
-    return array
-
-
-def return_sectioned(gradient, rim_width, tile_cells):
-    rim_start = rim_width + tile_cells
-    rim_end = tile_cells - rim_width
-    from_left = from_behind(gradient[:, :, :, rim_start:], "col", 1)
-    from_right = from_behind(gradient[:, :, :, :rim_width], "col", -1)
-    middle = gradient[:, :, :, rim_width:rim_start]
-    middle = middle.at[:, :, :, :rim_width].add(from_left)
-    middle = middle.at[:, :, :, rim_end:].add(from_right)
-    from_above = from_behind(middle[:, :, rim_start:, :], "row", 1)
-    from_below = from_behind(middle[:, :, :rim_width, :], "row", -1)
-    tile_grad = middle[:, :, rim_width:rim_start, :]
-    tile_grad = tile_grad.at[:, :, :rim_width, :].add(from_above)
-    tile_grad = tile_grad.at[:, :, rim_end:, :].add(from_below)
-    return tile_grad
-
-
 def body(object_field, probe_modes, amplitudes, offsets, counts):
     batches, slots = amplitudes.shape[:2]
     table = jnp.asarray(TABLES)
-    ordered = reorder(amplitudes.reshape(batches * slots, SIDE, SIDE)).reshape(batches, slots, SIDE, SIDE)
-    current = object_field
-    probe_total = None
-    for batch in range(batches):
-        extended = with_halo(current, (("row", 2), ("col", 3)), HALF)
-        extended = extended.reshape(2, 2, 2 * SIDE, 4, HALF).transpose(0, 1, 3, 2, 4)
-        gradient, probe_part = batch_terms(
-            extended, probe_modes, ordered[batch], offsets[batch, :, :, 0], counts[batch, 0], table
-        )
-        gradient = gradient.transpose(0, 1, 3, 2, 4).reshape(2, 2, 2 * SIDE, 2 * SIDE)
-        current = current - OBJECT_STEP * return_sectioned(gradient, HALF, SIDE)
-        probe_total = probe_part if probe_total is None else probe_total + probe_part
-    return (current, probe_modes - PROBE_STEP * lax.psum(probe_total, ("row", "col")))
+    extended, ordered = first_exchange(object_field, amplitudes.reshape(batches * slots, SIDE, SIDE))
+    ordered = ordered.reshape(batches, slots, SIDE, SIDE)
+    terms = lambda cells, batch: batch_terms(
+        cells, probe_modes, ordered[batch], offsets[batch, :, :, 0], counts[batch, 0], table
+    )
+    gradient, first_probe = terms(extended, 0)
+    extended = middle_exchange(extended, gradient)
+    gradient, second_probe = terms(extended, 1)
+    return last_exchange(extended, gradient, first_probe, second_probe, probe_modes)
 
 
 def solution(mesh):

time: 423 us -> 236 us (0.56)
  waiting for transfers between devices: 241 us -> 0 us
  Pallas kernels: 35.8 us -> 220 us
  starting transfers between devices: 64.8 us -> 0 us
  local copies, waits for them, and re-layouts: 47.6 us -> 14.7 us
  other arithmetic: 17.6 us -> 0 us
  between operations: 14.5 us -> 0.74 us
    pallas_call x1 -> x3, Pallas kernels: 4.06 us -> 202 us  [the longest x1 80.9 us: middle_exchange(): pl.pallas_call(middle_kernel, out_shape=EXTENDED, in_specs=vmem_specs(2),...]
    psum x1 -> x0, waiting for transfers between devices: 146 us -> none  [body(): lax.psum(probe_total, ('row', 'col'))]
    ppermute x16 -> x0, waiting for transfers between devices: 94.7 us -> none  [from_behind(): lax.ppermute(value, axis, [(source, source + steps) for source in range(l...]
    ppermute x16 -> x0, starting transfers between devices: 64.8 us -> none  [from_behind(): lax.ppermute(value, axis, [(source, source + steps) for source in range(l...]
    pallas_call x2, Pallas kernels: 31.8 us -> 17.5 us  [batch_terms(): pl.pallas_call(batch_kernel, out_shape=(jax.ShapeDtypeStruct((2, 2, 4, 2...]
    reshape x2 -> x0, local copies, waits for them, and re-layouts: 10.7 us -> none  [body(): extended.reshape(2, 2, 2 * SIDE, 4, HALF).transpose(0, 1, 3, 2, 4)]
    transpose x2 -> x0, local copies, waits for them, and re-layouts: 10.5 us -> none  [body(): gradient.transpose(0, 1, 3, 2, 4).reshape(2, 2, 2 * SIDE, 2 * SIDE)]
    slice x12 -> x0, local copies, waits for them, and re-layouts: 9.86 us -> none  [the longest x2 5.11 us: return_sectioned(): from_right = from_behind(gradient[:, :, :, :rim_width], 'col', -1)]
  transfers between devices with their start and end apart: 17 -> 0, of which waited for: 15 -> 0; matrix products, arithmetic and copies ran while one was open for 4% -> 0% of each run, Pallas kernels for 1% -> 0%
where the time goes in v2:
time: 236 us; the launch traced here: 235 us
  Pallas kernels  220 us (93%)
  local copies, waits for them, and re-layouts  14.7 us (6%)
    pallas_call x1, Pallas kernels, middle_exchange(): pl.pallas_call(middle_kernel, out_shape=EXTENDED, in_specs=vmem_specs(2),...  80.9 us
    pallas_call x1, Pallas kernels, last_exchange(): pl.pallas_call(last_kernel, out_shape=(jax.ShapeDtypeStruct((2, 2, SIDE,...  79.5 us
    pallas_call x1, Pallas kernels, first_exchange(): pl.pallas_call(first_kernel, out_shape=(EXTENDED, jax.ShapeDtypeStruct((s...  42 us
    pallas_call x2, Pallas kernels, batch_terms(): pl.pallas_call(batch_kernel, out_shape=(jax.ShapeDtypeStruct((2, 2, 4, 2...  17.5 us
    unnamed x22, local copies, waits for them, and re-layouts  12.5 us

profile of v2, /device:TPU:1, one launch (start us, length us, event | category | flops | bytes accessed | tf_op | source)
XLA Modules:
  0.0 235.3 jit_solution(18311094403861105376)
XLA Ops:
  0.6 1.3 fusion.2
  1.9 0.7 fusion.1
  2.6 0.0 copy-start.4
  2.6 1.4 copy-done.4
  4.0 0.0 copy-start.5
  4.1 1.2 copy-done.5
  5.3 0.0 copy-start.7
  5.3 0.9 copy-done.7
  6.2 0.0 copy-start.8
  6.2 0.9 copy-done.8
  7.1 0.0 copy-start.6
  7.1 0.0 copy-start.9
  7.1 42.0 %shard_map.95 = (f32[2,2,4,512,128]{4,3,2,1,0:T(8,128)}, f32[6,256,256]{2,1,0:T(8,128)S(1)}) custom-call(f32[2,2,256,256]{3,2,1,0:T(8,128)S(1)} %copy-done.5, f32[6,256,256]{2,1,0:T(8,128)S(1)} %bitcast.9, bf16[256,256]{1,0:T(8,128)(2,1)S(1)} %copy-done.8, bf16[256,256]{1,0:T(8,128)(2,1)S(1)} %copy-done.7), custom_call_target="tpu_custom_call" | custom-call | tf_op jit(solution)/shard_map/pallas_call | solution.py:438
  49.1 0.2 fusion
  49.2 0.0 copy-done.6
  49.2 0.0 copy-done.9
  49.2 0.0 copy-start.1
  49.3 2.2 copy-done.1
  51.4 8.7 %shard_map.96 = (f32[2,2,4,512,128]{4,3,2,1,0:T(8,128)S(1)}, f32[2,2,256,256]{3,2,1,0:T(8,128)S(1)}) custom-call(s32[2,3]{1,0:T(2,128)S(1)} %bitcast.15, s32[1]{0:T(128)} %bitcast.2.count_ref, f32[2,2,4,512,128]{4,3,2,1,0:T(8,128)S(1)} %copy-done.1, f32[2,2,256,256]{3,2,1,0:T(8,128)S(1)} %copy-done.6, f32[3,256,256]{2,1,0:T(8,128)S(1)} %get-tuple-element.19.amp_ref, ...), custom_call_target="tpu_custom_call" | custom-call | flops 3221225472 | bytes 12582912 | tf_op jit(solution)/shard_map/pallas_call | solution.py:735
  60.2 0.0 copy-start.2
  60.2 2.0 copy-done.2
  62.2 80.9 %shard_map.97.ext_ref = f32[2,2,4,512,128]{4,3,2,1,0:T(8,128)S(1)} custom-call(f32[2,2,4,512,128]{4,3,2,1,0:T(8,128)} %get-tuple-element.10.ext_ref, f32[2,2,4,512,128]{4,3,2,1,0:T(8,128)} %copy-done.2), custom_call_target="tpu_custom_call" | custom-call | tf_op jit(solution)/shard_map/pallas_call | solution.py:453
  143.1 0.0 copy-start
  143.1 8.8 %shard_map.98 = (f32[2,2,4,512,128]{4,3,2,1,0:T(8,128)S(1)}, f32[2,2,256,256]{3,2,1,0:T(8,128)S(1)}) custom-call(s32[2,3]{1,0:T(2,128)S(1)} %bitcast.14, s32[1]{0:T(128)} %bitcast.4.count_ref, f32[2,2,4,512,128]{4,3,2,1,0:T(8,128)S(1)} %shard_map.97.ext_ref, f32[2,2,256,256]{3,2,1,0:T(8,128)S(1)} %copy-done.6, f32[3,256,256]{2,1,0:T(8,128)S(1)} %get-tuple-element.18.amp_ref, ...), custom_call_target="tpu_custom_call" | custom-call | flops 3221225472 | bytes 12582912 | tf_op jit(solution)/shard_map/pallas_call | solution.py:735
  151.9 0.0 copy-done
  151.9 0.0 copy-start.3
  151.9 2.0 copy-done.3
  153.9 79.5 %shard_map.99 = (f32[2,2,256,256]{3,2,1,0:T(8,128)S(1)}, f32[1024,256]{1,0:T(8,128)S(1)}) custom-call(f32[2,2,4,512,128]{4,3,2,1,0:T(8,128)} %copy-done, f32[2,2,4,512,128]{4,3,2,1,0:T(8,128)} %copy-done.3, f32[1024,256]{1,0:T(8,128)S(1)} %bitcast.12, f32[1024,256]{1,0:T(8,128)S(1)} %bitcast.13, f32[1024,256]{1,0:T(8,128)S(1)} %bitcast.11), custom_call_target="tpu_custom_call" | custom-call | tf_op jit(solution)/shard_map/pallas_call | solution.py:470
  233.3 1.0 copy.12
  234.3 1.0 copy.13
Async XLA Ops:
  2.6 1.4 copy-start.4
  4.0 1.2 copy-start.5
  5.3 0.9 copy-start.7
  6.2 0.9 copy-start.8
  7.1 42.1 %copy-start.6 = (f32[2,2,256,256]{3,2,1,0:T(8,128)S(1)}, f32[2,2,256,256]{3,2,1,0:T(8,128)}, u32[]{:S(2)}) copy-start(f32[2,2,256,256]{3,2,1,0:T(8,128)} %probe_ref.3) | copy-start | bytes 3145732
  7.1 42.2 %copy-start.9 = (bf16[8,256,256]{2,1,0:T(8,128)(2,1)S(1)}, bf16[8,256,256]{2,1,0:T(8,128)(2,1)}, u32[]{:S(2)}) copy-start(bf16[8,256,256]{2,1,0:T(8,128)(2,1)} %constant.6.clone.table_ref) | copy-start | bytes 3145732
  49.2 2.2 copy-start.1
  60.2 2.0 copy-start.2
  143.1 8.8 %copy-start = (f32[2,2,4,512,128]{4,3,2,1,0:T(8,128)}, f32[2,2,4,512,128]{4,3,2,1,0:T(8,128)S(1)}, u32[]{:S(2)}) copy-start(f32[2,2,4,512,128]{4,3,2,1,0:T(8,128)S(1)} %shard_map.97.ext_ref) | copy-start | bytes 12582916
  151.9 2.0 copy-start.3

commit v3 on v2

--- a/solution.py
+++ b/solution.py
@@ -1,3 +1,4 @@
+import functools
 import math
 
 import jax
@@ -87,6 +88,11 @@
             "left": (self.row, self.col - 1),
             "right": (self.row, self.col + 1),
         }
+        middle, last = cols // 2, cols - 1
+        self.crosses = {"right": self.col == middle - 1, "left": self.col == middle}
+        self.relays = {"right": self.col == last, "left": self.col == 0}
+        self.relay = {"right": (self.row, last), "left": (self.row, 0)}
+        self.beyond = {"right": (self.row, middle), "left": (self.row, middle - 1)}
         self.send_sems, self.recv_sems = send_sems, recv_sems
         self.used = 0
         self.sent = []
@@ -99,18 +105,28 @@
             def _():
                 pl.semaphore_signal(barrier, inc=1, device_id=self.at[side], device_id_type=MESH)
 
+        inner = jnp.logical_or(self.crosses["left"], self.crosses["right"])
+        outer = jnp.logical_or(self.relays["left"], self.relays["right"])
+        for condition, devices in ((inner, self.relay), (outer, self.beyond)):
+
+            @pl.when(condition)
+            def _():
+                for side in ("left", "right"):
+                    pl.semaphore_signal(barrier, inc=1, device_id=devices[side], device_id_type=MESH)
+
         for peer in peers:
             pl.semaphore_signal(barrier, inc=1, device_id=peer, device_id_type=MESH)
-        pl.semaphore_wait(barrier, len(peers) + sum(self.has[side].astype(jnp.int32) for side in SIDES))
-
-    def copy(self, source, target, device):
+        extra = 2 * jnp.logical_or(inner, outer).astype(jnp.int32)
+        pl.semaphore_wait(barrier, len(peers) + extra + sum(self.has[side].astype(jnp.int32) for side in SIDES))
+
+    def copy(self, source, target, device, landing=None):
         index = self.used
         self.used += 1
         return pltpu.make_async_remote_copy(
             src_ref=source,
             dst_ref=target,
             send_sem=self.send_sems.at[index],
-            recv_sem=self.recv_sems.at[index],
+            recv_sem=self.recv_sems.at[index if landing is None else landing],
             device_id=device,
             device_id_type=MESH,
         )
@@ -134,6 +150,45 @@
 
         return arrived
 
+    def send_columns(self, source, target, side, slot, also=None):
+        rows = source.shape[-2]
+        lead = (slice(None),) * (len(source.shape) - 2)
+        first, second = (*lead, pl.ds(0, rows // 2)), (*lead, pl.ds(rows // 2, rows // 2))
+        item_index = self.used
+        head = self.copy(source.at[first], target.at[first], self.at[side])
+        tail = self.copy(source.at[second], target.at[second], self.at[side])
+        detour = self.copy(source.at[second], slot, self.relay[side])
+        onward = self.copy(slot, target.at[second], self.beyond[side], landing=item_index + 1)
+        both = lambda a: a if also is None else jnp.logical_and(a, also)
+        crosses = self.crosses[side]
+        going = [
+            (detour, both(crosses)),
+            (head, both(self.has[side])),
+            (tail, both(jnp.logical_and(self.has[side], jnp.logical_not(crosses)))),
+        ]
+        for item, condition in going:
+
+            @pl.when(condition)
+            def _():
+                item.start()
+
+        relays = both(self.relays[side])
+        self.sent += going + [(onward, relays)]
+        arrives = both(self.has[OPPOSITE[side]])
+
+        def arrived():
+            @pl.when(relays)
+            def _():
+                detour.wait_recv()
+                onward.start()
+
+            @pl.when(arrives)
+            def _():
+                head.wait_recv()
+                tail.wait_recv()
+
+        return arrived
+
     def finish(self):
         for item, condition in self.sent:
 
@@ -150,10 +205,26 @@
     lax.fori_loop(0, (stop - start) // step, one, 0)
 
 
-def first_kernel(tile_ref, amp_ref, order_ref, turn_ref, ext_ref, ordered_ref, send_sems, recv_sems):
+def first_kernel(
+    tile_ref, amp_ref, order_ref, turn_ref, ext_ref, ordered_ref,
+    planes, order, turn, tile_slots, corner_slots, local_sems, send_sems, recv_sems,
+):
     links = Links(send_sems, recv_sems)
+    upper, lower, own = pl.ds(0, HALF), pl.ds(3 * HALF, HALF), pl.ds(HALF, SIDE)
+    local = [
+        pltpu.make_async_copy(amp_ref, planes, local_sems.at[0]),
+        pltpu.make_async_copy(order_ref, order, local_sems.at[1]),
+        pltpu.make_async_copy(turn_ref, turn, local_sems.at[2]),
+    ]
+    inner = [
+        pltpu.make_async_copy(
+            tile_ref.at[:, :, :, pl.ds(block * HALF, HALF)], ext_ref.at[:, :, 1 + block, own], local_sems.at[3 + block]
+        )
+        for block in range(2)
+    ]
+    for item in local + inner:
+        item.start()
     links.greet()
-    upper, lower, own = pl.ds(0, HALF), pl.ds(3 * HALF, HALF), pl.ds(HALF, SIDE)
     waits, col_waits, corner_waits = [], [], []
     for layer in range(2):
         arrivals = []
@@ -166,17 +237,22 @@
                 links.send(tile_ref.at[:, layer, pl.ds(HALF, HALF), lane], ext_ref.at[:, layer, 1 + block, upper], "down")
             )
         waits.append(arrivals)
-    for layer in range(2):
-        col_waits.append(links.send(tile_ref.at[:, layer, :, pl.ds(0, HALF)], ext_ref.at[:, layer, 3, own], "left"))
-        col_waits.append(links.send(tile_ref.at[:, layer, :, pl.ds(HALF, HALF)], ext_ref.at[:, layer, 0, own], "right"))
+        for side, start, block in (("left", 0, 3), ("right", HALF, 0)):
+            col_waits.append(
+                links.send_columns(
+                    tile_ref.at[:, layer, :, pl.ds(start, HALF)],
+                    ext_ref.at[:, layer, block, own],
+                    side,
+                    tile_slots.at[layer],
+                )
+            )
 
     def clear(side, blocks, rows):
         @pl.when(jnp.logical_not(links.has[side]))
         def _():
-            for part in range(2):
-                for layer in range(2):
-                    for block in blocks:
-                        ext_ref[part, layer, block, rows, :] = jnp.zeros((rows.size, HALF), jnp.float32)
+            for part, layer in PLANES:
+                for block in blocks:
+                    ext_ref[part, layer, block, rows, :] = jnp.zeros((rows.size, HALF), jnp.float32)
 
     clear("up", (1, 2), upper)
     clear("down", (1, 2), lower)
@@ -187,36 +263,44 @@
 
             @pl.when(jnp.logical_not(jnp.logical_and(links.has[side], links.has[other])))
             def _():
-                for part in range(2):
-                    for layer in range(2):
-                        ext_ref[part, layer, block, rows, :] = jnp.zeros((HALF, HALF), jnp.float32)
-
-    for part in range(2):
-        for layer in range(2):
-            for block in range(2):
-                ext_ref[part, layer, 1 + block, own, :] = tile_ref[part, layer, :, block * HALF : (block + 1) * HALF]
+                for part, layer in PLANES:
+                    ext_ref[part, layer, block, rows, :] = jnp.zeros((HALF, HALF), jnp.float32)
+
+    for item in local:
+        item.wait()
 
     def one_plane(index, carry):
-        ordered_ref[index] = reorder_plane(amp_ref[index], order_ref[...], turn_ref[...])
+        ordered_ref[index] = reorder_plane(planes[index], order[...], turn[...])
         return carry
 
-    lax.fori_loop(0, amp_ref.shape[0], one_plane, 0)
+    lax.fori_loop(0, planes.shape[0], one_plane, 0)
+    for arrived in col_waits:
+        arrived()
     for layer in range(2):
         for arrived in waits[layer]:
             arrived()
-        for rows, side in ((upper, "up"), (lower, "down")):
+        for number, (rows, side) in enumerate(((upper, "up"), (lower, "down"))):
             for block, to, target in ((1, "left", 3), (2, "right", 0)):
                 corner_waits.append(
-                    links.send(
-                        ext_ref.at[:, layer, block, rows], ext_ref.at[:, layer, target, rows], to, also=links.has[side]
+                    links.send_columns(
+                        ext_ref.at[:, layer, block, rows],
+                        ext_ref.at[:, layer, target, rows],
+                        to,
+                        corner_slots.at[layer, number],
+                        also=links.has[side],
                     )
                 )
-    for arrived in col_waits + corner_waits:
+    for arrived in corner_waits:
         arrived()
+    for item in inner:
+        item.wait()
     links.finish()
 
 
-def collect_columns(links, grad_ref, from_left, from_right, total, order):
+PLANES = [(part, layer) for layer in range(2) for part in range(2)]
+
+
+def collect_columns(links, grad_ref, from_left, from_right, total, slots, order):
     for side, buffer in (("left", from_left), ("right", from_right)):
 
         @pl.when(jnp.logical_not(links.has[side]))
@@ -228,8 +312,8 @@
     for part, layer in order:
         arrivals.append(
             (
-                links.send(grad_ref.at[part, layer, 0], from_right.at[part, layer], "left"),
-                links.send(grad_ref.at[part, layer, 3], from_left.at[part, layer], "right"),
+                links.send_columns(grad_ref.at[part, layer, 0], from_right.at[part, layer], "left", slots.at[part, layer]),
+                links.send_columns(grad_ref.at[part, layer, 3], from_left.at[part, layer], "right", slots.at[part, layer]),
             )
         )
 
@@ -247,13 +331,12 @@
     return finish
 
 
-PLANES = [(part, layer) for layer in range(2) for part in range(2)]
-
-
-def middle_kernel(ext_ref, grad_ref, out_ref, from_left, from_right, from_up, from_down, total, send_sems, recv_sems):
+def middle_kernel(
+    ext_ref, grad_ref, out_ref, from_left, from_right, slots, from_up, from_down, total, halo_slots, send_sems, recv_sems
+):
     links = Links(send_sems, recv_sems)
     links.greet()
-    finish_columns = collect_columns(links, grad_ref, from_left, from_right, total, PLANES)
+    finish_columns = collect_columns(links, grad_ref, from_left, from_right, total, slots, PLANES)
     for side, buffer in (("up", from_up), ("down", from_down)):
 
         @pl.when(jnp.logical_not(links.has[side]))
@@ -294,8 +377,9 @@
                     rows, near = pl.ds(row, 64), pl.ds(row - offset, 64)
                     gradient = total[part, layer, block, rows, :] + buffer[part, layer, block, near, :]
                     out_ref[part, layer, 1 + block, rows, :] = ext_ref[part, layer, 1 + block, rows, :] - step * gradient
-        halos.append(links.send(out_ref.at[part, layer, 1], out_ref.at[part, layer, 3], "left"))
-        halos.append(links.send(out_ref.at[part, layer, 2], out_ref.at[part, layer, 0], "right"))
+        slot = halo_slots.at[part, layer]
+        halos.append(links.send_columns(out_ref.at[part, layer, 1], out_ref.at[part, layer, 3], "left", slot))
+        halos.append(links.send_columns(out_ref.at[part, layer, 2], out_ref.at[part, layer, 0], "right", slot))
     for arrived in halos:
         arrived()
     links.finish()
@@ -303,7 +387,7 @@
 
 def last_kernel(
     ext_ref, grad_ref, first_probe_ref, second_probe_ref, probe_ref, object_ref, new_probe_ref,
-    from_left, from_right, from_up, from_down, total, partial, pair, quarters, sums, gathered, send_sems, recv_sems,
+    from_left, from_right, slots, from_up, from_down, total, partial, pair, landings, sums, gathered, send_sems, recv_sems,
 ):
     links = Links(send_sems, recv_sems)
     row, col = links.row, links.col
@@ -311,16 +395,13 @@
     y_high, z = lax.rem(row, 2), row // 2
     y = y_high * 2 + y_low
     partner = (row, col + 1 - 2 * core)
-    groups = [
-        (z, lambda k: (k * 2 + y_high, col)),
-        (x, lambda k: (row, y_low * 8 + k * 2 + core)),
-        (y, lambda k: (z * 2 + k // 2, lax.rem(k, 2) * 8 + x * 2 + core)),
-    ]
+    plane = lambda k: ((k // 4) * 2 + y_high, y_low * 8 + lax.rem(k, 4) * 2 + core)
+    line = lambda k: (z * 2 + k // 2, lax.rem(k, 2) * 8 + x * 2 + core)
+    groups = [(z * 4 + x, plane, 16), (y, line, 4)]
     peers = [partner]
-    for place, device in groups:
-        peers += [device(lax.rem(place + k, 4)) for k in range(1, 4)]
+    for place, device, members in groups:
+        peers += [device(lax.rem(place + k, members)) for k in range(1, members)]
     links.greet(peers)
-    finish_columns = collect_columns(links, grad_ref, from_left, from_right, total, PLANES)
     count = 4 * SIDE
     half = count // 2
 
@@ -337,6 +418,7 @@
 
     by_rows(0, count, 64, add_probe)
     swap = start(partial.at[rows_at((1 - core) * half, half)], pair, partner)
+    finish_columns = collect_columns(links, grad_ref, from_left, from_right, total, slots, PLANES)
     for side, buffer in (("up", from_up), ("down", from_down)):
 
         @pl.when(jnp.logical_not(links.has[side]))
@@ -344,8 +426,42 @@
             for part, layer in PLANES:
                 buffer[part, layer] = jnp.zeros((2, HALF, HALF), jnp.float32)
 
+    swap.wait_recv()
+    base = core * half
+
+    def add_pair(index, carry):
+        near = pl.ds(pl.multiple_of(index * 64, 64), 64)
+        mine = rows_at(base + index * 64, 64)
+        sums[mine, :] = partial[mine, :] + pair[near, :]
+        return carry
+
+    lax.fori_loop(0, half // 64, add_pair, 0)
+    gathers = [swap]
+    places = []
     arrivals = []
-    for index, (part, layer) in enumerate(PLANES):
+
+    def scatter(number, base, size):
+        place, device, members = groups[number]
+        items = []
+        for k in range(1, members):
+            other = lax.rem(place + k, members)
+            source = sums.at[rows_at(base + other * size, size)]
+            items.append(start(source, landings[number].at[k - 1], device(other)))
+        gathers.extend(items)
+        places.append((place, device, members, base, size))
+        return items
+
+    def reduce(number, items, base, size):
+        for item in items:
+            item.wait_recv()
+        mine = rows_at(base, size)
+        value = sums[mine, :]
+        for k in range(len(items)):
+            value = value + landings[number][k]
+        (gathered if number == len(groups) - 1 else sums)[mine, :] = value
+
+    def rows_out(index):
+        part, layer = PLANES[index]
         finish_columns(index)
         arrivals.append(
             (
@@ -353,42 +469,24 @@
                 links.send(total.at[part, layer, :, pl.ds(3 * HALF, HALF)], from_up.at[part, layer], "down"),
             )
         )
-    swap.wait_recv()
-    base = core * half
-
-    def add_pair(index, carry):
-        near = pl.ds(pl.multiple_of(index * 64, 64), 64)
-        mine = rows_at(base + index * 64, 64)
-        sums[mine, :] = partial[mine, :] + pair[near, :]
-        return carry
-
-    lax.fori_loop(0, half // 64, add_pair, 0)
-    size = half
-    places = []
-    for number, (place, device) in enumerate(groups):
-        size = size // 4
-        landing = quarters[number]
-        items = []
-        for k in range(1, 4):
-            other = lax.rem(place + k, 4)
-            items.append(start(sums.at[rows_at(base + other * size, size)], landing.at[k - 1], device(other)))
-        places.append((place, device, base, size))
-        base = base + place * size
-        for item in items:
-            item.wait_recv()
-        for item in items:
-            item.wait_send()
-        for begin in range(0, size, 32):
-            step = min(32, size)
-            mine = rows_at(base + begin, step)
-            value = sums[mine, :]
-            for k in range(3):
-                value = value + landing[k, pl.ds(begin, step), :]
-            (gathered if number == 2 else sums)[mine, :] = value
-    gathers = [swap]
-    for place, device, group_base, size in reversed(places):
+
+    size = half // 16
+    items = scatter(0, base, size)
+    rows_out(0)
+    rows_out(1)
+    base = base + groups[0][0] * size
+    reduce(0, items, base, size)
+    size = size // 4
+    items = scatter(1, base, size)
+    rows_out(2)
+    rows_out(3)
+    base = base + groups[1][0] * size
+    reduce(1, items, base, size)
+    for place, device, members, group_base, size in reversed(places):
         mine = rows_at(group_base + place * size, size)
-        items = [start(gathered.at[mine], gathered.at[mine], device(lax.rem(place + k, 4))) for k in range(1, 4)]
+        items = [
+            start(gathered.at[mine], gathered.at[mine], device(lax.rem(place + k, members))) for k in range(1, members)
+        ]
         gathers += items
         for item in items:
             item.wait_recv()
@@ -422,31 +520,43 @@
     return [pl.BlockSpec(memory_space=pltpu.VMEM)] * count
 
 
-def comm_params(identity):
-    return pltpu.CompilerParams(collective_id=identity, has_side_effects=True, vmem_limit_bytes=48 << 20)
+def comm_params(identity, limit):
+    return pltpu.CompilerParams(collective_id=identity, has_side_effects=True, vmem_limit_bytes=limit << 20)
 
 
 def semaphores(count):
     return [pltpu.SemaphoreType.DMA((count,)), pltpu.SemaphoreType.DMA((count,))]
 
 
+def f32(*shape):
+    return pltpu.VMEM(shape, jnp.float32)
+
+
 EXTENDED = jax.ShapeDtypeStruct((2, 2, 4, 2 * SIDE, HALF), jnp.float32)
 
 
 def first_exchange(tile, amplitudes):
-    slots = amplitudes.shape[0]
+    planes = amplitudes.shape[0]
     return pl.pallas_call(
         first_kernel,
-        out_shape=(EXTENDED, jax.ShapeDtypeStruct((slots, SIDE, SIDE), jnp.float32)),
-        in_specs=vmem_specs(4),
+        out_shape=(EXTENDED, jax.ShapeDtypeStruct((planes, SIDE, SIDE), jnp.float32)),
+        in_specs=[pl.BlockSpec(memory_space=pltpu.HBM)] * 4,
         out_specs=tuple(vmem_specs(2)),
-        scratch_shapes=semaphores(20),
-        compiler_params=comm_params(0),
+        scratch_shapes=[
+            f32(planes, SIDE, SIDE),
+            pltpu.VMEM((SIDE, SIDE), jnp.bfloat16),
+            pltpu.VMEM((SIDE, SIDE), jnp.bfloat16),
+            f32(2, 2, HALF, HALF),
+            f32(2, 2, 2, HALF // 2, HALF),
+            pltpu.SemaphoreType.DMA((5,)),
+            *semaphores(8 + 16 + 32),
+        ],
+        compiler_params=comm_params(0, 14),
     )(tile, amplitudes, jnp.asarray(ORDER), jnp.asarray(ORDER.T))
 
 
 def columns_buffers():
-    return [pltpu.VMEM((2, 2, 2 * SIDE, HALF), jnp.float32)] * 2
+    return [f32(2, 2, 2 * SIDE, HALF), f32(2, 2, 2 * SIDE, HALF), f32(2, 2, SIDE, HALF)]
 
 
 def middle_exchange(extended, gradient):
@@ -457,11 +567,13 @@
         out_specs=vmem_specs(1)[0],
         scratch_shapes=[
             *columns_buffers(),
-            *[pltpu.VMEM((2, 2, 2, SIDE, HALF), jnp.float32)] * 2,
-            pltpu.VMEM((2, 2, 2, 2 * SIDE, HALF), jnp.float32),
-            *semaphores(24),
+            f32(2, 2, 2, SIDE, HALF),
+            f32(2, 2, 2, SIDE, HALF),
+            f32(2, 2, 2, 2 * SIDE, HALF),
+            f32(2, 2, SIDE, HALF),
+            *semaphores(32 + 8 + 32),
         ],
-        compiler_params=comm_params(1),
+        compiler_params=comm_params(1, 24),
     )(extended, gradient)
 
 
@@ -477,22 +589,23 @@
         out_specs=tuple(vmem_specs(2)),
         scratch_shapes=[
             *columns_buffers(),
-            *[pltpu.VMEM((2, 2, 2, HALF, HALF), jnp.float32)] * 2,
-            pltpu.VMEM((2, 2, 2, 2 * SIDE, HALF), jnp.float32),
-            pltpu.VMEM(flat, jnp.float32),
-            pltpu.VMEM((2 * SIDE, SIDE), jnp.float32),
-            [pltpu.VMEM((3, 2 * SIDE // 4**k, SIDE), jnp.float32) for k in (1, 2, 3)],
-            pltpu.VMEM(flat, jnp.float32),
-            pltpu.VMEM(flat, jnp.float32),
-            *semaphores(36),
+            f32(2, 2, 2, HALF, HALF),
+            f32(2, 2, 2, HALF, HALF),
+            f32(2, 2, 2, 2 * SIDE, HALF),
+            f32(*flat),
+            f32(2 * SIDE, SIDE),
+            [f32(15, 2 * SIDE // 16, SIDE), f32(3, 2 * SIDE // 64, SIDE)],
+            f32(*flat),
+            f32(*flat),
+            *semaphores(32 + 8 + 2 + 2 * 18),
         ],
-        compiler_params=comm_params(2),
+        compiler_params=comm_params(2, 26),
     )(extended, gradient, first_probe.reshape(flat), second_probe.reshape(flat), probe_modes.reshape(flat))
     return new_object, new_probe.reshape(probe_modes.shape)
 
 
 def batch_kernel(
-    offset_ref, count_ref, ext_ref, probe_ref, amp_ref, table_ref, grad_ref, probe_grad_ref,
+    batch, offset_ref, count_ref, ext_ref, probe_ref, amp_ref, table_ref, grad_ref, probe_grad_ref,
     obj, psi, right_a, right_b, yield_a, yield_b, left_a, left_b, out_a, out_b,
 ):
     lanes = lax.broadcasted_iota(jnp.int32, (CHUNK, HALF), 1)
@@ -503,7 +616,7 @@
             body(pl.multiple_of(index * CHUNK, CHUNK))
             return carry
 
-        lax.fori_loop(0, total // CHUNK, step, 0)
+        lax.fori_loop(0, total // CHUNK, step, 0, unroll=True)
 
     def bf(value):
         return value.astype(jnp.bfloat16)
@@ -598,8 +711,8 @@
         return [ref[first, second, pl.ds(row, CHUNK), lane] for lane in (lo, hi)]
 
     def one_slot(slot, carry):
-        start_row = offset_ref[0, slot]
-        start_col = offset_ref[1, slot]
+        start_row = offset_ref[batch, 0, slot, 0]
+        start_col = offset_ref[batch, 1, slot, 0]
         base = start_col // HALF
         shift = start_col % HALF
         take_left = lanes < HALF - shift
@@ -659,7 +772,7 @@
                     intensity = waves[0][0][k] * waves[0][0][k] + waves[0][1][k] * waves[0][1][k]
                     for re, im in waves[1:]:
                         intensity = intensity + (re[k] * re[k] + im[k] * im[k])
-                    amplitude = amp_ref[slot, pl.ds(base_row + row, CHUNK), lane]
+                    amplitude = amp_ref[batch * (amp_ref.shape[0] // 2) + slot, pl.ds(base_row + row, CHUNK), lane]
                     ratio = 1.0 - amplitude * lax.rsqrt(jnp.maximum(intensity, AMPLITUDE_FLOOR**2))
                     target = right_a if k == 0 else right_b
                     for mode, (re, im) in enumerate(waves):
@@ -725,15 +838,15 @@
         chunks(HALF, first_back)
         return carry
 
-    lax.fori_loop(0, count_ref[0], one_slot, 0)
-
-
-def batch_terms(extended, probe_modes, amplitudes, offsets, counts, table):
+    lax.fori_loop(0, count_ref[batch, 0, 0], one_slot, 0)
+
+
+def batch_terms(batch, extended, probe_modes, amplitudes, offsets, counts, table):
     vmem = pl.BlockSpec(memory_space=pltpu.VMEM)
     smem = pl.BlockSpec(memory_space=pltpu.SMEM)
     field = pltpu.VMEM((2, 2, SIDE, SIDE), jnp.float32)
     return pl.pallas_call(
-        batch_kernel,
+        functools.partial(batch_kernel, batch),
         out_shape=(
             jax.ShapeDtypeStruct((2, 2, 4, 2 * SIDE, HALF), jnp.float32),
             jax.ShapeDtypeStruct((2, MODES, SIDE, SIDE), jnp.float32),
@@ -752,7 +865,7 @@
             pltpu.VMEM((SIDE, MODES * SIDE), jnp.float32),
             pltpu.VMEM((SIDE, MODES * SIDE), jnp.float32),
         ],
-        compiler_params=pltpu.CompilerParams(vmem_limit_bytes=40 << 20),
+        compiler_params=pltpu.CompilerParams(vmem_limit_bytes=26 << 20),
         cost_estimate=pl.CostEstimate(flops=3 * 64 * SIDE**3, bytes_accessed=12 << 20, transcendentals=0),
     )(offsets, counts, extended, probe_modes, amplitudes, table)
 
@@ -761,10 +874,7 @@
     batches, slots = amplitudes.shape[:2]
     table = jnp.asarray(TABLES)
     extended, ordered = first_exchange(object_field, amplitudes.reshape(batches * slots, SIDE, SIDE))
-    ordered = ordered.reshape(batches, slots, SIDE, SIDE)
-    terms = lambda cells, batch: batch_terms(
-        cells, probe_modes, ordered[batch], offsets[batch, :, :, 0], counts[batch, 0], table
-    )
+    terms = lambda cells, batch: batch_terms(batch, cells, probe_modes, ordered, offsets, counts, table)
     gradient, first_probe = terms(extended, 0)
     extended = middle_exchange(extended, gradient)
     gradient, second_probe = terms(extended, 1)

time: 236 us -> 199 us (0.84)
  Pallas kernels: 220 us -> 186 us
  local copies, waits for them, and re-layouts: 14.7 us -> 10.4 us
    pallas_call x3, Pallas kernels: 59.5 us -> 45.8 us  [the longest x1 33.4 us: first_exchange(): pl.pallas_call(first_kernel, out_shape=(EXTENDED, jax.ShapeDtypeStruct((p...]
    pallas_call x1, Pallas kernels: 80.9 us -> 70.6 us  [middle_exchange(): pl.pallas_call(middle_kernel, out_shape=EXTENDED, in_specs=vmem_specs(2),...]
    pallas_call x1, Pallas kernels: 79.5 us -> 69.9 us  [last_exchange(): pl.pallas_call(last_kernel, out_shape=(jax.ShapeDtypeStruct((2, 2, SIDE,...]
    unnamed x22 -> x20, local copies, waits for them, and re-layouts: 12.5 us -> 10.4 us
where the time goes in v3:
time: 199 us; the launch traced here: 197 us
  Pallas kernels  186 us (93%)
  local copies, waits for them, and re-layouts  10.4 us (5%)
    pallas_call x1, Pallas kernels, middle_exchange(): pl.pallas_call(middle_kernel, out_shape=EXTENDED, in_specs=vmem_specs(2),...  70.6 us
    pallas_call x1, Pallas kernels, last_exchange(): pl.pallas_call(last_kernel, out_shape=(jax.ShapeDtypeStruct((2, 2, SIDE,...  69.9 us
    pallas_call x1, Pallas kernels, first_exchange(): pl.pallas_call(first_kernel, out_shape=(EXTENDED, jax.ShapeDtypeStruct((p...  33.4 us
    pallas_call x2, Pallas kernels, batch_terms(): pl.pallas_call(functools.partial(batch_kernel, batch), out_shape=(jax.Sha...  12.4 us
    unnamed x20, local copies, waits for them, and re-layouts  10.4 us

profile of v3, /device:TPU:1, one launch (start us, length us, event | category | flops | bytes accessed | tf_op | source)
XLA Modules:
  0.0 197.4 jit_solution(12103951467430834140)
XLA Ops:
  0.6 0.7 copy.11.count_ref
  1.4 0.8 copy.10.offset_ref
  2.2 0.0 copy-start
  2.2 1.4 copy-done
  3.6 0.0 copy-start.1
  3.6 1.2 copy-done.1
  4.8 0.0 copy-start.4
  4.8 0.9 copy-done.4
  5.7 0.0 copy-start.5
  5.7 0.9 copy-done.5
  6.6 33.4 %shard_map.95 = (f32[2,2,4,512,128]{4,3,2,1,0:T(8,128)S(1)}, f32[6,256,256]{2,1,0:T(8,128)S(1)}) custom-call(f32[2,2,256,256]{3,2,1,0:T(8,128)S(1)} %copy-done.1, f32[6,256,256]{2,1,0:T(8,128)S(1)} %bitcast.5, bf16[256,256]{1,0:T(8,128)(2,1)S(1)} %copy-done.5, bf16[256,256]{1,0:T(8,128)(2,1)S(1)} %copy-done.4), custom_call_target="tpu_custom_call" | custom-call | tf_op jit(solution)/shard_map/pallas_call | solution.py:540
  40.0 0.0 copy-start.2
  40.0 1.2 copy-done.2
  41.2 0.0 copy-start.6
  41.2 1.2 copy-done.6
  42.5 7.9 %shard_map.96 = (f32[2,2,4,512,128]{4,3,2,1,0:T(8,128)S(1)}, f32[2,2,256,256]{3,2,1,0:T(8,128)S(1)}) custom-call(s32[2,2,3,1]{3,2,1,0:T(4,128)S(1)} %copy.10.offset_ref, s32[2,1,1]{2,1,0:T(1,128)S(1)} %copy.11.count_ref, f32[2,2,4,512,128]{4,3,2,1,0:T(8,128)S(1)} %get-tuple-element.10.ext_ref, f32[2,2,256,256]{3,2,1,0:T(8,128)S(1)} %copy-done.2, ...), custom_call_target="tpu_custom_call" | custom-call | flops 3221225472 | bytes 12582912 | tf_op jit(solution)/shard_map/pallas_call | solution.py:848
  50.4 0.0 copy-start.3
  50.4 0.0 copy-start.7
  50.4 70.6 %shard_map.97.ext_ref = f32[2,2,4,512,128]{4,3,2,1,0:T(8,128)S(1)} custom-call(f32[2,2,4,512,128]{4,3,2,1,0:T(8,128)S(1)} %get-tuple-element.10.ext_ref, f32[2,2,4,512,128]{4,3,2,1,0:T(8,128)S(1)} %get-tuple-element.12.grad_ref), custom_call_target="tpu_custom_call" | custom-call | tf_op jit(solution)/shard_map/pallas_call | solution.py:563
  121.0 0.0 copy-done.3
  121.0 0.0 copy-done.7
  121.1 4.5 %shard_map.98 = (f32[2,2,4,512,128]{4,3,2,1,0:T(8,128)S(1)}, f32[2,2,256,256]{3,2,1,0:T(8,128)S(1)}) custom-call(s32[2,2,3,1]{3,2,1,0:T(4,128)S(1)} %copy.10.offset_ref, s32[2,1,1]{2,1,0:T(1,128)S(1)} %copy.11.count_ref, f32[2,2,4,512,128]{4,3,2,1,0:T(8,128)S(1)} %shard_map.97.ext_ref, f32[2,2,256,256]{3,2,1,0:T(8,128)S(1)} %copy-done.3, ...), custom_call_target="tpu_custom_call" | custom-call | flops 3221225472 | bytes 12582912 | tf_op jit(solution)/shard_map/pallas_call | solution.py:848
  125.5 69.9 %shard_map.99 = (f32[2,2,256,256]{3,2,1,0:T(8,128)S(1)}, f32[1024,256]{1,0:T(8,128)S(1)}) custom-call(f32[2,2,4,512,128]{4,3,2,1,0:T(8,128)S(1)} %shard_map.97.ext_ref, f32[2,2,4,512,128]{4,3,2,1,0:T(8,128)S(1)} %get-tuple-element.13.grad_ref, f32[1024,256]{1,0:T(8,128)S(1)} %bitcast.8, f32[1024,256]{1,0:T(8,128)S(1)} %bitcast.9, f32[1024,256]{1,0:T(8,128)S(1)} %bitcast.7), custom_call_target="tpu_custom_call" | custom-call | tf_op jit(solution)/shard_map/pallas_call | solution.py:582
  195.4 1.0 copy.16
  196.4 1.0 copy.17
Async XLA Ops:
  2.2 1.4 copy-start
  3.6 1.2 copy-start.1
  4.8 0.9 copy-start.4
  5.7 0.9 copy-start.5
  40.0 1.2 copy-start.2
  41.2 1.2 copy-start.6
  50.4 70.7 %copy-start.3 = (f32[2,2,256,256]{3,2,1,0:T(8,128)S(1)}, f32[2,2,256,256]{3,2,1,0:T(8,128)}, u32[]{:S(2)}) copy-start(f32[2,2,256,256]{3,2,1,0:T(8,128)} %probe_ref.3) | copy-start | bytes 3145732
  50.4 70.7 %copy-start.7 = (bf16[8,256,256]{2,1,0:T(8,128)(2,1)S(1)}, bf16[8,256,256]{2,1,0:T(8,128)(2,1)}, u32[]{:S(2)}) copy-start(bf16[8,256,256]{2,1,0:T(8,128)(2,1)} %constant.6.clone.table_ref) | copy-start | bytes 3145732

commit v4 on v3

--- a/solution.py
+++ b/solution.py
@@ -89,10 +89,11 @@
             "right": (self.row, self.col + 1),
         }
         middle, last = cols // 2, cols - 1
+        relays = {"right": (last, last - 2, last - 4), "left": (0, 2, 4)}
         self.crosses = {"right": self.col == middle - 1, "left": self.col == middle}
-        self.relays = {"right": self.col == last, "left": self.col == 0}
-        self.relay = {"right": (self.row, last), "left": (self.row, 0)}
         self.beyond = {"right": (self.row, middle), "left": (self.row, middle - 1)}
+        self.relay = {side: [(self.row, col) for col in relays[side]] for side in relays}
+        self.relays = {side: [self.col == col for col in relays[side]] for side in relays}
         self.send_sems, self.recv_sems = send_sems, recv_sems
         self.used = 0
         self.sent = []
@@ -106,27 +107,30 @@
                 pl.semaphore_signal(barrier, inc=1, device_id=self.at[side], device_id_type=MESH)
 
         inner = jnp.logical_or(self.crosses["left"], self.crosses["right"])
-        outer = jnp.logical_or(self.relays["left"], self.relays["right"])
-        for condition, devices in ((inner, self.relay), (outer, self.beyond)):
+        outer = functools.reduce(jnp.logical_or, self.relays["left"] + self.relays["right"])
+        extra = 6 * inner.astype(jnp.int32) + 2 * outer.astype(jnp.int32)
+        for condition, devices in (
+            (inner, self.relay["left"] + self.relay["right"]),
+            (outer, list(self.beyond.values())),
+        ):
 
             @pl.when(condition)
             def _():
-                for side in ("left", "right"):
-                    pl.semaphore_signal(barrier, inc=1, device_id=devices[side], device_id_type=MESH)
+                for device in devices:
+                    pl.semaphore_signal(barrier, inc=1, device_id=device, device_id_type=MESH)
 
         for peer in peers:
             pl.semaphore_signal(barrier, inc=1, device_id=peer, device_id_type=MESH)
-        extra = 2 * jnp.logical_or(inner, outer).astype(jnp.int32)
         pl.semaphore_wait(barrier, len(peers) + extra + sum(self.has[side].astype(jnp.int32) for side in SIDES))
 
-    def copy(self, source, target, device, landing=None):
+    def copy(self, source, target, device):
         index = self.used
         self.used += 1
         return pltpu.make_async_remote_copy(
             src_ref=source,
             dst_ref=target,
             send_sem=self.send_sems.at[index],
-            recv_sem=self.recv_sems.at[index if landing is None else landing],
+            recv_sem=self.recv_sems.at[index],
             device_id=device,
             device_id_type=MESH,
         )
@@ -150,44 +154,53 @@
 
         return arrived
 
-    def send_columns(self, source, target, side, slot, also=None):
+    def send_columns(self, source, target, side, slots, also=None):
         rows = source.shape[-2]
         lead = (slice(None),) * (len(source.shape) - 2)
-        first, second = (*lead, pl.ds(0, rows // 2)), (*lead, pl.ds(rows // 2, rows // 2))
-        item_index = self.used
-        head = self.copy(source.at[first], target.at[first], self.at[side])
-        tail = self.copy(source.at[second], target.at[second], self.at[side])
-        detour = self.copy(source.at[second], slot, self.relay[side])
-        onward = self.copy(slot, target.at[second], self.beyond[side], landing=item_index + 1)
+        halves = [(*lead, pl.ds(k * rows // 2, rows // 2)) for k in range(2)]
+        quarters = [(*lead, pl.ds(k * rows // 4, rows // 4)) for k in range(4)]
         both = lambda a: a if also is None else jnp.logical_and(a, also)
         crosses = self.crosses[side]
-        going = [
-            (detour, both(crosses)),
-            (head, both(self.has[side])),
-            (tail, both(jnp.logical_and(self.has[side], jnp.logical_not(crosses)))),
-        ]
+        direct = both(jnp.logical_and(self.has[side], jnp.logical_not(crosses)))
+        whole = [(self.copy(source.at[at], target.at[at], self.at[side]), direct) for at in halves]
+        first = self.copy(source.at[quarters[0]], target.at[quarters[0]], self.at[side])
+        detours, onwards = [], []
+        for k in range(3):
+            at = quarters[k + 1]
+            detours.append(self.copy(source.at[at], slots.at[k], self.relay[side][k]))
+            onwards.append(self.copy(slots.at[k], target.at[at], self.beyond[side]))
+        going = [(item, both(crosses)) for item in [*detours, first]] + whole
         for item, condition in going:
 
             @pl.when(condition)
             def _():
                 item.start()
 
-        relays = both(self.relays[side])
-        self.sent += going + [(onward, relays)]
-        arrives = both(self.has[OPPOSITE[side]])
-
-        def arrived():
-            @pl.when(relays)
+        relays = [both(here) for here in self.relays[side]]
+        self.sent += going + list(zip(onwards, relays))
+        receives_parts = self.crosses[OPPOSITE[side]]
+        receives_whole = both(jnp.logical_and(self.has[OPPOSITE[side]], jnp.logical_not(receives_parts)))
+        receives_parts = both(receives_parts)
+
+        def forward():
+            for detour, onward, here in zip(detours, onwards, relays):
+
+                @pl.when(here)
+                def _():
+                    detour.wait_recv()
+                    onward.start()
+
+        def arrived(half):
+            @pl.when(receives_whole)
             def _():
-                detour.wait_recv()
-                onward.start()
-
-            @pl.when(arrives)
+                whole[half][0].wait_recv()
+
+            @pl.when(receives_parts)
             def _():
-                head.wait_recv()
-                tail.wait_recv()
-
-        return arrived
+                for item in (first, onwards[0]) if half == 0 else onwards[1:]:
+                    item.wait_recv()
+
+        return forward, arrived
 
     def finish(self):
         for item, condition in self.sent:
@@ -206,7 +219,7 @@
 
 
 def first_kernel(
-    tile_ref, amp_ref, order_ref, turn_ref, ext_ref, ordered_ref,
+    tile_ref, amp_ref, order_ref, turn_ref, table_ref, probe_ref, ext_ref, ordered_ref, table_out, probe_out,
     planes, order, turn, tile_slots, corner_slots, local_sems, send_sems, recv_sems,
 ):
     links = Links(send_sems, recv_sems)
@@ -222,7 +235,11 @@
         )
         for block in range(2)
     ]
-    for item in local + inner:
+    extra = [
+        pltpu.make_async_copy(table_ref, table_out, local_sems.at[5]),
+        pltpu.make_async_copy(probe_ref, probe_out, local_sems.at[6]),
+    ]
+    for item in local + inner + extra:
         item.start()
     links.greet()
     waits, col_waits, corner_waits = [], [], []
@@ -274,8 +291,8 @@
         return carry
 
     lax.fori_loop(0, planes.shape[0], one_plane, 0)
-    for arrived in col_waits:
-        arrived()
+    for forward, _ in col_waits:
+        forward()
     for layer in range(2):
         for arrived in waits[layer]:
             arrived()
@@ -290,10 +307,13 @@
                         also=links.has[side],
                     )
                 )
-    for arrived in corner_waits:
-        arrived()
-    for item in inner:
+    for forward, _ in corner_waits:
+        forward()
+    for item in inner + extra:
         item.wait()
+    for _, arrived in col_waits + corner_waits:
+        for half in range(2):
+            arrived(half)
     links.finish()
 
 
@@ -317,16 +337,18 @@
             )
         )
 
-    def finish(index):
+    def finish(index, half):
         part, layer = order[index]
-        for arrived in arrivals[index]:
-            arrived()
+        for forward, arrived in arrivals[index]:
+            if half == 0:
+                forward()
+            arrived(half)
 
         def add(rows):
             total[part, layer, 0, rows, :] = grad_ref[part, layer, 1, rows, :] + from_left[part, layer, rows, :]
             total[part, layer, 1, rows, :] = grad_ref[part, layer, 2, rows, :] + from_right[part, layer, rows, :]
 
-        by_rows(0, 2 * SIDE, 64, add)
+        by_rows(half * SIDE, (half + 1) * SIDE, 64, add)
 
     return finish
 
@@ -353,13 +375,11 @@
 
     arrivals = []
     for index, (part, layer) in enumerate(PLANES):
-        finish_columns(index)
-        arrivals.append(
-            (
-                links.send(total.at[part, layer, :, pl.ds(0, SIDE)], from_down.at[part, layer], "up"),
-                links.send(total.at[part, layer, :, pl.ds(SIDE, SIDE)], from_up.at[part, layer], "down"),
-            )
-        )
+        finish_columns(index, 0)
+        up = links.send(total.at[part, layer, :, pl.ds(0, SIDE)], from_down.at[part, layer], "up")
+        finish_columns(index, 1)
+        down = links.send(total.at[part, layer, :, pl.ds(SIDE, SIDE)], from_up.at[part, layer], "down")
+        arrivals.append((up, down))
     step_up = jnp.where(links.has["up"], OBJECT_STEP, 0.0).astype(jnp.float32)
     step_down = jnp.where(links.has["down"], OBJECT_STEP, 0.0).astype(jnp.float32)
     halos = []
@@ -380,8 +400,13 @@
         slot = halo_slots.at[part, layer]
         halos.append(links.send_columns(out_ref.at[part, layer, 1], out_ref.at[part, layer, 3], "left", slot))
         halos.append(links.send_columns(out_ref.at[part, layer, 2], out_ref.at[part, layer, 0], "right", slot))
-    for arrived in halos:
-        arrived()
+        for forward, _ in halos[2 * index - 2 : 2 * index]:
+            forward()
+    for forward, _ in halos[-2:]:
+        forward()
+    for _, arrived in halos:
+        for half in range(2):
+            arrived(half)
     links.finish()
 
 
@@ -462,13 +487,11 @@
 
     def rows_out(index):
         part, layer = PLANES[index]
-        finish_columns(index)
-        arrivals.append(
-            (
-                links.send(total.at[part, layer, :, pl.ds(0, HALF)], from_down.at[part, layer], "up"),
-                links.send(total.at[part, layer, :, pl.ds(3 * HALF, HALF)], from_up.at[part, layer], "down"),
-            )
-        )
+        finish_columns(index, 0)
+        up = links.send(total.at[part, layer, :, pl.ds(0, HALF)], from_down.at[part, layer], "up")
+        finish_columns(index, 1)
+        down = links.send(total.at[part, layer, :, pl.ds(3 * HALF, HALF)], from_up.at[part, layer], "down")
+        arrivals.append((up, down))
 
     size = half // 16
     items = scatter(0, base, size)
@@ -535,28 +558,34 @@
 EXTENDED = jax.ShapeDtypeStruct((2, 2, 4, 2 * SIDE, HALF), jnp.float32)
 
 
-def first_exchange(tile, amplitudes):
+def first_exchange(tile, amplitudes, table, probe_modes):
     planes = amplitudes.shape[0]
+    inputs = (tile, amplitudes, jnp.asarray(ORDER), jnp.asarray(ORDER.T), table, probe_modes)
     return pl.pallas_call(
         first_kernel,
-        out_shape=(EXTENDED, jax.ShapeDtypeStruct((planes, SIDE, SIDE), jnp.float32)),
-        in_specs=[pl.BlockSpec(memory_space=pltpu.HBM)] * 4,
-        out_specs=tuple(vmem_specs(2)),
+        out_shape=(
+            EXTENDED,
+            jax.ShapeDtypeStruct((planes, SIDE, SIDE), jnp.float32),
+            jax.ShapeDtypeStruct(table.shape, table.dtype),
+            jax.ShapeDtypeStruct(probe_modes.shape, probe_modes.dtype),
+        ),
+        in_specs=[pl.BlockSpec(memory_space=pltpu.HBM)] * 6,
+        out_specs=tuple(vmem_specs(4)),
         scratch_shapes=[
             f32(planes, SIDE, SIDE),
             pltpu.VMEM((SIDE, SIDE), jnp.bfloat16),
             pltpu.VMEM((SIDE, SIDE), jnp.bfloat16),
-            f32(2, 2, HALF, HALF),
-            f32(2, 2, 2, HALF // 2, HALF),
-            pltpu.SemaphoreType.DMA((5,)),
-            *semaphores(8 + 16 + 32),
+            f32(2, 3, 2, SIDE // 4, HALF),
+            f32(2, 2, 3, 2, HALF // 4, HALF),
+            pltpu.SemaphoreType.DMA((7,)),
+            *semaphores(8 + 9 * 12),
         ],
         compiler_params=comm_params(0, 14),
-    )(tile, amplitudes, jnp.asarray(ORDER), jnp.asarray(ORDER.T))
+    )(*[pltpu.with_memory_space_constraint(value, pltpu.HBM) for value in inputs])
 
 
 def columns_buffers():
-    return [f32(2, 2, 2 * SIDE, HALF), f32(2, 2, 2 * SIDE, HALF), f32(2, 2, SIDE, HALF)]
+    return [f32(2, 2, 2 * SIDE, HALF), f32(2, 2, 2 * SIDE, HALF), f32(2, 2, 3, HALF, HALF)]
 
 
 def middle_exchange(extended, gradient):
@@ -570,8 +599,8 @@
             f32(2, 2, 2, SIDE, HALF),
             f32(2, 2, 2, SIDE, HALF),
             f32(2, 2, 2, 2 * SIDE, HALF),
-            f32(2, 2, SIDE, HALF),
-            *semaphores(32 + 8 + 32),
+            f32(2, 2, 3, HALF, HALF),
+            *semaphores(72 + 8 + 72),
         ],
         compiler_params=comm_params(1, 24),
     )(extended, gradient)
@@ -597,7 +626,7 @@
             [f32(15, 2 * SIDE // 16, SIDE), f32(3, 2 * SIDE // 64, SIDE)],
             f32(*flat),
             f32(*flat),
-            *semaphores(32 + 8 + 2 + 2 * 18),
+            *semaphores(72 + 8 + 2 + 2 * 18),
         ],
         compiler_params=comm_params(2, 26),
     )(extended, gradient, first_probe.reshape(flat), second_probe.reshape(flat), probe_modes.reshape(flat))
@@ -873,7 +902,9 @@
 def body(object_field, probe_modes, amplitudes, offsets, counts):
     batches, slots = amplitudes.shape[:2]
     table = jnp.asarray(TABLES)
-    extended, ordered = first_exchange(object_field, amplitudes.reshape(batches * slots, SIDE, SIDE))
+    extended, ordered, table, probe_modes = first_exchange(
+        object_field, amplitudes.reshape(batches * slots, SIDE, SIDE), table, probe_modes
+    )
     terms = lambda cells, batch: batch_terms(batch, cells, probe_modes, ordered, offsets, counts, table)
     gradient, first_probe = terms(extended, 0)
     extended = middle_exchange(extended, gradient)

time: 199 us -> 190 us (0.955)
  local copies, waits for them, and re-layouts: 10.4 us -> 3.47 us
    unnamed x20 -> x4, local copies, waits for them, and re-layouts: 10.4 us -> 3.47 us
    pallas_call x2, Pallas kernels: 12.4 us -> 8.93 us  [batch_terms(): pl.pallas_call(functools.partial(batch_kernel, batch), out_shape=(jax.Sha...]
    pallas_call x1, Pallas kernels: 33.4 us -> 35.9 us  [first_exchange(): pl.pallas_call(first_kernel, out_shape=(EXTENDED, jax.ShapeDtypeStruct((p...]
where the time goes in v4:
time: 190 us; the launch traced here: 189 us
  Pallas kernels  185 us (97%)
  local copies, waits for them, and re-layouts  3.47 us (2%)
    pallas_call x1, Pallas kernels, middle_exchange(): pl.pallas_call(middle_kernel, out_shape=EXTENDED, in_specs=vmem_specs(2),...  71 us
    pallas_call x1, Pallas kernels, last_exchange(): pl.pallas_call(last_kernel, out_shape=(jax.ShapeDtypeStruct((2, 2, SIDE,...  69.5 us
    pallas_call x1, Pallas kernels, first_exchange(): pl.pallas_call(first_kernel, out_shape=(EXTENDED, jax.ShapeDtypeStruct((p...  35.9 us
    pallas_call x2, Pallas kernels, batch_terms(): pl.pallas_call(functools.partial(batch_kernel, batch), out_shape=(jax.Sha...  8.93 us

profile of v4, /device:TPU:1, one launch (start us, length us, event | category | flops | bytes accessed | tf_op | source)
XLA Modules:
  0.0 189.5 jit_solution(1685124736648620970)
XLA Ops:
  0.6 0.7 copy.11.count_ref
  1.4 0.8 copy.10.offset_ref
  2.2 35.9 %shard_map.95 = (f32[2,2,4,512,128]{4,3,2,1,0:T(8,128)S(1)}, f32[6,256,256]{2,1,0:T(8,128)S(1)}, bf16[8,256,256]{2,1,0:T(8,128)(2,1)S(1)}, f32[2,2,256,256]{3,2,1,0:T(8,128)S(1)}) custom-call(f32[2,2,256,256]{3,2,1,0:T(8,128)} %tile_ref.1, f32[6,256,256]{2,1,0:T(8,128)} %bitcast.9, bf16[256,256]{1,0:T(8,128)(2,1)} %constant.7.clone.order_ref, ...), custom_call_target="tpu_custom_call" | custom-call | tf_op jit(solution)/shard_map/pallas_call | solution.py:564
  38.0 4.5 %shard_map.96 = (f32[2,2,4,512,128]{4,3,2,1,0:T(8,128)S(1)}, f32[2,2,256,256]{3,2,1,0:T(8,128)S(1)}) custom-call(s32[2,2,3,1]{3,2,1,0:T(4,128)S(1)} %copy.10.offset_ref, s32[2,1,1]{2,1,0:T(1,128)S(1)} %copy.11.count_ref, f32[2,2,4,512,128]{4,3,2,1,0:T(8,128)S(1)} %get-tuple-element.12.ext_ref, f32[2,2,256,256]{3,2,1,0:T(8,128)S(1)} %get-tuple-element.13.probe_ref, ...), custom_call_target="tpu_custom_call" | custom-call | flops 3221225472 | bytes 12582912 | tf_op jit(solution)/shard_map/pallas_call | solution.py:877
  42.5 71.0 %shard_map.97.ext_ref = f32[2,2,4,512,128]{4,3,2,1,0:T(8,128)S(1)} custom-call(f32[2,2,4,512,128]{4,3,2,1,0:T(8,128)S(1)} %get-tuple-element.12.ext_ref, f32[2,2,4,512,128]{4,3,2,1,0:T(8,128)S(1)} %get-tuple-element.16.grad_ref), custom_call_target="tpu_custom_call" | custom-call | tf_op jit(solution)/shard_map/pallas_call | solution.py:592
  113.6 4.4 %shard_map.98 = (f32[2,2,4,512,128]{4,3,2,1,0:T(8,128)S(1)}, f32[2,2,256,256]{3,2,1,0:T(8,128)S(1)}) custom-call(s32[2,2,3,1]{3,2,1,0:T(4,128)S(1)} %copy.10.offset_ref, s32[2,1,1]{2,1,0:T(1,128)S(1)} %copy.11.count_ref, f32[2,2,4,512,128]{4,3,2,1,0:T(8,128)S(1)} %shard_map.97.ext_ref, f32[2,2,256,256]{3,2,1,0:T(8,128)S(1)} %get-tuple-element.13.probe_ref, ...), custom_call_target="tpu_custom_call" | custom-call | flops 3221225472 | bytes 12582912 | tf_op jit(solution)/shard_map/pallas_call | solution.py:877
  118.0 69.5 %shard_map.99 = (f32[2,2,256,256]{3,2,1,0:T(8,128)S(1)}, f32[1024,256]{1,0:T(8,128)S(1)}) custom-call(f32[2,2,4,512,128]{4,3,2,1,0:T(8,128)S(1)} %shard_map.97.ext_ref, f32[2,2,4,512,128]{4,3,2,1,0:T(8,128)S(1)} %get-tuple-element.17.grad_ref, f32[1024,256]{1,0:T(8,128)S(1)} %bitcast.7, f32[1024,256]{1,0:T(8,128)S(1)} %bitcast.8, f32[1024,256]{1,0:T(8,128)S(1)} %bitcast.6), custom_call_target="tpu_custom_call" | custom-call | tf_op jit(solution)/shard_map/pallas_call | solution.py:611
  187.6 1.0 copy.16
  188.5 1.0 copy.17

commit v5 on v4

--- a/solution.py
+++ b/solution.py
@@ -16,6 +16,10 @@
 HALF = SIDE // 2
 MODES = 2
 CHUNK = 16
+RELAYED_CORNER_LAYERS = 1
+MIDDLE_DIRECT_GRADIENTS = (0,)
+MIDDLE_DIRECT_HALOS = (3,)
+LAST_DIRECT_GRADIENTS = (0,)
 MESH = pl.DeviceIdType.MESH
 SIDES = ("up", "down", "left", "right")
 OPPOSITE = {"up": "down", "down": "up", "left": "right", "right": "left"}
@@ -154,7 +158,16 @@
 
         return arrived
 
-    def send_columns(self, source, target, side, slots, also=None):
+    def send_straight(self, source, target, side, also):
+        rows = source.shape[-2]
+        lead = (slice(None),) * (len(source.shape) - 2)
+        halves = [(*lead, pl.ds(k * rows // 2, rows // 2)) for k in range(2)]
+        waits = [self.send(source.at[at], target.at[at], side, also) for at in halves]
+        return (lambda: None), (lambda half: waits[half]())
+
+    def send_columns(self, source, target, side, slots, also=None, relay=True):
+        if not relay:
+            return self.send_straight(source, target, side, also)
         rows = source.shape[-2]
         lead = (slice(None),) * (len(source.shape) - 2)
         halves = [(*lead, pl.ds(k * rows // 2, rows // 2)) for k in range(2)]
@@ -244,6 +257,16 @@
     links.greet()
     waits, col_waits, corner_waits = [], [], []
     for layer in range(2):
+        for side, start, block in (("left", 0, 3), ("right", HALF, 0)):
+            col_waits.append(
+                links.send_columns(
+                    tile_ref.at[:, layer, :, pl.ds(start, HALF)],
+                    ext_ref.at[:, layer, block, own],
+                    side,
+                    tile_slots.at[layer],
+                )
+            )
+    for layer in range(2):
         arrivals = []
         for block in range(2):
             lane = pl.ds(block * HALF, HALF)
@@ -254,15 +277,6 @@
                 links.send(tile_ref.at[:, layer, pl.ds(HALF, HALF), lane], ext_ref.at[:, layer, 1 + block, upper], "down")
             )
         waits.append(arrivals)
-        for side, start, block in (("left", 0, 3), ("right", HALF, 0)):
-            col_waits.append(
-                links.send_columns(
-                    tile_ref.at[:, layer, :, pl.ds(start, HALF)],
-                    ext_ref.at[:, layer, block, own],
-                    side,
-                    tile_slots.at[layer],
-                )
-            )
 
     def clear(side, blocks, rows):
         @pl.when(jnp.logical_not(links.has[side]))
@@ -305,6 +319,7 @@
                         to,
                         corner_slots.at[layer, number],
                         also=links.has[side],
+                        relay=layer < RELAYED_CORNER_LAYERS,
                     )
                 )
     for forward, _ in corner_waits:
@@ -320,7 +335,7 @@
 PLANES = [(part, layer) for layer in range(2) for part in range(2)]
 
 
-def collect_columns(links, grad_ref, from_left, from_right, total, slots, order):
+def collect_columns(links, grad_ref, from_left, from_right, total, slots, order, straight):
     for side, buffer in (("left", from_left), ("right", from_right)):
 
         @pl.when(jnp.logical_not(links.has[side]))
@@ -329,11 +344,12 @@
                 buffer[part, layer] = jnp.zeros((2 * SIDE, HALF), jnp.float32)
 
     arrivals = []
-    for part, layer in order:
+    for number, (part, layer) in enumerate(order):
+        relay = number not in straight
         arrivals.append(
             (
-                links.send_columns(grad_ref.at[part, layer, 0], from_right.at[part, layer], "left", slots.at[part, layer]),
-                links.send_columns(grad_ref.at[part, layer, 3], from_left.at[part, layer], "right", slots.at[part, layer]),
+                links.send_columns(grad_ref.at[part, layer, 0], from_right.at[part, layer], "left", slots.at[part, layer], relay=relay),
+                links.send_columns(grad_ref.at[part, layer, 3], from_left.at[part, layer], "right", slots.at[part, layer], relay=relay),
             )
         )
 
@@ -358,7 +374,7 @@
 ):
     links = Links(send_sems, recv_sems)
     links.greet()
-    finish_columns = collect_columns(links, grad_ref, from_left, from_right, total, slots, PLANES)
+    finish_columns = collect_columns(links, grad_ref, from_left, from_right, total, slots, PLANES, MIDDLE_DIRECT_GRADIENTS)
     for side, buffer in (("up", from_up), ("down", from_down)):
 
         @pl.when(jnp.logical_not(links.has[side]))
@@ -398,8 +414,8 @@
                     gradient = total[part, layer, block, rows, :] + buffer[part, layer, block, near, :]
                     out_ref[part, layer, 1 + block, rows, :] = ext_ref[part, layer, 1 + block, rows, :] - step * gradient
         slot = halo_slots.at[part, layer]
-        halos.append(links.send_columns(out_ref.at[part, layer, 1], out_ref.at[part, layer, 3], "left", slot))
-        halos.append(links.send_columns(out_ref.at[part, layer, 2], out_ref.at[part, layer, 0], "right", slot))
+        halos.append(links.send_columns(out_ref.at[part, layer, 1], out_ref.at[part, layer, 3], "left", slot, relay=index not in MIDDLE_DIRECT_HALOS))
+        halos.append(links.send_columns(out_ref.at[part, layer, 2], out_ref.at[part, layer, 0], "right", slot, relay=index not in MIDDLE_DIRECT_HALOS))
         for forward, _ in halos[2 * index - 2 : 2 * index]:
             forward()
     for forward, _ in halos[-2:]:
@@ -443,7 +459,7 @@
 
     by_rows(0, count, 64, add_probe)
     swap = start(partial.at[rows_at((1 - core) * half, half)], pair, partner)
-    finish_columns = collect_columns(links, grad_ref, from_left, from_right, total, slots, PLANES)
+    finish_columns = collect_columns(links, grad_ref, from_left, from_right, total, slots, PLANES, LAST_DIRECT_GRADIENTS)
     for side, buffer in (("up", from_up), ("down", from_down)):
 
         @pl.when(jnp.logical_not(links.has[side]))
@@ -462,72 +478,109 @@
 
     lax.fori_loop(0, half // 64, add_pair, 0)
     gathers = [swap]
-    places = []
-    arrivals = []
-
-    def scatter(number, base, size):
-        place, device, members = groups[number]
+
+    piece = half // 16
+    plane_base = base + (z * 4 + x) * piece
+    mine = rows_at(plane_base, piece)
+    plane_peers = [device for device in peers[1:16]]
+    line_peers = peers[16:]
+
+    def spread_plane():
         items = []
-        for k in range(1, members):
-            other = lax.rem(place + k, members)
-            source = sums.at[rows_at(base + other * size, size)]
-            items.append(start(source, landings[number].at[k - 1], device(other)))
+        for k in range(1, 16):
+            other = lax.rem(z * 4 + x + k, 16)
+            source = sums.at[rows_at(base + other * piece, piece)]
+            items.append(start(source, landings[0].at[k - 1], plane_peers[k - 1]))
         gathers.extend(items)
-        places.append((place, device, members, base, size))
         return items
 
-    def reduce(number, items, base, size):
+    def add_plane(items):
         for item in items:
             item.wait_recv()
-        mine = rows_at(base, size)
         value = sums[mine, :]
-        for k in range(len(items)):
-            value = value + landings[number][k]
-        (gathered if number == len(groups) - 1 else sums)[mine, :] = value
-
-    def rows_out(index):
-        part, layer = PLANES[index]
-        finish_columns(index, 0)
-        up = links.send(total.at[part, layer, :, pl.ds(0, HALF)], from_down.at[part, layer], "up")
-        finish_columns(index, 1)
-        down = links.send(total.at[part, layer, :, pl.ds(3 * HALF, HALF)], from_up.at[part, layer], "down")
-        arrivals.append((up, down))
-
-    size = half // 16
-    items = scatter(0, base, size)
-    rows_out(0)
-    rows_out(1)
-    base = base + groups[0][0] * size
-    reduce(0, items, base, size)
-    size = size // 4
-    items = scatter(1, base, size)
-    rows_out(2)
-    rows_out(3)
-    base = base + groups[1][0] * size
-    reduce(1, items, base, size)
-    for place, device, members, group_base, size in reversed(places):
-        mine = rows_at(group_base + place * size, size)
-        items = [
-            start(gathered.at[mine], gathered.at[mine], device(lax.rem(place + k, members))) for k in range(1, members)
-        ]
-        gathers += items
+        for k in range(15):
+            value = value + landings[0][k]
+        landings[1][y] = value
+
+    def spread_line():
+        items = [start(landings[1].at[y], landings[1].at[y], device) for device in line_peers]
+        gathers.extend(items)
+        return items
+
+    def add_line(items):
         for item in items:
             item.wait_recv()
-    mine = rows_at(core * half, half)
-    swap_back = start(gathered.at[mine], gathered.at[mine], partner)
-    for index, (part, layer) in enumerate(PLANES):
-        for arrived in arrivals[index]:
+        gathered[mine, :] = (landings[1][0] + landings[1][1]) + (landings[1][2] + landings[1][3])
+
+    def share_plane():
+        items = [start(gathered.at[mine], gathered.at[mine], device) for device in plane_peers]
+        gathers.extend(items)
+        return items
+
+    def await_all(items):
+        for item in items:
+            item.wait_recv()
+
+    held, arrivals = {}, {}
+
+    def issue(number):
+        part, layer = PLANES[number // 2]
+        block = number % 2
+        up = links.send(total.at[part, layer, block, pl.ds(0, HALF)], from_down.at[part, layer, block], "up")
+        down = links.send(total.at[part, layer, block, pl.ds(3 * HALF, HALF)], from_up.at[part, layer, block], "down")
+        held[number] = [links.sent.pop(), links.sent.pop()]
+        arrivals[number] = (up, down)
+
+    def retire(number):
+        for item, condition in held[number]:
+
+            @pl.when(condition)
+            def _():
+                item.wait_send()
+
+    def columns_in(index):
+        finish_columns(index, 0)
+        finish_columns(index, 1)
+
+    items = spread_plane()
+    columns_in(0)
+    issue(0)
+    issue(1)
+    columns_in(1)
+    retire(0)
+    issue(2)
+    retire(1)
+    issue(3)
+    add_plane(items)
+    items = spread_line()
+    columns_in(2)
+    retire(2)
+    issue(4)
+    retire(3)
+    issue(5)
+    add_line(items)
+    items = share_plane()
+    columns_in(3)
+    retire(4)
+    issue(6)
+    retire(5)
+    issue(7)
+    await_all(items)
+    retire(6)
+    retire(7)
+    own_half = gathered.at[rows_at(base, half)]
+    swap_back = start(own_half, own_half, partner)
+    for number in range(2 * len(PLANES)):
+        (part, layer), block = PLANES[number // 2], number % 2
+        for arrived in arrivals[number]:
             arrived()
-        for block in range(2):
-            lane = pl.ds(block * HALF, HALF)
-            for begin, buffer in ((HALF, from_up), (SIDE, from_down)):
-                for offset in range(0, HALF, 64):
-                    rows, near = pl.ds(begin + offset, 64), pl.ds(offset, 64)
-                    gradient = total[part, layer, block, rows, :] + buffer[part, layer, block, near, :]
-                    target = pl.ds(begin - HALF + offset, 64)
-                    object_ref[part, layer, target, lane] = (
-                        ext_ref[part, layer, 1 + block, rows, :] - OBJECT_STEP * gradient
-                    )
+        lane = pl.ds(block * HALF, HALF)
+        for begin, buffer in ((HALF, from_up), (SIDE, from_down)):
+            for offset in range(0, HALF, 64):
+                rows, near = pl.ds(begin + offset, 64), pl.ds(offset, 64)
+                gradient = total[part, layer, block, rows, :] + buffer[part, layer, block, near, :]
+                target = pl.ds(begin - HALF + offset, 64)
+                object_ref[part, layer, target, lane] = ext_ref[part, layer, 1 + block, rows, :] - OBJECT_STEP * gradient
     swap_back.wait_recv()
 
     def finish_probe(rows):
@@ -623,10 +676,10 @@
             f32(2, 2, 2, 2 * SIDE, HALF),
             f32(*flat),
             f32(2 * SIDE, SIDE),
-            [f32(15, 2 * SIDE // 16, SIDE), f32(3, 2 * SIDE // 64, SIDE)],
+            [f32(15, 2 * SIDE // 16, SIDE), f32(4, 2 * SIDE // 16, SIDE)],
             f32(*flat),
             f32(*flat),
-            *semaphores(72 + 8 + 2 + 2 * 18),
+            *semaphores(72 + 16 + 2 + 33),
         ],
         compiler_params=comm_params(2, 26),
     )(extended, gradient, first_probe.reshape(flat), second_probe.reshape(flat), probe_modes.reshape(flat))

time: 190 us -> 178 us (0.937)
  Pallas kernels: 185 us -> 173 us
    pallas_call x1, Pallas kernels: 69.5 us -> 56.7 us  [last_exchange(): pl.pallas_call(last_kernel, out_shape=(jax.ShapeDtypeStruct((2, 2, SIDE,...]
    pallas_call x2, Pallas kernels: 8.93 us -> 15.8 us  [batch_terms(): pl.pallas_call(functools.partial(batch_kernel, batch), out_shape=(jax.Sha...]
    pallas_call x1, Pallas kernels: 71 us -> 64.4 us  [middle_exchange(): pl.pallas_call(middle_kernel, out_shape=EXTENDED, in_specs=vmem_specs(2),...]
where the time goes in v5:
time: 178 us; the launch traced here: 177 us
  Pallas kernels  173 us (97%)
  local copies, waits for them, and re-layouts  3.47 us (2%)
    pallas_call x1, Pallas kernels, middle_exchange(): pl.pallas_call(middle_kernel, out_shape=EXTENDED, in_specs=vmem_specs(2),...  64.4 us
    pallas_call x1, Pallas kernels, last_exchange(): pl.pallas_call(last_kernel, out_shape=(jax.ShapeDtypeStruct((2, 2, SIDE,...  56.7 us
    pallas_call x1, Pallas kernels, first_exchange(): pl.pallas_call(first_kernel, out_shape=(EXTENDED, jax.ShapeDtypeStruct((p...  35.9 us
    pallas_call x2, Pallas kernels, batch_terms(): pl.pallas_call(functools.partial(batch_kernel, batch), out_shape=(jax.Sha...  15.8 us

profile of v5, /device:TPU:1, one launch (start us, length us, event | category | flops | bytes accessed | tf_op | source)
XLA Modules:
  0.0 177.0 jit_solution(7587870312838874905)
XLA Ops:
  0.6 0.7 copy.11.count_ref
  1.4 0.8 copy.10.offset_ref
  2.2 35.9 %shard_map.95 = (f32[2,2,4,512,128]{4,3,2,1,0:T(8,128)S(1)}, f32[6,256,256]{2,1,0:T(8,128)S(1)}, bf16[8,256,256]{2,1,0:T(8,128)(2,1)S(1)}, f32[2,2,256,256]{3,2,1,0:T(8,128)S(1)}) custom-call(f32[2,2,256,256]{3,2,1,0:T(8,128)} %tile_ref.1, f32[6,256,256]{2,1,0:T(8,128)} %bitcast.9, bf16[256,256]{1,0:T(8,128)(2,1)} %constant.7.clone.order_ref, ...), custom_call_target="tpu_custom_call" | custom-call | tf_op jit(solution)/shard_map/pallas_call | solution.py:617
  38.0 7.9 %shard_map.96 = (f32[2,2,4,512,128]{4,3,2,1,0:T(8,128)S(1)}, f32[2,2,256,256]{3,2,1,0:T(8,128)S(1)}) custom-call(s32[2,2,3,1]{3,2,1,0:T(4,128)S(1)} %copy.10.offset_ref, s32[2,1,1]{2,1,0:T(1,128)S(1)} %copy.11.count_ref, f32[2,2,4,512,128]{4,3,2,1,0:T(8,128)S(1)} %get-tuple-element.12.ext_ref, f32[2,2,256,256]{3,2,1,0:T(8,128)S(1)} %get-tuple-element.13.probe_ref, ...), custom_call_target="tpu_custom_call" | custom-call | flops 3221225472 | bytes 12582912 | tf_op jit(solution)/shard_map/pallas_call | solution.py:930
  46.0 64.4 %shard_map.97.ext_ref = f32[2,2,4,512,128]{4,3,2,1,0:T(8,128)S(1)} custom-call(f32[2,2,4,512,128]{4,3,2,1,0:T(8,128)S(1)} %get-tuple-element.12.ext_ref, f32[2,2,4,512,128]{4,3,2,1,0:T(8,128)S(1)} %get-tuple-element.16.grad_ref), custom_call_target="tpu_custom_call" | custom-call | tf_op jit(solution)/shard_map/pallas_call | solution.py:645
  110.4 7.9 %shard_map.98 = (f32[2,2,4,512,128]{4,3,2,1,0:T(8,128)S(1)}, f32[2,2,256,256]{3,2,1,0:T(8,128)S(1)}) custom-call(s32[2,2,3,1]{3,2,1,0:T(4,128)S(1)} %copy.10.offset_ref, s32[2,1,1]{2,1,0:T(1,128)S(1)} %copy.11.count_ref, f32[2,2,4,512,128]{4,3,2,1,0:T(8,128)S(1)} %shard_map.97.ext_ref, f32[2,2,256,256]{3,2,1,0:T(8,128)S(1)} %get-tuple-element.13.probe_ref, ...), custom_call_target="tpu_custom_call" | custom-call | flops 3221225472 | bytes 12582912 | tf_op jit(solution)/shard_map/pallas_call | solution.py:930
  118.3 56.7 %shard_map.99 = (f32[2,2,256,256]{3,2,1,0:T(8,128)S(1)}, f32[1024,256]{1,0:T(8,128)S(1)}) custom-call(f32[2,2,4,512,128]{4,3,2,1,0:T(8,128)S(1)} %shard_map.97.ext_ref, f32[2,2,4,512,128]{4,3,2,1,0:T(8,128)S(1)} %get-tuple-element.17.grad_ref, f32[1024,256]{1,0:T(8,128)S(1)} %bitcast.7, f32[1024,256]{1,0:T(8,128)S(1)} %bitcast.8, f32[1024,256]{1,0:T(8,128)S(1)} %bitcast.6), custom_call_target="tpu_custom_call" | custom-call | tf_op jit(solution)/shard_map/pallas_call | solution.py:664
  175.0 1.0 copy.16
  176.0 1.0 copy.17

commit v6 on v5

--- a/solution.py
+++ b/solution.py
@@ -16,6 +16,7 @@
 HALF = SIDE // 2
 MODES = 2
 CHUNK = 16
+IN_FLIGHT = 2
 RELAYED_CORNER_LAYERS = 1
 MIDDLE_DIRECT_GRADIENTS = (0,)
 MIDDLE_DIRECT_HALOS = (3,)
@@ -389,37 +390,61 @@
             for part, layer in PLANES:
                 out_ref[part, layer, block] = jnp.zeros((2 * SIDE, HALF), jnp.float32)
 
-    arrivals = []
-    for index, (part, layer) in enumerate(PLANES):
-        finish_columns(index, 0)
-        up = links.send(total.at[part, layer, :, pl.ds(0, SIDE)], from_down.at[part, layer], "up")
-        finish_columns(index, 1)
-        down = links.send(total.at[part, layer, :, pl.ds(SIDE, SIDE)], from_up.at[part, layer], "down")
-        arrivals.append((up, down))
     step_up = jnp.where(links.has["up"], OBJECT_STEP, 0.0).astype(jnp.float32)
     step_down = jnp.where(links.has["down"], OBJECT_STEP, 0.0).astype(jnp.float32)
-    halos = []
-    for index, (part, layer) in enumerate(PLANES):
-        for arrived in arrivals[index]:
+    held, arrivals, halos = {}, {}, []
+    pieces = 2 * len(PLANES)
+
+    def issue(number):
+        (part, layer), block = PLANES[number // 2], number % 2
+        if block == 0:
+            finish_columns(number // 2, 0)
+        up = links.send(total.at[part, layer, block, pl.ds(0, SIDE)], from_down.at[part, layer, block], "up")
+        if block == 0:
+            finish_columns(number // 2, 1)
+        down = links.send(total.at[part, layer, block, pl.ds(SIDE, SIDE)], from_up.at[part, layer, block], "down")
+        held[number] = [links.sent.pop(), links.sent.pop()]
+        arrivals[number] = (up, down)
+
+    def retire(number):
+        for item, condition in held[number]:
+
+            @pl.when(condition)
+            def _():
+                item.wait_send()
+
+    for number in range(IN_FLIGHT):
+        issue(number)
+    for number in range(pieces):
+        (part, layer), block = PLANES[number // 2], number % 2
+        for arrived in arrivals[number]:
             arrived()
-        for block in range(2):
-            for start, buffer, offset, step in (
-                (0, from_up, 0, step_up),
-                (HALF, from_up, 0, OBJECT_STEP),
-                (SIDE, from_down, SIDE, OBJECT_STEP),
-                (3 * HALF, from_down, SIDE, step_down),
-            ):
-                for row in range(start, start + HALF, 64):
-                    rows, near = pl.ds(row, 64), pl.ds(row - offset, 64)
-                    gradient = total[part, layer, block, rows, :] + buffer[part, layer, block, near, :]
-                    out_ref[part, layer, 1 + block, rows, :] = ext_ref[part, layer, 1 + block, rows, :] - step * gradient
-        slot = halo_slots.at[part, layer]
-        halos.append(links.send_columns(out_ref.at[part, layer, 1], out_ref.at[part, layer, 3], "left", slot, relay=index not in MIDDLE_DIRECT_HALOS))
-        halos.append(links.send_columns(out_ref.at[part, layer, 2], out_ref.at[part, layer, 0], "right", slot, relay=index not in MIDDLE_DIRECT_HALOS))
-        for forward, _ in halos[2 * index - 2 : 2 * index]:
-            forward()
-    for forward, _ in halos[-2:]:
-        forward()
+        retire(number)
+        if number + IN_FLIGHT < pieces:
+            issue(number + IN_FLIGHT)
+        for start, buffer, offset, step in (
+            (0, from_up, 0, step_up),
+            (HALF, from_up, 0, OBJECT_STEP),
+            (SIDE, from_down, SIDE, OBJECT_STEP),
+            (3 * HALF, from_down, SIDE, step_down),
+        ):
+            for row in range(start, start + HALF, 64):
+                rows, near = pl.ds(row, 64), pl.ds(row - offset, 64)
+                gradient = total[part, layer, block, rows, :] + buffer[part, layer, block, near, :]
+                out_ref[part, layer, 1 + block, rows, :] = ext_ref[part, layer, 1 + block, rows, :] - step * gradient
+        side, target = (("left", 3), ("right", 0))[block]
+        halos.append(
+            links.send_columns(
+                out_ref.at[part, layer, 1 + block],
+                out_ref.at[part, layer, target],
+                side,
+                halo_slots.at[part, layer],
+                relay=number // 2 not in MIDDLE_DIRECT_HALOS,
+            )
+        )
+        if number:
+            halos[number - 1][0]()
+    halos[-1][0]()
     for _, arrived in halos:
         for half in range(2):
             arrived(half)
@@ -653,7 +678,7 @@
             f32(2, 2, 2, SIDE, HALF),
             f32(2, 2, 2, 2 * SIDE, HALF),
             f32(2, 2, 3, HALF, HALF),
-            *semaphores(72 + 8 + 72),
+            *semaphores(72 + 16 + 72),
         ],
         compiler_params=comm_params(1, 24),
     )(extended, gradient)

time: 178 us -> 179 us (level)
    pallas_call x2, Pallas kernels: 15.8 us -> 12.4 us  [batch_terms(): pl.pallas_call(functools.partial(batch_kernel, batch), out_shape=(jax.Sha...]
    pallas_call x1, Pallas kernels: 64.4 us -> 67.3 us  [middle_exchange(): pl.pallas_call(middle_kernel, out_shape=EXTENDED, in_specs=vmem_specs(2),...]
where the time goes in v6:
time: 179 us; the launch traced here: 178 us
  Pallas kernels  174 us (97%)
  local copies, waits for them, and re-layouts  3.47 us (2%)
    pallas_call x1, Pallas kernels, middle_exchange(): pl.pallas_call(middle_kernel, out_shape=EXTENDED, in_specs=vmem_specs(2),...  67.3 us
    pallas_call x1, Pallas kernels, last_exchange(): pl.pallas_call(last_kernel, out_shape=(jax.ShapeDtypeStruct((2, 2, SIDE,...  58.4 us
    pallas_call x1, Pallas kernels, first_exchange(): pl.pallas_call(first_kernel, out_shape=(EXTENDED, jax.ShapeDtypeStruct((p...  35.9 us
    pallas_call x2, Pallas kernels, batch_terms(): pl.pallas_call(functools.partial(batch_kernel, batch), out_shape=(jax.Sha...  12.4 us

profile of v6, /device:TPU:1, one launch (start us, length us, event | category | flops | bytes accessed | tf_op | source)
XLA Modules:
  0.0 178.2 jit_solution(12101167799196108836)
XLA Ops:
  0.6 0.7 copy.11.count_ref
  1.4 0.8 copy.10.offset_ref
  2.2 35.9 %shard_map.95 = (f32[2,2,4,512,128]{4,3,2,1,0:T(8,128)S(1)}, f32[6,256,256]{2,1,0:T(8,128)S(1)}, bf16[8,256,256]{2,1,0:T(8,128)(2,1)S(1)}, f32[2,2,256,256]{3,2,1,0:T(8,128)S(1)}) custom-call(f32[2,2,256,256]{3,2,1,0:T(8,128)} %tile_ref.1, f32[6,256,256]{2,1,0:T(8,128)} %bitcast.9, bf16[256,256]{1,0:T(8,128)(2,1)} %constant.7.clone.order_ref, ...), custom_call_target="tpu_custom_call" | custom-call | tf_op jit(solution)/shard_map/pallas_call | solution.py:642
  38.0 7.9 %shard_map.96 = (f32[2,2,4,512,128]{4,3,2,1,0:T(8,128)S(1)}, f32[2,2,256,256]{3,2,1,0:T(8,128)S(1)}) custom-call(s32[2,2,3,1]{3,2,1,0:T(4,128)S(1)} %copy.10.offset_ref, s32[2,1,1]{2,1,0:T(1,128)S(1)} %copy.11.count_ref, f32[2,2,4,512,128]{4,3,2,1,0:T(8,128)S(1)} %get-tuple-element.12.ext_ref, f32[2,2,256,256]{3,2,1,0:T(8,128)S(1)} %get-tuple-element.13.probe_ref, ...), custom_call_target="tpu_custom_call" | custom-call | flops 3221225472 | bytes 12582912 | tf_op jit(solution)/shard_map/pallas_call | solution.py:955
  46.0 67.3 %shard_map.97.ext_ref = f32[2,2,4,512,128]{4,3,2,1,0:T(8,128)S(1)} custom-call(f32[2,2,4,512,128]{4,3,2,1,0:T(8,128)S(1)} %get-tuple-element.12.ext_ref, f32[2,2,4,512,128]{4,3,2,1,0:T(8,128)S(1)} %get-tuple-element.16.grad_ref), custom_call_target="tpu_custom_call" | custom-call | tf_op jit(solution)/shard_map/pallas_call | solution.py:670
  113.3 4.4 %shard_map.98 = (f32[2,2,4,512,128]{4,3,2,1,0:T(8,128)S(1)}, f32[2,2,256,256]{3,2,1,0:T(8,128)S(1)}) custom-call(s32[2,2,3,1]{3,2,1,0:T(4,128)S(1)} %copy.10.offset_ref, s32[2,1,1]{2,1,0:T(1,128)S(1)} %copy.11.count_ref, f32[2,2,4,512,128]{4,3,2,1,0:T(8,128)S(1)} %shard_map.97.ext_ref, f32[2,2,256,256]{3,2,1,0:T(8,128)S(1)} %get-tuple-element.13.probe_ref, ...), custom_call_target="tpu_custom_call" | custom-call | flops 3221225472 | bytes 12582912 | tf_op jit(solution)/shard_map/pallas_call | solution.py:955
  117.8 58.4 %shard_map.99 = (f32[2,2,256,256]{3,2,1,0:T(8,128)S(1)}, f32[1024,256]{1,0:T(8,128)S(1)}) custom-call(f32[2,2,4,512,128]{4,3,2,1,0:T(8,128)S(1)} %shard_map.97.ext_ref, f32[2,2,4,512,128]{4,3,2,1,0:T(8,128)S(1)} %get-tuple-element.17.grad_ref, f32[1024,256]{1,0:T(8,128)S(1)} %bitcast.7, f32[1024,256]{1,0:T(8,128)S(1)} %bitcast.8, f32[1024,256]{1,0:T(8,128)S(1)} %bitcast.6), custom_call_target="tpu_custom_call" | custom-call | tf_op jit(solution)/shard_map/pallas_call | solution.py:689
  176.2 1.0 copy.16
  177.2 1.0 copy.17

commit v7 on v6

--- a/solution.py
+++ b/solution.py
@@ -818,8 +818,8 @@
         return [ref[first, second, pl.ds(row, CHUNK), lane] for lane in (lo, hi)]
 
     def one_slot(slot, carry):
-        start_row = offset_ref[batch, 0, slot, 0]
-        start_col = offset_ref[batch, 1, slot, 0]
+        start_row = offset_ref[batch * 2, slot]
+        start_col = offset_ref[batch * 2 + 1, slot]
         base = start_col // HALF
         shift = start_col % HALF
         take_left = lanes < HALF - shift
@@ -945,7 +945,7 @@
         chunks(HALF, first_back)
         return carry
 
-    lax.fori_loop(0, count_ref[batch, 0, 0], one_slot, 0)
+    lax.fori_loop(0, count_ref[batch], one_slot, 0)
 
 
 def batch_terms(batch, extended, probe_modes, amplitudes, offsets, counts, table):
@@ -983,6 +983,7 @@
     extended, ordered, table, probe_modes = first_exchange(
         object_field, amplitudes.reshape(batches * slots, SIDE, SIDE), table, probe_modes
     )
+    offsets, counts = offsets.reshape(2 * batches, slots), counts.reshape(batches)
     terms = lambda cells, batch: batch_terms(batch, cells, probe_modes, ordered, offsets, counts, table)
     gradient, first_probe = terms(extended, 0)
     extended = middle_exchange(extended, gradient)

time: 179 us -> 177 us (0.989)
    pallas_call x1, Pallas kernels: 58.4 us -> 54.3 us  [last_exchange(): pl.pallas_call(last_kernel, out_shape=(jax.ShapeDtypeStruct((2, 2, SIDE,...]
    pallas_call x1, Pallas kernels: 67.3 us -> 70.5 us  [middle_exchange(): pl.pallas_call(middle_kernel, out_shape=EXTENDED, in_specs=vmem_specs(2),...]
where the time goes in v7:
time: 177 us; the launch traced here: 175 us
  Pallas kernels  173 us (98%)
  local copies, waits for them, and re-layouts  1.95 us (1%)
    pallas_call x1, Pallas kernels, middle_exchange(): pl.pallas_call(middle_kernel, out_shape=EXTENDED, in_specs=vmem_specs(2),...  70.5 us
    pallas_call x1, Pallas kernels, last_exchange(): pl.pallas_call(last_kernel, out_shape=(jax.ShapeDtypeStruct((2, 2, SIDE,...  54.3 us
    pallas_call x1, Pallas kernels, first_exchange(): pl.pallas_call(first_kernel, out_shape=(EXTENDED, jax.ShapeDtypeStruct((p...  35.9 us
    pallas_call x2, Pallas kernels, batch_terms(): pl.pallas_call(functools.partial(batch_kernel, batch), out_shape=(jax.Sha...  12.1 us

profile of v7, /device:TPU:1, one launch (start us, length us, event | category | flops | bytes accessed | tf_op | source)
XLA Modules:
  0.0 175.4 jit_solution(18107763904460529304)
XLA Ops:
  0.6 0.0 copy-start.1
  0.6 0.0 copy-start
  0.7 35.9 %shard_map.95 = (f32[2,2,4,512,128]{4,3,2,1,0:T(8,128)S(1)}, f32[6,256,256]{2,1,0:T(8,128)S(1)}, bf16[8,256,256]{2,1,0:T(8,128)(2,1)S(1)}, f32[2,2,256,256]{3,2,1,0:T(8,128)S(1)}) custom-call(f32[2,2,256,256]{3,2,1,0:T(8,128)} %tile_ref.1, f32[6,256,256]{2,1,0:T(8,128)} %bitcast.15, bf16[256,256]{1,0:T(8,128)(2,1)} %constant.7.clone.order_ref, ...), custom_call_target="tpu_custom_call" | custom-call | tf_op jit(solution)/shard_map/pallas_call | solution.py:642
  36.6 0.0 copy-done.1
  36.6 0.0 copy-done
  36.6 4.3 %shard_map.96 = (f32[2,2,4,512,128]{4,3,2,1,0:T(8,128)S(1)}, f32[2,2,256,256]{3,2,1,0:T(8,128)S(1)}) custom-call(s32[4,3]{1,0:T(4,128)S(1)} %bitcast.11, s32[2]{0:T(128)S(1)} %bitcast.13, f32[2,2,4,512,128]{4,3,2,1,0:T(8,128)S(1)} %get-tuple-element.12.ext_ref, f32[2,2,256,256]{3,2,1,0:T(8,128)S(1)} %get-tuple-element.13.probe_ref, ...), custom_call_target="tpu_custom_call" | custom-call | flops 3221225472 | bytes 12582912 | tf_op jit(solution)/shard_map/pallas_call | solution.py:955
  40.9 70.5 %shard_map.97.ext_ref = f32[2,2,4,512,128]{4,3,2,1,0:T(8,128)S(1)} custom-call(f32[2,2,4,512,128]{4,3,2,1,0:T(8,128)S(1)} %get-tuple-element.12.ext_ref, f32[2,2,4,512,128]{4,3,2,1,0:T(8,128)S(1)} %get-tuple-element.16.grad_ref), custom_call_target="tpu_custom_call" | custom-call | tf_op jit(solution)/shard_map/pallas_call | solution.py:670
  111.4 7.8 %shard_map.98 = (f32[2,2,4,512,128]{4,3,2,1,0:T(8,128)S(1)}, f32[2,2,256,256]{3,2,1,0:T(8,128)S(1)}) custom-call(s32[4,3]{1,0:T(4,128)S(1)} %bitcast.12, s32[2]{0:T(128)S(1)} %bitcast.14, f32[2,2,4,512,128]{4,3,2,1,0:T(8,128)S(1)} %shard_map.97.ext_ref, f32[2,2,256,256]{3,2,1,0:T(8,128)S(1)} %get-tuple-element.13.probe_ref, ...), custom_call_target="tpu_custom_call" | custom-call | flops 3221225472 | bytes 12582912 | tf_op jit(solution)/shard_map/pallas_call | solution.py:955
  119.2 54.3 %shard_map.99 = (f32[2,2,256,256]{3,2,1,0:T(8,128)S(1)}, f32[1024,256]{1,0:T(8,128)S(1)}) custom-call(f32[2,2,4,512,128]{4,3,2,1,0:T(8,128)S(1)} %shard_map.97.ext_ref, f32[2,2,4,512,128]{4,3,2,1,0:T(8,128)S(1)} %get-tuple-element.17.grad_ref, f32[1024,256]{1,0:T(8,128)S(1)} %bitcast.9, f32[1024,256]{1,0:T(8,128)S(1)} %bitcast.10, f32[1024,256]{1,0:T(8,128)S(1)} %bitcast.8), custom_call_target="tpu_custom_call" | custom-call | tf_op jit(solution)/shard_map/pallas_call | solution.py:689
  173.5 1.0 copy.12
  174.5 1.0 copy.13
Async XLA Ops:
  0.6 35.9 %copy-start.1 = (s32[2,1,1]{0,2,1:T(1,128)S(1)}, s32[2,1,1]{0,2,1:T(1,128)}, u32[]{:S(2)}) copy-start(s32[2,1,1]{0,2,1:T(1,128)} %param.12) | copy-start | bytes 28
  0.6 35.9 %copy-start = (s32[2,2,3,1]{2,3,1,0:T(1,128)S(1)}, s32[2,2,3,1]{2,3,1,0:T(1,128)}, u32[]{:S(2)}) copy-start(s32[2,2,3,1]{2,3,1,0:T(1,128)} %param.11) | copy-start | bytes 148

commit v8 on v7

--- a/solution.py
+++ b/solution.py
@@ -229,7 +229,7 @@
         body(pl.ds(pl.multiple_of(start + index * step, 8), step))
         return carry
 
-    lax.fori_loop(0, (stop - start) // step, one, 0)
+    lax.fori_loop(0, (stop - start) // step, one, 0, unroll=True)
 
 
 def first_kernel(
@@ -501,7 +501,7 @@
         sums[mine, :] = partial[mine, :] + pair[near, :]
         return carry
 
-    lax.fori_loop(0, half // 64, add_pair, 0)
+    lax.fori_loop(0, half // 64, add_pair, 0, unroll=True)
     gathers = [swap]
 
     piece = half // 16

time: 177 us -> 175 us (0.989); the launches traced: 175 us -> 176 us
    pallas_call x1, Pallas kernels: 54.3 us -> 59.4 us  [last_exchange(): pl.pallas_call(last_kernel, out_shape=(jax.ShapeDtypeStruct((2, 2, SIDE,...]
    pallas_call x2, Pallas kernels: 12.1 us -> 8.74 us  [batch_terms(): pl.pallas_call(functools.partial(batch_kernel, batch), out_shape=(jax.Sha...]
where the time goes in v8:
time: 175 us; the launch traced here: 176 us
  Pallas kernels  174 us (99%)
  local copies, waits for them, and re-layouts  1.95 us (1%)
    pallas_call x1, Pallas kernels, middle_exchange(): pl.pallas_call(middle_kernel, out_shape=EXTENDED, in_specs=vmem_specs(2),...  69.5 us
    pallas_call x1, Pallas kernels, last_exchange(): pl.pallas_call(last_kernel, out_shape=(jax.ShapeDtypeStruct((2, 2, SIDE,...  59.4 us
    pallas_call x1, Pallas kernels, first_exchange(): pl.pallas_call(first_kernel, out_shape=(EXTENDED, jax.ShapeDtypeStruct((p...  35.9 us
    pallas_call x2, Pallas kernels, batch_terms(): pl.pallas_call(functools.partial(batch_kernel, batch), out_shape=(jax.Sha...  8.74 us

profile of v8, /device:TPU:1, one launch (start us, length us, event | category | flops | bytes accessed | tf_op | source)
XLA Modules:
  0.0 176.2 jit_solution(1627945813376454609)
XLA Ops:
  0.6 0.0 copy-start.1
  0.6 0.0 copy-start
  0.7 35.9 %shard_map.95 = (f32[2,2,4,512,128]{4,3,2,1,0:T(8,128)S(1)}, f32[6,256,256]{2,1,0:T(8,128)S(1)}, bf16[8,256,256]{2,1,0:T(8,128)(2,1)S(1)}, f32[2,2,256,256]{3,2,1,0:T(8,128)S(1)}) custom-call(f32[2,2,256,256]{3,2,1,0:T(8,128)} %tile_ref.1, f32[6,256,256]{2,1,0:T(8,128)} %bitcast.15, bf16[256,256]{1,0:T(8,128)(2,1)} %constant.7.clone.order_ref, ...), custom_call_target="tpu_custom_call" | custom-call | tf_op jit(solution)/shard_map/pallas_call | solution.py:642
  36.6 0.0 copy-done.1
  36.6 0.0 copy-done
  36.6 4.4 %shard_map.96 = (f32[2,2,4,512,128]{4,3,2,1,0:T(8,128)S(1)}, f32[2,2,256,256]{3,2,1,0:T(8,128)S(1)}) custom-call(s32[4,3]{1,0:T(4,128)S(1)} %bitcast.11, s32[2]{0:T(128)S(1)} %bitcast.13, f32[2,2,4,512,128]{4,3,2,1,0:T(8,128)S(1)} %get-tuple-element.12.ext_ref, f32[2,2,256,256]{3,2,1,0:T(8,128)S(1)} %get-tuple-element.13.probe_ref, ...), custom_call_target="tpu_custom_call" | custom-call | flops 3221225472 | bytes 12582912 | tf_op jit(solution)/shard_map/pallas_call | solution.py:955
  41.0 69.5 %shard_map.97.ext_ref = f32[2,2,4,512,128]{4,3,2,1,0:T(8,128)S(1)} custom-call(f32[2,2,4,512,128]{4,3,2,1,0:T(8,128)S(1)} %get-tuple-element.12.ext_ref, f32[2,2,4,512,128]{4,3,2,1,0:T(8,128)S(1)} %get-tuple-element.16.grad_ref), custom_call_target="tpu_custom_call" | custom-call | tf_op jit(solution)/shard_map/pallas_call | solution.py:670
  110.5 4.4 %shard_map.98 = (f32[2,2,4,512,128]{4,3,2,1,0:T(8,128)S(1)}, f32[2,2,256,256]{3,2,1,0:T(8,128)S(1)}) custom-call(s32[4,3]{1,0:T(4,128)S(1)} %bitcast.12, s32[2]{0:T(128)S(1)} %bitcast.14, f32[2,2,4,512,128]{4,3,2,1,0:T(8,128)S(1)} %shard_map.97.ext_ref, f32[2,2,256,256]{3,2,1,0:T(8,128)S(1)} %get-tuple-element.13.probe_ref, ...), custom_call_target="tpu_custom_call" | custom-call | flops 3221225472 | bytes 12582912 | tf_op jit(solution)/shard_map/pallas_call | solution.py:955
  114.8 59.4 %shard_map.99 = (f32[2,2,256,256]{3,2,1,0:T(8,128)S(1)}, f32[1024,256]{1,0:T(8,128)S(1)}) custom-call(f32[2,2,4,512,128]{4,3,2,1,0:T(8,128)S(1)} %shard_map.97.ext_ref, f32[2,2,4,512,128]{4,3,2,1,0:T(8,128)S(1)} %get-tuple-element.17.grad_ref, f32[1024,256]{1,0:T(8,128)S(1)} %bitcast.9, f32[1024,256]{1,0:T(8,128)S(1)} %bitcast.10, f32[1024,256]{1,0:T(8,128)S(1)} %bitcast.8), custom_call_target="tpu_custom_call" | custom-call | tf_op jit(solution)/shard_map/pallas_call | solution.py:689
  174.2 1.0 copy.12
  175.2 1.0 copy.13
Async XLA Ops:
  0.6 35.9 %copy-start.1 = (s32[2,1,1]{0,2,1:T(1,128)S(1)}, s32[2,1,1]{0,2,1:T(1,128)}, u32[]{:S(2)}) copy-start(s32[2,1,1]{0,2,1:T(1,128)} %param.12) | copy-start | bytes 28
  0.6 35.9 %copy-start = (s32[2,2,3,1]{2,3,1,0:T(1,128)S(1)}, s32[2,2,3,1]{2,3,1,0:T(1,128)}, u32[]{:S(2)}) copy-start(s32[2,2,3,1]{2,3,1,0:T(1,128)} %param.11) | copy-start | bytes 148
